TPU v7x, 32 devices: a whole 2x2x4 slice. The times are simulated.
32 devices in a mesh: dp: 8 (over y, x, core), tensor: 4 (over z).
Axes of the slice: x: 2, y: 2, z: 4, core: 2. Of those that a mesh axis runs over, the one named last changes fastest.
Arguments:
- layer_input: bfloat16 [8, 1024, 1024], P('dp', 'tensor'), may hold values from -6 to 6
- document_lengths: int32 [8, 8], P('dp'), may hold values from 1 to 512, 1024 in all within a row
- attention_norm_gain: float32 [1024], replicated, may hold values from 0.25 to 1.75
- feedfwd_norm_gain: float32 [1024], replicated, may hold values from 0.25 to 1.75
- query_key_value_weight: bfloat16 [3, 1024, 1024], P(None, None, 'tensor'), may hold values from -0.1875 to 0.1875
- output_weight: bfloat16 [1024, 1024], P('tensor'), may hold values from -0.75 to 0.75
- up_weight: bfloat16 [1024, 4096], P(None, 'tensor'), may hold values from -0.1875 to 0.1875
- down_weight: bfloat16 [4096, 1024], P('tensor'), may hold values from -0.09375 to 0.09375
- adapter_query_key_value_first: bfloat16 [3, 1024, 128], replicated, may hold values from -0.1875 to 0.1875
- adapter_query_key_value_second: bfloat16 [3, 128, 1024], P(None, None, 'tensor'), may hold values from -0.5 to 0.5
- adapter_output_first: bfloat16 [1024, 128], P('tensor'), may hold values from -0.75 to 0.75
- adapter_output_second: bfloat16 [128, 1024], replicated, may hold values from -0.5 to 0.5
- adapter_up_first: bfloat16 [1024, 128], replicated, may hold values from -0.1875 to 0.1875
- adapter_up_second: bfloat16 [128, 4096], P(None, 'tensor'), may hold values from -0.5 to 0.5
- adapter_down_first: bfloat16 [4096, 128], P('tensor'), may hold values from -0.09375 to 0.09375
- adapter_down_second: bfloat16 [128, 1024], replicated, may hold values from -0.5 to 0.5
- cotangent: bfloat16 [8, 1024, 1024], P('dp', 'tensor'), may hold values from -6 to 6
Outputs:
- layer_output: bfloat16 [8, 1024, 1024], P('dp', 'tensor')
- grad_in: float32 [8, 1024, 1024], P('dp', 'tensor')
- grad_a_qkv: float32 [3, 1024, 128], replicated
- grad_b_qkv: float32 [3, 128, 1024], P(None, None, 'tensor')
- grad_a_out: float32 [1024, 128], P('tensor')
- grad_b_out: float32 [128, 1024], replicated
- grad_a_up: float32 [1024, 128], replicated
- grad_b_up: float32 [128, 4096], P(None, 'tensor')
- grad_a_down: float32 [4096, 128], P('tensor')
- grad_b_down: float32 [128, 1024], replicated
Inputs may be any that keep to these rules, and one draw needn't show every extreme that they name: `document_lengths`: in each row the 8 lengths are positive, sum to 1024, and the largest is exactly 512; the documents lie in the row in the order given.
All inputs are finite; a program needn't handle non-finite values.
Results may differ from a plain program's by a relative error of at most 0.012.
Values may be sent and summed in bfloat16 or wider, within the bound.
No kernel may reach another device: no remote copies, remote signals or barrier semaphores. Data moves between devices by JAX's collectives and lax.ppermute only.
A program may use at most 128 MiB of HBM per device.

v0:
```python
import math

import jax
import jax.numpy as jnp
from jax import lax
from jax.experimental import pallas as pl
from jax.experimental.pallas import tpu as pltpu
from jax.sharding import PartitionSpec as P

HEAD_DIM = 64
ROT = 16
HALF = ROT // 2
BLOCK = 256
MOST_DOC = 512

EPSILON = 1e-05
ADAPTER_SCALE = 0.25
MASKED = -1e30
VMEM_GRANT = 12 << 20
BF = jnp.bfloat16
F32 = jnp.float32


def mm(left, right, left_dim, right_dim):
    return lax.dot_general(
        left, right, (((left_dim,), (right_dim,)), ((), ())), preferred_element_type=F32
    )


def call(kernel, operands, outputs, scratch=(), flops=0, exps=0, scalars=0):
    spaces = [pltpu.SMEM] * scalars + [pltpu.VMEM] * (len(operands) - scalars)
    moved = sum(math.prod(s) * jnp.dtype(d).itemsize for s, d in outputs)
    return pl.pallas_call(
        kernel,
        in_specs=[pl.BlockSpec(memory_space=space) for space in spaces],
        out_specs=[pl.BlockSpec(memory_space=pltpu.VMEM) for _ in outputs],
        out_shape=[jax.ShapeDtypeStruct(s, d) for s, d in outputs],
        scratch_shapes=list(scratch),
        compiler_params=pltpu.CompilerParams(vmem_limit_bytes=VMEM_GRANT),
        cost_estimate=pl.CostEstimate(
            flops=flops, bytes_accessed=2 * moved, transcendentals=exps
        ),
    )(*operands)


def places_kernel(places_ref, lengths_ref, start_ref, cos_ref, sin_ref, *shards):
    count, seq_len = lengths_ref.shape[1], start_ref.shape[1]
    pos = lax.broadcasted_iota(jnp.int32, (HALF, seq_len), 1)
    start, end = jnp.zeros((HALF, seq_len), jnp.int32), jnp.int32(0)
    for j in range(count):
        end = end + lengths_ref[0, j]
        start = jnp.where(pos >= end, end, start)
    start_ref[...] = start[:1]
    row = lax.broadcasted_iota(jnp.int32, (HALF, seq_len), 0).astype(F32)
    inverse = jnp.exp(row * (-2.0 * math.log(10000.0) / ROT))
    angles = (pos - start).astype(F32) * inverse
    cos_ref[...] = jnp.cos(angles)
    sin_ref[...] = jnp.sin(angles)
    n = len(shards) // 2
    for k in range(n):
        at = lanes(places_ref[k], seq_len // n)
        shards[k][...] = cos_ref[:, at]
        shards[n + k][...] = sin_ref[:, at]


def turn(value, cosine, sine):
    lead, tail = value[:HALF], value[HALF:ROT]
    return jnp.concatenate(
        [lead * cosine - tail * sine, tail * cosine + lead * sine, value[ROT:]], axis=0
    )


def lanes(place, count):
    return pl.ds(pl.multiple_of(place * count, 128), count)


def merge_kernel(
    qkv_ref,
    qkv_first_ref,
    qkv_second_ref,
    up_ref,
    up_first_ref,
    up_second_ref,
    out_ref,
    out_first_ref,
    out_second_ref,
    down_ref,
    down_first_ref,
    down_second_ref,
    gain_a_ref,
    gain_m_ref,
    in_full_ref,
    up_full_ref,
    out_full_ref,
    down_full_ref,
):
    cols = qkv_ref.shape[2]

    def joined(weight, first, second):
        return weight.astype(F32) + ADAPTER_SCALE * mm(first, second, 1, 0)

    def column(row):
        return jnp.broadcast_to(row, (128, row.shape[1])).T

    def times(value, tall):
        return jnp.concatenate(
            [value[:, k : k + 128] * tall for k in range(0, value.shape[1], 128)], axis=1
        )

    gain_a, gain_m = column(gain_a_ref[...]), column(gain_m_ref[...])

    for i in range(3):
        in_full_ref[:, i * cols : (i + 1) * cols] = times(
            joined(qkv_ref[i], qkv_first_ref[i], qkv_second_ref[i]), gain_a
        ).astype(BF)
    up_full_ref[...] = times(
        joined(up_ref[...], up_first_ref[...], up_second_ref[...]), gain_m
    ).astype(BF)
    out_full_ref[...] = joined(out_ref[...], out_first_ref[...], out_second_ref[...]).astype(BF)
    down_full_ref[...] = joined(down_ref[...], down_first_ref[...], down_second_ref[...]).astype(
        BF
    )


def merge_weights(qkv, up, out, down, qkv_ab, up_ab, out_ab, down_ab, gain_a, gain_m):
    steps = 4
    width, cols = qkv.shape[1], qkv.shape[2]
    hidden, rank = up.shape[1], up_ab[0].shape[1]
    rows, out_rows, down_rows = width // steps, cols // steps, hidden // steps

    def fixed(shape):
        return pl.BlockSpec(shape, lambda s: (0,) * len(shape))

    def moving(shape):
        return pl.BlockSpec(shape, lambda s: (s,) + (0,) * (len(shape) - 1))

    def middle(shape):
        return pl.BlockSpec(shape, lambda s: (0, s, 0))

    return pl.pallas_call(
        merge_kernel,
        grid=(steps,),
        in_specs=[
            middle((3, rows, cols)),
            middle((3, rows, rank)),
            fixed((3, rank, cols)),
            moving((rows, hidden)),
            moving((rows, rank)),
            fixed((rank, hidden)),
            moving((out_rows, width)),
            moving((out_rows, rank)),
            fixed((rank, width)),
            moving((down_rows, width)),
            moving((down_rows, rank)),
            fixed((rank, width)),
            pl.BlockSpec((1, rows), lambda s: (0, s)),
            pl.BlockSpec((1, rows), lambda s: (0, s)),
        ],
        out_specs=[
            moving((rows, 3 * cols)),
            moving((rows, hidden)),
            moving((out_rows, width)),
            moving((down_rows, width)),
        ],
        out_shape=[
            jax.ShapeDtypeStruct((width, 3 * cols), BF),
            jax.ShapeDtypeStruct((width, hidden), BF),
            jax.ShapeDtypeStruct((cols, width), BF),
            jax.ShapeDtypeStruct((hidden, width), BF),
        ],
        compiler_params=pltpu.CompilerParams(vmem_limit_bytes=VMEM_GRANT),
        cost_estimate=pl.CostEstimate(
            flops=2 * rank * width * (4 * cols + 2 * hidden),
            bytes_accessed=4 * width * (4 * cols + 2 * hidden),
            transcendentals=0,
        ),
    )(
        qkv,
        qkv_ab[0],
        qkv_ab[1],
        up,
        up_ab[0],
        up_ab[1],
        out,
        out_ab[0],
        out_ab[1],
        down,
        down_ab[0],
        down_ab[1],
        gain_a,
        gain_m,
    )


def project_kernel(
    x_ref,
    gain_a_ref,
    gain_m_ref,
    cos_ref,
    sin_ref,
    qkv_weight_ref,
    qkv_first_ref,
    qkv_second_ref,
    up_first_ref,
    up_ref,
    up_second_ref,
    qkv_ref,
    low_ref,
    hat_ref,
    act_ref,
    slope_ref,
    mlp_ref,
):
    rank = up_first_ref.shape[1]
    cols = qkv_weight_ref.shape[2]
    values = x_ref[...].astype(F32)
    center = values - jnp.mean(values, axis=-1, keepdims=True)
    hat = center * lax.rsqrt(jnp.mean(center * center, axis=-1, keepdims=True) + EPSILON)
    hat_ref[...] = hat.astype(BF)
    attn_in = (hat * gain_a_ref[...]).astype(BF)
    feed_in = (hat * gain_m_ref[...]).astype(BF)
    cosine, sine = cos_ref[...], sin_ref[...]

    def one_third(i, carry):
        low = mm(attn_in, qkv_first_ref[i], 1, 0).astype(BF)
        low_ref[:, lanes(i, rank)] = low
        pre = mm(attn_in, qkv_weight_ref[i], 1, 0) + ADAPTER_SCALE * mm(
            low, qkv_second_ref[i], 1, 0
        )
        pre = pre.T
        turned = (i < 2).astype(F32)
        scale = jnp.where(i == 0, HEAD_DIM**-0.5, 1.0)
        cos_here = 1.0 + turned * (cosine - 1.0)
        sin_here = turned * sine
        for head in range(cols // HEAD_DIM):
            rows = turn(pre[head * HEAD_DIM : (head + 1) * HEAD_DIM], cos_here, sin_here)
            qkv_ref[i, head] = (rows * scale).astype(BF)
        return carry

    lax.fori_loop(0, 3, one_third, 0)
    low = mm(feed_in, up_first_ref[...], 1, 0).astype(BF)
    low_ref[:, 3 * rank :] = low
    mlp_ref[...] = feed_in

    def one_block(k, carry):
        part = lanes(k, BLOCK)
        pre = mm(mlp_ref[...], up_ref[:, part], 1, 0) + ADAPTER_SCALE * mm(
            low, up_second_ref[:, part], 1, 0
        )
        cdf = 0.5 * (1.0 + lax.erf(pre * (2.0**-0.5)))
        act_ref[:, part] = (pre * cdf).astype(BF)
        slope_ref[:, part] = (
            cdf + pre * (jnp.exp(-0.5 * pre * pre) * (1.0 / math.sqrt(2.0 * math.pi)))
        ).astype(BF)
        return carry

    lax.fori_loop(0, up_ref.shape[1] // BLOCK, one_block, 0)


def project(rows, gains, turns, weights):
    count, width = rows.shape
    cols, hidden, rank = weights[0].shape[2], weights[4].shape[1], weights[3].shape[1]
    return call(
        project_kernel,
        [rows, *gains, *turns, *weights],
        [
            ((3, cols // HEAD_DIM, HEAD_DIM, count), BF),
            ((count, 4 * rank), BF),
            ((count, width), BF),
            ((count, hidden), BF),
            ((count, hidden), BF),
        ],
        [pltpu.VMEM((count, width), BF)],
        flops=2 * count * width * (3 * cols + hidden + 4 * rank),
        exps=2 * count * hidden,
    )


def allowed_pairs(start, query_block, key_block):
    key_pos = key_block * BLOCK + lax.broadcasted_iota(jnp.int32, (BLOCK, BLOCK), 0)
    keep = key_pos >= start
    if key_block == query_block:
        query_pos = query_block * BLOCK + lax.broadcasted_iota(jnp.int32, (BLOCK, BLOCK), 1)
        keep = keep & (key_pos <= query_pos)
    return keep


def key_blocks(query_block):
    return range(max(0, query_block - MOST_DOC // BLOCK), query_block + 1)


def attend_forward(n, places_ref, start_ref, *rest):
    chunks, outs, log_ref = rest[:n], rest[n : 2 * n], rest[2 * n]
    qkv, mixed_all = rest[2 * n + 1 :]
    seq_len = start_ref.shape[1]
    count = seq_len // n
    heads = qkv.shape[1]
    for c in range(n):
        qkv[:, :, :, lanes(places_ref[c], count)] = chunks[c][...]

    def one_head(head, carry):
        queries, keys, values = qkv[0, head], qkv[1, head], qkv[2, head]
        keys_t = keys.T
        for i in range(seq_len // BLOCK):
            at = slice(i * BLOCK, (i + 1) * BLOCK)
            start = start_ref[:, at]
            scores = []
            for j in key_blocks(i):
                raw = mm(keys_t[j * BLOCK : (j + 1) * BLOCK], queries[:, at], 1, 0)
                scores.append(jnp.where(allowed_pairs(start, i, j), raw, MASKED))
            peak = jnp.max(scores[0], axis=0, keepdims=True)
            for block in scores[1:]:
                peak = jnp.maximum(peak, jnp.max(block, axis=0, keepdims=True))
            total, mixed = 0.0, 0.0
            for j, block in zip(key_blocks(i), scores):
                terms = jnp.exp(block - peak)
                total = total + jnp.sum(terms, axis=0, keepdims=True)
                mixed = mixed + mm(
                    values[:, j * BLOCK : (j + 1) * BLOCK], terms.astype(BF), 1, 0
                )
            mixed_all[head, :, at] = (mixed / total).astype(BF)
            log_ref[head, :, at] = peak + jnp.log(total)
        return carry

    lax.fori_loop(0, heads, one_head, 0)
    for c in range(n):
        outs[c][...] = mixed_all[:, :, lanes(places_ref[c], count)]


def attend_backward(n, places_ref, start_ref, cos_ref, sin_ref, log_ref, *rest):
    chunks, outs, grads, results = (rest[k * n : (k + 1) * n] for k in range(4))
    qkv, mixed_all, grad_all, result = rest[4 * n :]
    seq_len = start_ref.shape[1]
    count = seq_len // n
    heads = qkv.shape[1]
    for c in range(n):
        at = lanes(places_ref[c], count)
        qkv[:, :, :, at] = chunks[c][...]
        mixed_all[:, :, at] = outs[c][...]
        grad_all[:, :, at] = grads[c][...]
    cosine, sine = cos_ref[...], -sin_ref[...]
    blocks = seq_len // BLOCK

    def one_head(head, carry):
        queries, keys, values = qkv[0, head], qkv[1, head], qkv[2, head]
        grad = grad_all[head]
        inner = jnp.sum(
            grad.astype(F32) * mixed_all[head].astype(F32), axis=0, keepdims=True
        )
        keys_t, values_t = keys.T, values.T
        grad_keys, grad_values = [0.0] * blocks, [0.0] * blocks
        for i in range(blocks):
            at = slice(i * BLOCK, (i + 1) * BLOCK)
            start, log_total, inner_here = start_ref[:, at], log_ref[head, :, at], inner[:, at]
            query, grad_here = queries[:, at], grad[:, at]
            grad_query = 0.0
            for j in key_blocks(i):
                there = slice(j * BLOCK, (j + 1) * BLOCK)
                raw = mm(keys_t[there], query, 1, 0)
                terms = jnp.exp(jnp.where(allowed_pairs(start, i, j), raw, MASKED) - log_total)
                grad_terms = mm(values_t[there], grad_here, 1, 0)
                grad_scores = (terms * (grad_terms - inner_here)).astype(BF)
                grad_values[j] = grad_values[j] + mm(grad_here, terms.astype(BF), 1, 1)
                grad_keys[j] = grad_keys[j] + mm(query, grad_scores, 1, 1)
                grad_query = grad_query + mm(keys[:, there], grad_scores, 1, 0)
            grad_query = turn(grad_query * (HEAD_DIM**-0.5), cosine[:, at], sine[:, at])
            result[0, head, :, at] = grad_query.astype(BF)
        for j in range(blocks):
            there = slice(j * BLOCK, (j + 1) * BLOCK)
            result[1, head, :, there] = turn(
                grad_keys[j], cosine[:, there], sine[:, there]
            ).astype(BF)
            result[2, head, :, there] = grad_values[j].astype(BF)
        return carry

    lax.fori_loop(0, heads, one_head, 0)
    for c in range(n):
        results[c][...] = result[:, :, :, lanes(places_ref[c], count)]


def forward_attention(places, start, chunks):
    n = len(chunks)
    _, heads, _, count = chunks[0].shape
    seq_len = n * count
    pairs = heads * seq_len * seq_len // 2
    *outs, log_total = call(
        lambda *refs: attend_forward(n, *refs),
        [places, start, *chunks],
        [((heads, HEAD_DIM, count), BF)] * n + [((heads, 1, seq_len), F32)],
        [
            pltpu.VMEM((3, heads, HEAD_DIM, seq_len), BF),
            pltpu.VMEM((heads, HEAD_DIM, seq_len), BF),
        ],
        flops=pairs * 4 * HEAD_DIM * 4,
        exps=pairs,
        scalars=1,
    )
    return outs, log_total


def backward_attention(places, start, cosine, sine, log_total, chunks, outs, grads):
    n = len(chunks)
    _, heads, _, count = chunks[0].shape
    seq_len = n * count
    pairs = heads * seq_len * seq_len // 2
    return call(
        lambda *refs: attend_backward(n, *refs),
        [places, start, cosine, sine, log_total, *chunks, *outs, *grads],
        [((3, heads, HEAD_DIM, count), BF)] * n,
        [
            pltpu.VMEM((3, heads, HEAD_DIM, seq_len), BF),
            pltpu.VMEM((heads, HEAD_DIM, seq_len), BF),
            pltpu.VMEM((heads, HEAD_DIM, seq_len), BF),
            pltpu.VMEM((3, heads, HEAD_DIM, seq_len), BF),
        ],
        flops=pairs * 10 * HEAD_DIM * 4,
        exps=pairs,
        scalars=1,
    )


def out_kernel(
    mixed_ref, act_ref, out_full_ref, down_full_ref, out_first_ref, down_first_ref, *rest
):
    arrived_ref = rest[0] if len(rest) % 2 else None
    piece_ref, low_ref = rest[len(rest) % 2 :][:2]
    rank = out_first_ref.shape[1]
    cols, count = out_full_ref.shape[0], act_ref.shape[0]
    mixed = mixed_ref[...].reshape(cols, count)
    act = act_ref[...]
    total = mm(mixed, out_full_ref[...], 0, 0) + mm(act, down_full_ref[...], 1, 0)
    if arrived_ref is not None:
        total = total + arrived_ref[...].astype(F32)
    piece_ref[...] = total.astype(piece_ref.dtype)
    if len(rest) > 3:
        rest[-2][...] = total.astype(BF)
        rest[-1][...] = jnp.zeros(rest[-1].shape, BF)
    low_ref[:, :rank] = mm(mixed, out_first_ref[...], 0, 0).astype(BF)
    low_ref[:, rank:] = mm(act, down_first_ref[...], 1, 0).astype(BF)


def out_piece(
    mixed, act, out_full, down_full, out_first, down_first, dtype, arrived=None, both=False
):
    count, hidden = act.shape
    width, rank = out_full.shape[1], out_first.shape[1]
    operands = [mixed, act, out_full, down_full, out_first, down_first]
    return call(
        out_kernel,
        operands + ([] if arrived is None else [arrived]),
        [((count, width), dtype), ((count, 2 * rank), BF)]
        + ([((count, width), BF), ((8, 128), BF)] if both else []),
        flops=2 * count * (out_full.shape[0] + hidden) * width,
    )


def pull_kernel(
    g_ref,
    slope_ref,
    out_full_ref,
    down_ref,
    out_second_ref,
    down_second_ref,
    mixed_ref,
    low_ref,
    up_ref,
):
    grad = g_ref[...]
    mixed = mm(out_full_ref[...], grad, 1, 1)
    for head in range(mixed.shape[0] // HEAD_DIM):
        mixed_ref[head] = mixed[head * HEAD_DIM : (head + 1) * HEAD_DIM].astype(BF)
    rank = out_second_ref.shape[0]
    low_ref[:, :rank] = (ADAPTER_SCALE * mm(grad, out_second_ref[...], 1, 1)).astype(BF)
    low_ref[:, rank:] = (ADAPTER_SCALE * mm(grad, down_second_ref[...], 1, 1)).astype(BF)
    for begin in range(0, up_ref.shape[1], BLOCK):
        part = slice(begin, begin + BLOCK)
        up_ref[:, part] = (
            mm(grad, down_ref[part], 1, 1) * slope_ref[:, part].astype(F32)
        ).astype(BF)


def pull_back(grad, slope, out_full, down_full, out_second, down_second):
    count, width = grad.shape
    hidden, cols, twice = slope.shape[1], out_full.shape[0], 2 * out_second.shape[0]
    return call(
        pull_kernel,
        [grad, slope, out_full, down_full, out_second, down_second],
        [
            ((cols // HEAD_DIM, HEAD_DIM, count), BF),
            ((count, twice), BF),
            ((count, hidden), BF),
        ],
        flops=2 * count * width * (cols + hidden + twice),
    )


def slot_code(slot, bits):
    return sum(((slot >> b) & 1) << (bits - 1 - b) for b in range(bits))


def part_sizes(members):
    sizes = []
    while members > 1:
        members //= 2
        sizes.append(members)
    return sizes + [1]


def spread(me, members, fields, parts):
    bits = members.bit_length() - 1
    for size, part in zip(part_sizes(members), parts):
        for k in range(size):
            slot = k + (size if part is not parts[-1] else 0)
            owner = me ^ slot_code(slot, bits)
            low = 0
            for field in fields:
                rows = field.shape[0] // members
                at = pl.ds(pl.multiple_of(owner * rows, rows), rows)
                part[k, low : low + rows] = field[at]
                low += rows


def gather_spread(me, members, fields, parts):
    bits = members.bit_length() - 1
    for size, part in zip(part_sizes(members), parts):
        for k in range(size):
            slot = k + (size if part is not parts[-1] else 0)
            owner = me ^ slot_code(slot, bits)
            low = 0
            for field in fields:
                rows = field.shape[0] // members
                at = pl.ds(pl.multiple_of(owner * rows, rows), rows)
                field[at] = part[k, low : low + rows]
                low += rows


def early_kernel(chunks, packs, me_ref, up_second_ref, gain_ref, *rest):
    fields = 8
    more = rest[fields * chunks :]
    before, more = (more[:3], more[3:]) if packs != 1 else (None, more)
    if packs > 1:
        parts, more = more[: packs - 1], more[packs - 1 :]
        out_ref, shared_ref, split_ref = more
    else:
        shared_ref, split_ref, out_ref = more
    rank = up_second_ref.shape[0]
    shared_up, shared_out, up_b, down_a, out_a = 0.0, 0.0, 0.0, 0.0, 0.0
    for c in range(chunks):
        grad, grad_up, hat, act, low, low_out, grad_low, mixed = (
            ref[...] for ref in rest[c * fields : (c + 1) * fields]
        )
        mixed = mixed.reshape(-1, mixed.shape[-1])
        low_up_grad = (ADAPTER_SCALE * mm(grad_up, up_second_ref[...], 1, 1)).astype(BF)
        shared_up = shared_up + mm(low_up_grad, hat, 0, 0)
        shared_out = shared_out + mm(low_out, grad, 0, 0)
        up_b = up_b + mm(low[:, 3 * rank :], grad_up, 0, 0)
        down_a = down_a + mm(grad_low[:, rank:], act, 0, 0)
        out_a = out_a + mm(grad_low[:, :rank], mixed, 0, 1)
    shared_up = shared_up * gain_ref[...]
    shared_out = ADAPTER_SCALE * shared_out
    up_b = ADAPTER_SCALE * up_b
    if before is not None:
        shared_up = shared_up + before[0][:rank]
        shared_out = shared_out + before[0][rank:]
        up_b = up_b + before[1][:rank]
        down_a = down_a + before[1][rank:]
        out_a = out_a + before[2][...]
    shared_ref[:rank] = shared_up.astype(shared_ref.dtype)
    shared_ref[rank:] = shared_out.astype(shared_ref.dtype)
    split_ref[:rank] = up_b.astype(split_ref.dtype)
    split_ref[rank:] = down_a.astype(split_ref.dtype)
    out_ref[...] = out_a.astype(out_ref.dtype)
    if packs > 1:
        members = 1 << (packs - 2)
        spread(me_ref[0], members, (shared_ref, split_ref), parts)


def part_shapes(members, rows, width):
    return [((size, rows, width), BF) for size in part_sizes(members)]


def early_sums(me, items, up_second, gain, before=None, members=0):
    width, hidden, rank = items[0][0].shape[1], items[0][1].shape[1], up_second.shape[0]
    cols = items[0][7].shape[0] * HEAD_DIM
    sums = [((3 * rank, width), F32), ((2 * rank, hidden), F32), ((rank, cols), F32)]
    operands = [me, up_second, gain] + [array for item in items for array in item]
    scratch = []
    if before is None:
        packs, outputs = 1, sums
    elif not members:
        packs, outputs = 0, sums
    else:
        packs = members.bit_length() + 1
        outputs = part_shapes(members, 5 * rank // members, width) + [((rank, cols), BF)]
        scratch = [pltpu.VMEM((3 * rank, width), BF), pltpu.VMEM((2 * rank, hidden), BF)]
    return call(
        lambda *refs: early_kernel(len(items), packs, *refs),
        operands + ([] if before is None else list(before)),
        outputs,
        scratch,
        flops=2 * len(items) * items[0][0].shape[0] * rank * 6 * width,
        scalars=1,
    )


def in_kernel(grad_pre_ref, grad_up_ref, in_full_ref, up_full_ref, *rest):
    piece_ref = rest[-1]
    grad_pre = grad_pre_ref[...].reshape(in_full_ref.shape[1], grad_up_ref.shape[0])
    total = mm(grad_pre, in_full_ref[...], 0, 1) + mm(grad_up_ref[...], up_full_ref[...], 1, 1)
    if len(rest) > 1:
        total = total + rest[0][...].astype(F32)
    piece_ref[...] = total.astype(piece_ref.dtype)


def in_piece(grad_pre, grad_up, in_full, up_full, dtype, arrived=None):
    count, hidden = grad_up.shape
    width = up_full.shape[0]
    operands = [grad_pre, grad_up, in_full, up_full]
    (piece,) = call(
        in_kernel,
        operands + ([] if arrived is None else [arrived]),
        [((count, width), dtype)],
        flops=2 * count * (in_full.shape[1] + hidden) * width,
    )
    return piece


def late_kernel(chunks, packs, me_ref, second_ref, gain_ref, *rest):
    fields = 3
    more = rest[fields * chunks :]
    rank, cols = second_ref.shape[1], second_ref.shape[2]
    out_ref, more = more[0], more[1:]
    shared_ref, split_ref = more[-2:]

    def one_third(i, carry):
        shared, split = 0.0, 0.0
        for c in range(chunks):
            grad_pre, low, hat = rest[c * fields : (c + 1) * fields]
            part = grad_pre[i].reshape(cols, -1)
            low_grad = (ADAPTER_SCALE * mm(part, second_ref[i], 0, 1)).astype(BF)
            shared = shared + mm(low_grad, hat[...], 0, 0)
            split = split + mm(low[:, lanes(i, rank)], part, 0, 1)
        shared_ref[pl.ds(pl.multiple_of(i * rank, rank), rank)] = (
            shared * gain_ref[...]
        ).astype(BF)
        split_ref[:, lanes(i, cols)] = (ADAPTER_SCALE * split).astype(BF)
        return carry

    lax.fori_loop(0, 3, one_third, 0, unroll=True)
    split_ref[:, 3 * cols :] = out_ref[...].astype(BF)
    if packs:
        spread(me_ref[0], 1 << (packs - 1), (shared_ref, split_ref), more[:packs])


def late_sums(me, items, second, gain, out_a, members=0):
    width, rank, cols = items[0][2].shape[1], second.shape[1], second.shape[2]
    sums = [((3 * rank, width), BF), ((rank, 4 * cols), BF)]
    packs = members.bit_length() if members else 0
    return call(
        lambda *refs: late_kernel(len(items), packs, *refs),
        [me, second, gain] + [array for item in items for array in item] + [out_a],
        part_shapes(members, 4 * rank // members, width) if packs else sums,
        [pltpu.VMEM(*spec) for spec in sums] if packs else [],
        flops=2 * len(items) * items[0][1].shape[0] * rank * 3 * (width + 2 * cols),
        scalars=1,
    )


def early_unpack_kernel(packs, me_ref, *rest):
    parts = rest[:packs]
    up_a_ref, out_b_ref, down_b_ref, up_b_ref, down_a_ref, shared_ref, split_ref = rest[packs:]
    rank = out_b_ref.shape[0]
    gather_spread(me_ref[0], 1 << (packs - 1), (shared_ref, split_ref), parts)
    up_a_ref[...] = shared_ref[:rank].astype(F32).T
    out_b_ref[...] = shared_ref[rank : 2 * rank].astype(F32)
    down_b_ref[...] = shared_ref[2 * rank :].astype(F32)
    up_b_ref[...] = split_ref[:rank].astype(F32)
    down_a_ref[...] = split_ref[rank:].astype(F32).T


def late_unpack_kernel(packs, me_ref, *rest):
    parts = rest[:packs]
    a_ref, b_ref, out_a_ref, shared_ref, split_ref = rest[packs:]
    rank, cols = b_ref.shape[1], b_ref.shape[2]
    gather_spread(me_ref[0], 1 << (packs - 1), (shared_ref, split_ref), parts)
    for i in range(3):
        a_ref[i] = shared_ref[i * rank : (i + 1) * rank].astype(F32).T
        b_ref[i] = split_ref[:, i * cols : (i + 1) * cols].astype(F32)
    out_a_ref[...] = split_ref[:, 3 * cols :].astype(F32).T


def output_kernel(x_ref, own_ref, *rest):
    total = x_ref[...].astype(F32) + own_ref[...]
    for ref in rest[:-1]:
        total = total + ref[...].astype(F32)
    rest[-1][...] = total.astype(BF)


def input_grad_kernel(x_ref, g_ref, own_ref, *rest):
    total = own_ref[...]
    for ref in rest[:-1]:
        total = total + ref[...].astype(F32)
    hat, scale = normalize(x_ref[...])
    mean_grad = jnp.mean(total, axis=-1, keepdims=True)
    mean_cross = jnp.mean(total * hat, axis=-1, keepdims=True)
    rest[-1][...] = g_ref[...].astype(F32) + scale * (total - mean_grad - hat * mean_cross)


def add_kernel(left_ref, right_ref, sum_ref):
    sum_ref[...] = (left_ref[...].astype(F32) + right_ref[...].astype(F32)).astype(BF)


def added(left, right):
    return call(add_kernel, [left, right], [(left.shape, BF)])[0]


def fold_kernel(arrived_ref, *rest):
    parts, results = rest[: len(rest) // 2], rest[len(rest) // 2 :]
    for part, result in zip(parts, results):
        size = part.shape[0]
        low = size if part is not parts[-1] else 0
        result[...] = (
            part[...].astype(F32) + arrived_ref[low : low + size].astype(F32)
        ).astype(BF)


def close_kernel(shared_ref, arrived_ref, split_ref, both_ref):
    rows = shared_ref.shape[1]
    both_ref[:, :rows] = (
        shared_ref[...].astype(F32) + arrived_ref[...].astype(F32)
    ).astype(BF)
    both_ref[:, rows:] = split_ref[...]


def join_kernel(first_ref, second_ref, both_ref):
    size = first_ref.shape[0]
    both_ref[:size] = first_ref[...]
    both_ref[size:] = second_ref[...]


def swap_pairs(n):
    return [(i, i ^ 1) for i in range(n)]


def mirror_pairs(n):
    return [(i, n - 1 - i) for i in range(n)]


def together(*values):
    return lax.optimization_barrier(values)


def after(value, *earlier):
    return lax.optimization_barrier((value, earlier))[0]


def ring_scatter(piece, pieces):
    up = [(i, (i + 1) % pieces) for i in range(pieces)]
    running = piece(1, None)
    for k in range(2, pieces + 1):
        running = piece(k % pieces, lax.ppermute(running, "tensor", up))
    return running


class GroupSum:
    def __init__(self, parts, n_shared):
        self.parts, self.n_shared = list(parts), n_shared
        self.members, self.n = lax.axis_size("dp"), lax.axis_size("tensor")
        self.bits = len(self.parts) - 1
        self.steps = [("down", b) for b in range(self.bits)]
        jump = 1
        while jump < self.n:
            self.steps.append(("across", jump))
            jump *= 2
        self.steps += [("back", b) for b in reversed(range(self.bits))]
        self.moving, self.at, self.results = None, 0, []

    def start(self):
        kind, which = self.steps[self.at]
        if kind == "across":
            pairs = [(k, k ^ which) for k in range(self.n)]
            self.moving = lax.ppermute(self.shared, "tensor", pairs)
        else:
            pairs = [(k, k ^ (1 << which)) for k in range(self.members)]
            sent = self.parts[which] if kind == "down" else self.have
            self.moving = lax.ppermute(sent, "dp", pairs)

    def finish(self, *earlier):
        kind, which = self.steps[self.at]
        arrived = after(self.moving, *earlier) if earlier else self.moving
        if kind == "down":
            later = self.parts[which + 1 :]
            self.parts[which + 1 :] = call(
                fold_kernel, [arrived, *later], [(part.shape, BF) for part in later]
            )
            if which == self.bits - 1:
                own = self.parts[-1]
                self.shared, self.split = own[:, : self.n_shared], own[:, self.n_shared :]
            value = self.parts[-1]
        elif kind == "across":
            if self.steps[self.at + 1][0] == "back":
                (self.have,) = call(
                    close_kernel,
                    [self.shared, arrived, self.split],
                    [(self.parts[-1].shape, BF)],
                )
                self.results, value = [self.have], self.have
            else:
                self.shared = value = added(self.shared, arrived)
        else:
            self.results.append(arrived)
            value = arrived
            if which:
                rows = self.have.shape
                (self.have,) = call(
                    join_kernel, [self.have, arrived], [((2 * rows[0], *rows[1:]), BF)]
                )
                value = self.have
        self.at += 1
        return value

    def rest(self):
        while self.at < len(self.steps):
            self.start()
            self.finish()
        return self.results[::-1]


def slow_parts(me, shared, split, members):
    bits = members.bit_length() - 1
    width = shared.shape[1]
    both = jnp.concatenate(
        [
            shared.astype(BF).reshape(members, -1, width),
            split.astype(BF).reshape(members, -1, width),
        ],
        axis=1,
    )
    order = jnp.asarray([slot_code(slot, bits) for slot in range(members)], jnp.int32) ^ me
    both = both[order]
    parts, top = [], members
    for size in part_sizes(members)[:-1]:
        parts.append(both[size:top])
        top = size
    return parts + [both[:1]]


def slow_whole(me, parts, n_shared, members):
    bits = members.bit_length() - 1
    both = jnp.concatenate(parts[::-1], axis=0)
    order = jnp.asarray([slot_code(slot, bits) for slot in range(members)], jnp.int32)
    both = both[order[jnp.arange(members, dtype=jnp.int32) ^ me]].astype(F32)
    width = both.shape[-1]
    return both[:, :n_shared].reshape(-1, width), both[:, n_shared:].reshape(-1, width)


def normalize(inputs):
    values = inputs.astype(F32)
    center = values - jnp.mean(values, axis=-1, keepdims=True)
    inv_scale = lax.rsqrt(jnp.mean(center * center, axis=-1, keepdims=True) + EPSILON)
    return center * inv_scale, inv_scale


def whole_step(
    layer_input,
    document_lengths,
    attention_norm_gain,
    feedfwd_norm_gain,
    query_key_value_weight,
    output_weight,
    up_weight,
    down_weight,
    adapter_query_key_value_first,
    adapter_query_key_value_second,
    adapter_output_first,
    adapter_output_second,
    adapter_up_first,
    adapter_up_second,
    adapter_down_first,
    adapter_down_second,
    cotangent,
):
    own_x, own_g = layer_input[0], cotangent[0]
    shard_len, width = own_x.shape
    n = lax.axis_size("tensor")
    me = lax.axis_index("tensor")
    seq_len = shard_len * n
    rank = adapter_up_first.shape[1]
    cols = query_key_value_weight.shape[2]
    hidden = up_weight.shape[1]
    swap, mirror = swap_pairs(n), mirror_pairs(n)
    short = n == 4

    def send(value, pairs):
        return lax.ppermute(value, "tensor", pairs)

    members = lax.axis_size("dp")
    bits = members.bit_length() - 1
    tidy = short and hidden == width and 4 * cols == width and rank % (16 * members) == 0
    if short:
        owners = [me, me ^ 1, n - 1 - me, (n - 1 - me) ^ 1]
    else:
        owners = [lax.rem(me - k + n, n) for k in range(n)]
    places = jnp.stack(owners).astype(jnp.int32)
    me_dp = lax.axis_index("dp").astype(jnp.int32).reshape(1)
    places, me_dp, own_x = together(places, me_dp, own_x)
    turns = call(
        places_kernel,
        [places, document_lengths],
        [((1, seq_len), jnp.int32), ((HALF, seq_len), F32), ((HALF, seq_len), F32)]
        + [((HALF, shard_len), F32)] * (2 * n),
        scalars=2,
    )
    start, cosine, sine, turns = turns[0], turns[1], turns[2], turns[3:]
    gain_a, gain_m = attention_norm_gain[None], feedfwd_norm_gain[None]
    weights = (
        query_key_value_weight,
        adapter_query_key_value_first,
        adapter_query_key_value_second,
        adapter_up_first,
        up_weight,
        adapter_up_second,
    )

    def projected(k, rows):
        return project(rows, (gain_a, gain_m), (turns[k], turns[n + k]), weights)

    def merged():
        return merge_weights(
            query_key_value_weight,
            up_weight,
            output_weight,
            down_weight,
            (adapter_query_key_value_first, adapter_query_key_value_second),
            (adapter_up_first, adapter_up_second),
            (adapter_output_first, adapter_output_second),
            (adapter_down_first, adapter_down_second),
            gain_a,
            gain_m,
        )

    outward, inward, middle = [(0, 1), (3, 2)], [(1, 0), (2, 3)], [(1, 2), (2, 1)]
    if short:
        x_near, x_facing = send(own_x, swap), send(own_x, mirror)
        full = merged()
        first = projected(0, own_x)
        x_near, x_facing, first, full, own_g = together(x_near, x_facing, first, full, own_g)
        x_far = send(x_facing, swap)
        g_near, g_mid = send(own_g, swap), send(own_g, middle)
        state = [first, projected(1, x_near), projected(2, x_facing)]
        x_far, state = together(x_far, state)
        state = state + [projected(3, x_far)]
    else:
        full = merged()
        up_ring = [(i, (i + 1) % n) for i in range(n)]
        state, moving = [projected(0, own_x)], own_x
        for k in range(1, n):
            moving = send(moving, up_ring)
            state.append(projected(k, moving))
    in_full, up_full, out_full, down_full = full
    qkv, low, hat, act, slope = (list(field) for field in zip(*state))
    mixed, log_total = forward_attention(places, start, qkv)
    low_out = [None] * n

    def out_part(k, dtype, arrived=None, both=False):
        piece, low_out[k], *more = out_piece(
            mixed[k],
            act[k],
            out_full,
            down_full,
            adapter_output_first,
            adapter_down_first,
            dtype,
            arrived,
            both,
        )
        return (piece, more[0]) if both else piece

    def pulled(k, grad):
        return pull_back(
            grad,
            slope[k],
            out_full,
            down_full,
            adapter_output_second,
            adapter_down_second,
        )

    def early_item(k, grad, back):
        return (grad, back[2], hat[k], act[k], low[k], low_out[k], back[1], mixed[k])

    if short:
        y_facing, y_facing_low = out_part(2, F32, both=True)
        y_far, y_far_low = out_part(3, F32, both=True)
        y_1, y_2 = send(y_facing_low, outward), send(y_far_low, outward)
        g_near, g_mid = after((g_near, g_mid), y_facing, y_far)
        g_mid_far, g_end_far = send(g_near, middle), send(g_mid, inward)
        y_near, y_own = out_part(1, F32), out_part(0, F32)
        backs = [pulled(0, own_g), pulled(1, g_near)]
        g_mid_far, g_end_far = after((g_mid_far, g_end_far), backs, y_near, y_own)
        g_end = send(g_mid_far, inward)
        g_far = added(g_mid_far, g_end_far)
        y_3 = send(added(y_far, after(y_1, g_far)), middle)
        backs = backs + [None, pulled(3, g_far)]
        all_g = [own_g, g_near, None, g_far]
        before = early_sums(
            me_dp,
            [early_item(k, all_g[k], backs[k]) for k in (0, 1, 3)],
            adapter_up_second,
            gain_m,
        )
        y_5 = send(added(y_facing, after(y_2, before)), middle)
        g_end = after(g_end, before)
        g_facing = added(g_mid, g_end)
        backs[2] = pulled(2, g_facing)
        early = early_sums(
            me_dp,
            [early_item(2, g_facing, backs[2])],
            adapter_up_second,
            gain_m,
            before,
            members if tidy else 0,
        )
        y_near = added(y_near, after(y_3, early))
        y_4 = send(y_near, swap)
    else:
        y_own = ring_scatter(lambda k, arrived: out_part(k, BF if k else F32, arrived), n)
        backs, moving, all_g = [pulled(0, own_g)], own_g, [own_g]
        for k in range(1, n):
            moving = send(moving, up_ring)
            all_g.append(moving)
            backs.append(pulled(k, moving))
        early = early_sums(
            me_dp, [early_item(k, all_g[k], backs[k]) for k in range(n)], adapter_up_second, gain_m
        )

    *early, out_a = early
    if not tidy:
        early = slow_parts(me_dp[0], early[0], early[1].reshape(-1, width), members)
    early = GroupSum(early, 3 * rank // members)
    early.start()
    grads_mixed = [back[0] for back in backs]
    if short:
        last = early.finish()
        early.start()
        grads_mixed = after(grads_mixed, y_near, last)
    grad_pre = backward_attention(places, start, cosine, sine, log_total, qkv, mixed, grads_mixed)

    def in_part(k, dtype, arrived=None, last=None):
        pre = grad_pre[k] if last is None else after(grad_pre[k], last)
        return in_piece(pre, backs[k][2], in_full, up_full, dtype, arrived)

    def early_whole(parts):
        if not tidy:
            early_a, early_b = slow_whole(me_dp[0], parts, 3 * rank // members, members)
            early_b = early_b.reshape(2 * rank, hidden)
            return (
                early_a[:rank].T,
                early_a[rank : 2 * rank],
                early_a[2 * rank :],
                early_b[:rank],
                early_b[rank:].T,
            )
        return call(
            lambda *refs: early_unpack_kernel(bits + 1, *refs),
            [me_dp, *parts],
            [
                ((width, rank), F32),
                ((rank, width), F32),
                ((rank, width), F32),
                ((rank, hidden), F32),
                ((hidden, rank), F32),
            ],
            [pltpu.VMEM((3 * rank, width), BF), pltpu.VMEM((2 * rank, width), BF)],
            scalars=1,
        )

    def late_parts():
        late = late_sums(
            me_dp,
            [(grad_pre[k], low[k], hat[k]) for k in range(n)],
            adapter_query_key_value_second,
            gain_a,
            out_a,
            members if tidy else 0,
        )
        if not tidy:
            late = slow_parts(me_dp[0], late[0], late[1].reshape(-1, width), members)
        return GroupSum(late, 3 * rank // members)

    if short:
        last = early.finish(grad_pre)
        early.start()
        late = late_parts()
        late.start()
        dx_far = in_part(3, BF)
        last = late.finish(dx_far)
        late.start()
        last = early.finish(last)
        early.start()
        dx_swap = send(dx_far, swap)
        dx_near, dx_own = in_part(1, BF, last=last), in_part(0, F32, last=last)
        last = early.finish(dx_near, dx_own)
        early.start()
        last = late.finish(last)
        late.start()
        dx_facing = in_part(2, BF, after(dx_swap, last))
        last = late.finish(dx_facing)
        late.start()
        last = early.finish(last)
        early.start()
        last = late.finish(last)
        late.start()
        dx_a = send(dx_near, swap)
        dx_b = send(dx_facing, mirror)
        last = early.finish(last)
        early.start()
        (layer_output,) = call(
            output_kernel,
            [own_x, y_own, *after((y_4, y_5), last)],
            [((shard_len, width), BF)],
        )
        last = late.finish(last, layer_output)
        late.start()
        last = early.finish(last)
        early.start()
        last = late.finish(last)
        late.start()
        early.finish(last)
        early_done = early_whole(early.rest())
        last = late.finish(early_done)
        late.start()
        dx_parts = [dx_own, *after((dx_a, dx_b), last)]
    else:
        (layer_output,) = call(output_kernel, [own_x, y_own], [((shard_len, width), BF)])
        dx_parts = [
            ring_scatter(lambda k, arrived: in_part(k, BF if k else F32, arrived), n)
        ]
        early.finish()
        late = late_parts()
        early_done = early_whole(early.rest())
    (grad_in,) = call(
        input_grad_kernel, [own_x, own_g, *dx_parts], [((shard_len, width), F32)]
    )

    up_a, out_b, down_b, up_b, down_a = early_done
    late = late.rest()
    if tidy:
        a_qkv, b_qkv, out_a = call(
            lambda *refs: late_unpack_kernel(bits + 1, *refs),
            [me_dp, *late],
            [((3, width, rank), F32), ((3, rank, cols), F32), ((cols, rank), F32)],
            [pltpu.VMEM((3 * rank, width), BF), pltpu.VMEM((rank, width), BF)],
            scalars=1,
        )
    else:
        late_a, late_b = slow_whole(me_dp[0], late, 3 * rank // members, members)
        late_b = late_b.reshape(rank, 4 * cols)
        a_qkv = jnp.swapaxes(late_a.reshape(3, rank, width), 1, 2)
        b_qkv = jnp.stack([late_b[:, i * cols : (i + 1) * cols] for i in range(3)])
        out_a = late_b[:, 3 * cols :].T
    return (
        layer_output[None],
        grad_in[None],
        a_qkv,
        b_qkv,
        out_a,
        out_b,
        up_a,
        up_b,
        down_a,
        down_b,
    )


def solution(mesh):
    in_specs = (
        P("dp", "tensor", None),
        P("dp", None),
        P(),
        P(),
        P(None, None, "tensor"),
        P("tensor", None),
        P(None, "tensor"),
        P("tensor", None),
        P(),
        P(None, None, "tensor"),
        P("tensor", None),
        P(),
        P(),
        P(None, "tensor"),
        P("tensor", None),
        P(),
        P("dp", "tensor", None),
    )
    out_specs = (
        P("dp", "tensor", None),
        P("dp", "tensor", None),
        P(),
        P(None, None, "tensor"),
        P("tensor", None),
        P(),
        P(),
        P(None, "tensor"),
        P("tensor", None),
        P(),
    )
    return jax.shard_map(
        whole_step, mesh=mesh, in_specs=in_specs, out_specs=out_specs, check_vma=False
    )
```

profile of v0, /device:TPU:0, one launch (start us, length us, event | category | flops | bytes accessed | tf_op | source)
XLA Modules:
  0.0 211.0 jit_solution(12046756917171557983)
XLA Ops:
  0.7 3.1 %collective-permute-start = (bf16[256,1024]{1,0:T(8,128)(2,1)}, bf16[256,1024]{1,0:T(8,128)(2,1)S(1)}, u32[]{:S(2)}, u32[]{:S(2)}) collective-permute-start(bf16[256,1024]{1,0:T(8,128)(2,1)} %bitcast.11), channel_id=1, source_target_pairs={{0,1},{1,0},{2,3},{3,2},{4,5},{5,4},{6,7},{7,6},{8,9},{9,8},{10,11... | collective-permute-start | bytes 1572872 | tf_op jit(solution)/shard_map/ppermute | solution.py:895
  3.8 2.5 %collective-permute-start.1 = (bf16[256,1024]{1,0:T(8,128)(2,1)}, bf16[256,1024]{1,0:T(8,128)(2,1)S(1)}, u32[]{:S(2)}, u32[]{:S(2)}) collective-permute-start(bf16[256,1024]{1,0:T(8,128)(2,1)} %bitcast.12), channel_id=1, source_target_pairs={{0,3},{1,2},{2,1},{3,0},{4,7},{5,6},{6,5},{7,4},{8,11},{9,10},{10,... | collective-permute-start | bytes 1572872 | tf_op jit(solution)/shard_map/ppermute | solution.py:895
  22.3 2.8 %shard_map.242 = (bf16[1024,768]{1,0:T(8,128)(2,1)S(1)}, bf16[1024,1024]{1,0:T(8,128)(2,1)S(1)}, bf16[256,1024]{1,0:T(8,128)(2,1)S(1)}, bf16[1024,1024]{1,0:T(8,128)(2,1)S(1)}) custom-call(bf16[3,1024,256]{2,1,0:T(8,128)(2,1)S(1)} %copy-done.2, bf16[3,1024,128]{2,1,0:T(8,128)(2,1)S(1)} %copy-done.4, bf16[3,128,256]{2,1,0:T(8,128)(2,1)S(1)} %copy-done.7, ...), custom_call_target="tpu_custom_call" | custom-call | flops 805306368 | bytes 12582912 | tf_op jit(solution)/shard_map/pallas_call | solution.py:140
  25.2 4.3 %shard_map.241 = (bf16[3,4,64,256]{3,2,1,0:T(8,128)(2,1)S(1)}, bf16[256,512]{1,0:T(8,128)(2,1)S(1)}, bf16[256,1024]{1,0:T(8,128)(2,1)S(1)}, bf16[256,1024]{1,0:T(8,128)(2,1)S(1)}, bf16[256,1024]{1,0:T(8,128)(2,1)S(1)}) custom-call(bf16[256,1024]{1,0:T(8,128)(2,1)S(1)} %bitcast.13, f32[1,1024]{1,0:T(1,128)S(1)} %bitcast.29, f32[1,1024]{1,0:T(1,128)S(1)} %bitcast.22, ...), custom_call_target="tpu_custom_call" | custom-call | flops 1207959552 | bytes 4456448 | tf_op jit(solution)/shard_map/pallas_call | solution.py:33
  32.3 4.3 %shard_map.244 = (bf16[3,4,64,256]{3,2,1,0:T(8,128)(2,1)S(1)}, bf16[256,512]{1,0:T(8,128)(2,1)S(1)}, bf16[256,1024]{1,0:T(8,128)(2,1)S(1)}, bf16[256,1024]{1,0:T(8,128)(2,1)S(1)}, bf16[256,1024]{1,0:T(8,128)(2,1)S(1)}) custom-call(bf16[256,1024]{1,0:T(8,128)(2,1)S(1)} %collective-permute-done.1.x_ref, f32[1,1024]{1,0:T(1,128)S(1)} %bitcast.30, ...), custom_call_target="tpu_custom_call" | custom-call | flops 1207959552 | bytes 4456448 | tf_op jit(solution)/shard_map/pallas_call | solution.py:33
  36.6 4.3 %shard_map.243 = (bf16[3,4,64,256]{3,2,1,0:T(8,128)(2,1)S(1)}, bf16[256,512]{1,0:T(8,128)(2,1)S(1)}, bf16[256,1024]{1,0:T(8,128)(2,1)S(1)}, bf16[256,1024]{1,0:T(8,128)(2,1)S(1)}, bf16[256,1024]{1,0:T(8,128)(2,1)S(1)}) custom-call(bf16[256,1024]{1,0:T(8,128)(2,1)S(1)} %collective-permute-done.x_ref, f32[1,1024]{1,0:T(1,128)S(1)} %bitcast.31, ...), custom_call_target="tpu_custom_call" | custom-call | flops 1207959552 | bytes 4456448 | tf_op jit(solution)/shard_map/pallas_call | solution.py:33
  40.8 3.5 %collective-permute-done.2.x_ref = bf16[256,1024]{1,0:T(8,128)(2,1)S(1)} collective-permute-done((bf16[256,1024]{1,0:T(8,128)(2,1)S(1)}, bf16[256,1024]{1,0:T(8,128)(2,1)S(1)}, u32[]{:S(2)}, u32[]{:S(2)}) %collective-permute-start.2) | collective-permute-done | bytes 524320 | tf_op jit(solution)/shard_map/ppermute | solution.py:895
  44.4 4.3 %shard_map.245 = (bf16[3,4,64,256]{3,2,1,0:T(8,128)(2,1)S(1)}, bf16[256,512]{1,0:T(8,128)(2,1)S(1)}, bf16[256,1024]{1,0:T(8,128)(2,1)S(1)}, bf16[256,1024]{1,0:T(8,128)(2,1)S(1)}, bf16[256,1024]{1,0:T(8,128)(2,1)S(1)}) custom-call(bf16[256,1024]{1,0:T(8,128)(2,1)S(1)} %collective-permute-done.2.x_ref, f32[1,1024]{1,0:T(1,128)S(1)} %bitcast.32, ...), custom_call_target="tpu_custom_call" | custom-call | flops 1207959552 | bytes 4456448 | tf_op jit(solution)/shard_map/pallas_call | solution.py:33
  48.6 7.2 %shard_map.246 = (bf16[4,64,256]{2,1,0:T(8,128)(2,1)S(1)}, bf16[4,64,256]{2,1,0:T(8,128)(2,1)S(1)}, bf16[4,64,256]{2,1,0:T(8,128)(2,1)S(1)}, bf16[4,64,256]{2,1,0:T(8,128)(2,1)S(1)}, f32[4,1,1024]{2,1,0:T(1,128)S(1)}) custom-call(s32[4]{0:T(128)S(1)} %pad_add_fusion.places_ref.refs_0_, s32[1,1024]{1,0:T(1,128)S(1)} %get-tuple-element.172.refs_1_, ...), custom_call_target="tpu_custom_call" | custom-call | flops 2147483648 | bytes 1081344 | tf_op jit(solution)/shard_map/pallas_call | solution.py:33
  65.5 7.3 %collective-permute-done.7.right_ref = bf16[256,1024]{1,0:T(8,128)(2,1)S(1)} collective-permute-done((bf16[256,1024]{1,0:T(8,128)(2,1)S(1)}, bf16[256,1024]{1,0:T(8,128)(2,1)S(1)}, u32[]{:S(2)}, u32[]{:S(2)}) %collective-permute-start.7) | collective-permute-done | bytes 524320 | tf_op jit(solution)/shard_map/ppermute | solution.py:895
  74.1 4.6 %collective-permute-start.3 = (bf16[256,1024]{1,0:T(8,128)(2,1)S(1)}, bf16[256,1024]{1,0:T(8,128)(2,1)S(1)}, u32[]{:S(2)}, u32[]{:S(2)}) collective-permute-start(bf16[256,1024]{1,0:T(8,128)(2,1)S(1)} %get-tuple-element.225), channel_id=1, source_target_pairs={{0,1},{3,2},{4,5},{7,6},{8,9},{11,10},{12,13},{15,14},{16,17},{19,... | collective-permute-start | bytes 1572872 | tf_op jit(solution)/shard_map/ppermute | solution.py:895
  80.0 2.2 %shard_map.256 = (f32[384,1024]{1,0:T(8,128)S(1)}, f32[256,1024]{1,0:T(8,128)S(1)}, f32[128,256]{1,0:T(8,128)S(1)}) custom-call(s32[1]{0:T(128)} %bitcast.4.refs_0_, bf16[128,1024]{1,0:T(8,128)(2,1)S(1)} %copy-done.6, f32[1,1024]{1,0:T(1,128)S(1)} %bitcast.26, bf16[256,1024]{1,0:T(8,128)(2,1)S(1)} %bitcast.19, ...), custom_call_target="tpu_custom_call" | custom-call | flops 1207959552 | bytes 5505024 | tf_op jit(solution)/shard_map/pallas_call | solution.py:33
  82.3 2.1 collective-permute-done.9.right_ref
  89.0 11.3 %shard_map.263 = (bf16[3,4,64,256]{3,2,1,0:T(8,128)(2,1)S(1)}, bf16[3,4,64,256]{3,2,1,0:T(8,128)(2,1)S(1)}, bf16[3,4,64,256]{3,2,1,0:T(8,128)(2,1)S(1)}, bf16[3,4,64,256]{3,2,1,0:T(8,128)(2,1)S(1)}) custom-call(s32[4]{0:T(128)S(1)} %pad_add_fusion.places_ref.refs_0_, s32[1,1024]{1,0:T(1,128)S(1)} %get-tuple-element.172.refs_1_, ...), custom_call_target="tpu_custom_call" | custom-call | flops 5368709120 | bytes 3145728 | tf_op jit(solution)/shard_map/pallas_call | solution.py:33
  100.3 3.5 %shard_map.265 = (bf16[4,64,1024]{2,1,0:T(8,128)(2,1)S(1)}, bf16[2,64,1024]{2,1,0:T(8,128)(2,1)S(1)}, bf16[1,64,1024]{2,1,0:T(8,128)(2,1)S(1)}, bf16[1,64,1024]{2,1,0:T(8,128)(2,1)S(1)}) custom-call(s32[1]{0:T(128)} %bitcast.4.refs_0_, bf16[3,128,256]{2,1,0:T(8,128)(2,1)S(1)} %copy-done.8, f32[1,1024]{1,0:T(1,128)S(1)} %bitcast.33, ...), custom_call_target="tpu_custom_call" | custom-call | flops 1207959552 | bytes 2097152 | tf_op jit(solution)/shard_map/pallas_call | solution.py:33
  105.5 15.8 %collective-permute-start.11 = (bf16[256,1024]{1,0:T(8,128)(2,1)S(1)}, bf16[256,1024]{1,0:T(8,128)(2,1)S(1)}, u32[]{:S(2)}, u32[]{:S(2)}) collective-permute-start(bf16[256,1024]{1,0:T(8,128)(2,1)S(1)} %get-tuple-element.270), channel_id=1, source_target_pairs={{0,1},{3,2},{4,5},{7,6},{8,9},{11,10},{12,13},{15,14},{16,17},{19,... | collective-permute-start | bytes 1572872 | tf_op jit(solution)/shard_map/ppermute | solution.py:895
  124.9 3.7 %collective-permute-done.15.arrived_ref = bf16[1,80,1024]{2,1,0:T(8,128)(2,1)S(1)} collective-permute-done((bf16[1,80,1024]{2,1,0:T(8,128)(2,1)S(1)}, bf16[1,80,1024]{2,1,0:T(8,128)(2,1)S(1)}, u32[]{:S(2)}, u32[]{:S(2)}) %collective-permute-start.15) | collective-permute-done | bytes 163872 | tf_op jit(solution)/shard_map/ppermute | solution.py:786
  128.7 5.2 %collective-permute-start.17 = (bf16[1,48,1024]{2,1,0:T(8,128)(2,1)S(1)}, bf16[1,48,1024]{2,1,0:T(8,128)(2,1)S(1)}, u32[]{:S(2)}, u32[]{:S(2)}) collective-permute-start(bf16[1,48,1024]{2,1,0:T(8,128)(2,1)S(1)} %slice.16.left_ref), channel_id=1, source_target_pairs={{0,1},{1,0},{2,3},{3,2},{4,5},{5,4},{6,7},{7,6},{8,9},{9,8},{10,11... | collective-permute-start | bytes 294920 | tf_op jit(solution)/shard_map/ppermute | solution.py:782
  136.2 9.9 %collective-permute-done.17.right_ref = bf16[1,48,1024]{2,1,0:T(8,128)(2,1)S(1)} collective-permute-done((bf16[1,48,1024]{2,1,0:T(8,128)(2,1)S(1)}, bf16[1,48,1024]{2,1,0:T(8,128)(2,1)S(1)}, u32[]{:S(2)}, u32[]{:S(2)}) %collective-permute-start.17) | collective-permute-done | bytes 98336 | tf_op jit(solution)/shard_map/ppermute | solution.py:782
  147.8 2.6 %collective-permute-start.18 = (bf16[1,48,1024]{2,1,0:T(8,128)(2,1)S(1)}, bf16[1,48,1024]{2,1,0:T(8,128)(2,1)S(1)}, u32[]{:S(2)}, u32[]{:S(2)}) collective-permute-start(bf16[1,48,1024]{2,1,0:T(8,128)(2,1)S(1)} %shard_map.271.shared_ref), channel_id=1, source_target_pairs={{0,2},{1,3},{2,0},{3,1},{4,6},{5,7},{6,4},{7,5},{8,10},{9,11},{10,... | collective-permute-start | bytes 294920 | tf_op jit(solution)/shard_map/ppermute | solution.py:782
  151.4 2.2 %collective-permute-start.10 = (bf16[256,1024]{1,0:T(8,128)(2,1)S(1)}, bf16[256,1024]{1,0:T(8,128)(2,1)S(1)}, u32[]{:S(2)}, u32[]{:S(2)}) collective-permute-start(bf16[256,1024]{1,0:T(8,128)(2,1)S(1)} %shard_map.260), channel_id=1, source_target_pairs={{0,1},{1,0},{2,3},{3,2},{4,5},{5,4},{6,7},{7,6},{8,9},{9,8},{10,11... | collective-permute-start | bytes 1572872 | tf_op jit(solution)/shard_map/ppermute | solution.py:895
  157.0 10.3 %collective-permute-done.23.right_ref = bf16[1,48,1024]{2,1,0:T(8,128)(2,1)S(1)} collective-permute-done((bf16[1,48,1024]{2,1,0:T(8,128)(2,1)S(1)}, bf16[1,48,1024]{2,1,0:T(8,128)(2,1)S(1)}, u32[]{:S(2)}, u32[]{:S(2)}) %collective-permute-start.23) | collective-permute-done | bytes 98336 | tf_op jit(solution)/shard_map/ppermute | solution.py:782
  167.9 1.9 collective-permute-start.26
  170.8 3.7 %collective-permute-done.26.arrived_ref = bf16[1,48,1024]{2,1,0:T(8,128)(2,1)S(1)} collective-permute-done((bf16[1,48,1024]{2,1,0:T(8,128)(2,1)S(1)}, bf16[1,48,1024]{2,1,0:T(8,128)(2,1)S(1)}, u32[]{:S(2)}, u32[]{:S(2)}) %collective-permute-start.26) | collective-permute-done | bytes 98336 | tf_op jit(solution)/shard_map/ppermute | solution.py:782
  176.1 5.3 %collective-permute-done.27.second_ref.refs_3_ = bf16[1,64,1024]{2,1,0:T(8,128)(2,1)S(1)} collective-permute-done((bf16[1,64,1024]{2,1,0:T(8,128)(2,1)S(1)}, bf16[1,64,1024]{2,1,0:T(8,128)(2,1)S(1)}, u32[]{:S(2)}, u32[]{:S(2)}) %collective-permute-start.27) | collective-permute-done | bytes 131104 | tf_op jit(solution)/shard_map/ppermute | solution.py:786
  182.6 2.6 %collective-permute-start.25 = (bf16[256,1024]{1,0:T(8,128)(2,1)S(1)}, bf16[256,1024]{1,0:T(8,128)(2,1)S(1)}, u32[]{:S(2)}, u32[]{:S(2)}) collective-permute-start(bf16[256,1024]{1,0:T(8,128)(2,1)S(1)} %shard_map.273), channel_id=1, source_target_pairs={{0,3},{1,2},{2,1},{3,0},{4,7},{5,6},{6,5},{7,4},{8,11},{9,10},{10,... | collective-permute-start | bytes 1572872 | tf_op jit(solution)/shard_map/ppermute | solution.py:895
  185.2 1.7 shard_map.282
  186.9 2.4 %collective-permute-done.29.second_ref.refs_2_ = bf16[2,64,1024]{2,1,0:T(8,128)(2,1)S(1)} collective-permute-done((bf16[2,64,1024]{2,1,0:T(8,128)(2,1)S(1)}, bf16[2,64,1024]{2,1,0:T(8,128)(2,1)S(1)}, u32[]{:S(2)}, u32[]{:S(2)}) %collective-permute-start.29) | collective-permute-done | bytes 262176 | tf_op jit(solution)/shard_map/ppermute | solution.py:786
  189.4 6.5 %collective-permute-done.24.rest_0_ = bf16[256,1024]{1,0:T(8,128)(2,1)S(1)} collective-permute-done((bf16[256,1024]{1,0:T(8,128)(2,1)S(1)}, bf16[256,1024]{1,0:T(8,128)(2,1)S(1)}, u32[]{:S(2)}, u32[]{:S(2)}) %collective-permute-start.24) | collective-permute-done | bytes 524320 | tf_op jit(solution)/shard_map/ppermute | solution.py:895
  195.9 11.8 %collective-permute-done.25.rest_1_ = bf16[256,1024]{1,0:T(8,128)(2,1)S(1)} collective-permute-done((bf16[256,1024]{1,0:T(8,128)(2,1)S(1)}, bf16[256,1024]{1,0:T(8,128)(2,1)S(1)}, u32[]{:S(2)}, u32[]{:S(2)}) %collective-permute-start.25) | collective-permute-done | bytes 524320 | tf_op jit(solution)/shard_map/ppermute | solution.py:895
  207.6 1.7 shard_map.284
  209.4 1.6 shard_map.285
  (135 shorter events, 54.0 us)
Async XLA Ops:
  0.7 28.8 %collective-permute-start = (bf16[256,1024]{1,0:T(8,128)(2,1)}, bf16[256,1024]{1,0:T(8,128)(2,1)S(1)}, u32[]{:S(2)}, u32[]{:S(2)}) collective-permute-start(bf16[256,1024]{1,0:T(8,128)(2,1)} %bitcast.11), channel_id=1, source_target_pairs={{0,1},{1,0},{2,3},{3,2},{4,5},{5,4},{6,7},{7,6},{8,9},{9,8},{10,11... | collective-permute-start | bytes 1572872 | tf_op jit(solution)/shard_map/ppermute | solution.py:895
  3.8 25.7 %collective-permute-start.1 = (bf16[256,1024]{1,0:T(8,128)(2,1)}, bf16[256,1024]{1,0:T(8,128)(2,1)S(1)}, u32[]{:S(2)}, u32[]{:S(2)}) collective-permute-start(bf16[256,1024]{1,0:T(8,128)(2,1)} %bitcast.12), channel_id=1, source_target_pairs={{0,3},{1,2},{2,1},{3,0},{4,7},{5,6},{6,5},{7,4},{8,11},{9,10},{10,... | collective-permute-start | bytes 1572872 | tf_op jit(solution)/shard_map/ppermute | solution.py:895
  29.5 14.9 %collective-permute-start.2 = (bf16[256,1024]{1,0:T(8,128)(2,1)S(1)}, bf16[256,1024]{1,0:T(8,128)(2,1)S(1)}, u32[]{:S(2)}, u32[]{:S(2)}) collective-permute-start(bf16[256,1024]{1,0:T(8,128)(2,1)S(1)} %collective-permute-done.1.x_ref), channel_id=1, source_target_pairs={{0,1},{1,0},{2,3},{3,2},{4,5},{5,4},{6,7},{7,6},{8,9},{9,8},{10,11... | collective-permute-start | bytes 1572872 | tf_op jit(solution)/shard_map/ppermute | solution.py:895
  30.2 28.7 %collective-permute-start.4 = (bf16[256,1024]{1,0:T(8,128)(2,1)S(1)}, bf16[256,1024]{1,0:T(8,128)(2,1)S(1)}, u32[]{:S(2)}, u32[]{:S(2)}) collective-permute-start(bf16[256,1024]{1,0:T(8,128)(2,1)S(1)} %bitcast.16), channel_id=1, source_target_pairs={{0,1},{1,0},{2,3},{3,2},{4,5},{5,4},{6,7},{7,6},{8,9},{9,8},{10,11... | collective-permute-start | bytes 1572872 | tf_op jit(solution)/shard_map/ppermute | solution.py:895
  31.6 27.4 %collective-permute-start.5 = (bf16[256,1024]{1,0:T(8,128)(2,1)S(1)}, bf16[256,1024]{1,0:T(8,128)(2,1)S(1)}, u32[]{:S(2)}, u32[]{:S(2)}) collective-permute-start(bf16[256,1024]{1,0:T(8,128)(2,1)S(1)} %bitcast.17), channel_id=1, source_target_pairs={{1,2},{2,1},{5,6},{6,5},{9,10},{10,9},{13,14},{14,13},{17,18},{18,... | collective-permute-start | bytes 1572872 | tf_op jit(solution)/shard_map/ppermute | solution.py:895
  59.0 6.6 %collective-permute-start.6 = (bf16[256,1024]{1,0:T(8,128)(2,1)S(1)}, bf16[256,1024]{1,0:T(8,128)(2,1)S(1)}, u32[]{:S(2)}, u32[]{:S(2)}) collective-permute-start(bf16[256,1024]{1,0:T(8,128)(2,1)S(1)} %collective-permute-done.4.g_ref.refs_11_), channel_id=1, source_target_pairs={{1,2},{2,1},{5,6},{6,5},{9,10},{10,9},{13,14},{14,13},{17,18},{18,... | collective-permute-start | bytes 1572872 | tf_op jit(solution)/shard_map/ppermute | solution.py:895
  59.7 13.2 %collective-permute-start.7 = (bf16[256,1024]{1,0:T(8,128)(2,1)S(1)}, bf16[256,1024]{1,0:T(8,128)(2,1)S(1)}, u32[]{:S(2)}, u32[]{:S(2)}) collective-permute-start(bf16[256,1024]{1,0:T(8,128)(2,1)S(1)} %collective-permute-done.5.left_ref), channel_id=1, source_target_pairs={{1,0},{2,3},{5,4},{6,7},{9,8},{10,11},{13,12},{14,15},{17,16},{18,... | collective-permute-start | bytes 1572872 | tf_op jit(solution)/shard_map/ppermute | solution.py:895
  72.8 11.5 %collective-permute-start.9 = (bf16[256,1024]{1,0:T(8,128)(2,1)S(1)}, bf16[256,1024]{1,0:T(8,128)(2,1)S(1)}, u32[]{:S(2)}, u32[]{:S(2)}) collective-permute-start(bf16[256,1024]{1,0:T(8,128)(2,1)S(1)} %collective-permute-done.6.left_ref), channel_id=1, source_target_pairs={{1,0},{2,3},{5,4},{6,7},{9,8},{10,11},{13,12},{14,15},{17,16},{18,... | collective-permute-start | bytes 1572872 | tf_op jit(solution)/shard_map/ppermute | solution.py:895
  74.1 12.7 %collective-permute-start.3 = (bf16[256,1024]{1,0:T(8,128)(2,1)S(1)}, bf16[256,1024]{1,0:T(8,128)(2,1)S(1)}, u32[]{:S(2)}, u32[]{:S(2)}) collective-permute-start(bf16[256,1024]{1,0:T(8,128)(2,1)S(1)} %get-tuple-element.225), channel_id=1, source_target_pairs={{0,1},{3,2},{4,5},{7,6},{8,9},{11,10},{12,13},{15,14},{16,17},{19,... | collective-permute-start | bytes 1572872 | tf_op jit(solution)/shard_map/ppermute | solution.py:895
  86.7 2.2 %collective-permute-start.13 = (bf16[4,80,1024]{2,1,0:T(8,128)(2,1)S(1)}, bf16[4,80,1024]{2,1,0:T(8,128)(2,1)S(1)}, u32[]{:S(2)}, u32[]{:S(2)}) collective-permute-start(bf16[4,80,1024]{2,1,0:T(8,128)(2,1)S(1)} %get-tuple-element.264), channel_id=1, source_target_pairs={{0,4},{4,0},{8,12},{12,8},{16,20},{20,16},{24,28},{28,24},{1,5},{5... | collective-permute-start | bytes 1966088 | tf_op jit(solution)/shard_map/ppermute | solution.py:786
  86.9 0.9 collective-permute-start.8
  103.8 20.4 %collective-permute-start.16 = (bf16[4,64,1024]{2,1,0:T(8,128)(2,1)S(1)}, bf16[4,64,1024]{2,1,0:T(8,128)(2,1)S(1)}, u32[]{:S(2)}, u32[]{:S(2)}) collective-permute-start(bf16[4,64,1024]{2,1,0:T(8,128)(2,1)S(1)} %get-tuple-element.290), channel_id=1, source_target_pairs={{0,4},{4,0},{8,12},{12,8},{16,20},{20,16},{24,28},{28,24},{1,5},{5... | collective-permute-start | bytes 1572872 | tf_op jit(solution)/shard_map/ppermute | solution.py:786
  104.0 18.5 %collective-permute-start.14 = (bf16[2,80,1024]{2,1,0:T(8,128)(2,1)S(1)}, bf16[2,80,1024]{2,1,0:T(8,128)(2,1)S(1)}, u32[]{:S(2)}, u32[]{:S(2)}) collective-permute-start(bf16[2,80,1024]{2,1,0:T(8,128)(2,1)S(1)} %get-tuple-element.272), channel_id=1, source_target_pairs={{0,8},{4,12},{8,0},{12,4},{16,24},{20,28},{24,16},{28,20},{1,9},{5... | collective-permute-start | bytes 983048 | tf_op jit(solution)/shard_map/ppermute | solution.py:786
  105.5 44.9 %collective-permute-start.11 = (bf16[256,1024]{1,0:T(8,128)(2,1)S(1)}, bf16[256,1024]{1,0:T(8,128)(2,1)S(1)}, u32[]{:S(2)}, u32[]{:S(2)}) collective-permute-start(bf16[256,1024]{1,0:T(8,128)(2,1)S(1)} %get-tuple-element.270), channel_id=1, source_target_pairs={{0,1},{3,2},{4,5},{7,6},{8,9},{11,10},{12,13},{15,14},{16,17},{19,... | collective-permute-start | bytes 1572872 | tf_op jit(solution)/shard_map/ppermute | solution.py:895
  122.4 31.2 %collective-permute-start.21 = (bf16[256,1024]{1,0:T(8,128)(2,1)S(1)}, bf16[256,1024]{1,0:T(8,128)(2,1)S(1)}, u32[]{:S(2)}, u32[]{:S(2)}) collective-permute-start(bf16[256,1024]{1,0:T(8,128)(2,1)S(1)} %shard_map.266), channel_id=1, source_target_pairs={{0,1},{1,0},{2,3},{3,2},{4,5},{5,4},{6,7},{7,6},{8,9},{9,8},{10,11... | collective-permute-start | bytes 1572872 | tf_op jit(solution)/shard_map/ppermute | solution.py:895
  122.6 6.0 %collective-permute-start.15 = (bf16[1,80,1024]{2,1,0:T(8,128)(2,1)S(1)}, bf16[1,80,1024]{2,1,0:T(8,128)(2,1)S(1)}, u32[]{:S(2)}, u32[]{:S(2)}) collective-permute-start(bf16[1,80,1024]{2,1,0:T(8,128)(2,1)S(1)} %get-tuple-element.289), channel_id=1, source_target_pairs={{0,16},{4,20},{8,24},{12,28},{16,0},{20,4},{24,8},{28,12},{1,17},{... | collective-permute-start | bytes 491528 | tf_op jit(solution)/shard_map/ppermute | solution.py:786
  124.3 21.8 %collective-permute-start.19 = (bf16[2,64,1024]{2,1,0:T(8,128)(2,1)S(1)}, bf16[2,64,1024]{2,1,0:T(8,128)(2,1)S(1)}, u32[]{:S(2)}, u32[]{:S(2)}) collective-permute-start(bf16[2,64,1024]{2,1,0:T(8,128)(2,1)S(1)} %get-tuple-element.303), channel_id=1, source_target_pairs={{0,8},{4,12},{8,0},{12,4},{16,24},{20,28},{24,16},{28,20},{1,9},{5... | collective-permute-start | bytes 786440 | tf_op jit(solution)/shard_map/ppermute | solution.py:786
  128.7 17.4 %collective-permute-start.17 = (bf16[1,48,1024]{2,1,0:T(8,128)(2,1)S(1)}, bf16[1,48,1024]{2,1,0:T(8,128)(2,1)S(1)}, u32[]{:S(2)}, u32[]{:S(2)}) collective-permute-start(bf16[1,48,1024]{2,1,0:T(8,128)(2,1)S(1)} %slice.16.left_ref), channel_id=1, source_target_pairs={{0,1},{1,0},{2,3},{3,2},{4,5},{5,4},{6,7},{7,6},{8,9},{9,8},{10,11... | collective-permute-start | bytes 294920 | tf_op jit(solution)/shard_map/ppermute | solution.py:782
  146.2 8.6 %collective-permute-start.20 = (bf16[1,64,1024]{2,1,0:T(8,128)(2,1)S(1)}, bf16[1,64,1024]{2,1,0:T(8,128)(2,1)S(1)}, u32[]{:S(2)}, u32[]{:S(2)}) collective-permute-start(bf16[1,64,1024]{2,1,0:T(8,128)(2,1)S(1)} %get-tuple-element.306), channel_id=1, source_target_pairs={{0,16},{4,20},{8,24},{12,28},{16,0},{20,4},{24,8},{28,12},{1,17},{... | collective-permute-start | bytes 393224 | tf_op jit(solution)/shard_map/ppermute | solution.py:786
  147.8 8.5 %collective-permute-start.18 = (bf16[1,48,1024]{2,1,0:T(8,128)(2,1)S(1)}, bf16[1,48,1024]{2,1,0:T(8,128)(2,1)S(1)}, u32[]{:S(2)}, u32[]{:S(2)}) collective-permute-start(bf16[1,48,1024]{2,1,0:T(8,128)(2,1)S(1)} %shard_map.271.shared_ref), channel_id=1, source_target_pairs={{0,2},{1,3},{2,0},{3,1},{4,6},{5,7},{6,4},{7,5},{8,10},{9,11},{10,... | collective-permute-start | bytes 294920 | tf_op jit(solution)/shard_map/ppermute | solution.py:782
  150.4 19.3 %collective-permute-start.12 = (bf16[256,1024]{1,0:T(8,128)(2,1)S(1)}, bf16[256,1024]{1,0:T(8,128)(2,1)S(1)}, u32[]{:S(2)}, u32[]{:S(2)}) collective-permute-start(bf16[256,1024]{1,0:T(8,128)(2,1)S(1)} %shard_map.261), channel_id=1, source_target_pairs={{1,2},{2,1},{5,6},{6,5},{9,10},{10,9},{13,14},{14,13},{17,18},{18,... | collective-permute-start | bytes 1572872 | tf_op jit(solution)/shard_map/ppermute | solution.py:895
  151.4 18.4 %collective-permute-start.10 = (bf16[256,1024]{1,0:T(8,128)(2,1)S(1)}, bf16[256,1024]{1,0:T(8,128)(2,1)S(1)}, u32[]{:S(2)}, u32[]{:S(2)}) collective-permute-start(bf16[256,1024]{1,0:T(8,128)(2,1)S(1)} %shard_map.260), channel_id=1, source_target_pairs={{0,1},{1,0},{2,3},{3,2},{4,5},{5,4},{6,7},{7,6},{8,9},{9,8},{10,11... | collective-permute-start | bytes 1572872 | tf_op jit(solution)/shard_map/ppermute | solution.py:895
  156.3 10.9 %collective-permute-start.22 = (bf16[1,80,1024]{2,1,0:T(8,128)(2,1)S(1)}, bf16[1,80,1024]{2,1,0:T(8,128)(2,1)S(1)}, u32[]{:S(2)}, u32[]{:S(2)}) collective-permute-start(bf16[1,80,1024]{2,1,0:T(8,128)(2,1)S(1)} %shard_map.275.first_ref.refs_4_), channel_id=1, source_target_pairs={{0,16},{4,20},{8,24},{12,28},{16,0},{20,4},{24,8},{28,12},{1,17},{... | collective-permute-start | bytes 491528 | tf_op jit(solution)/shard_map/ppermute | solution.py:786
  156.9 10.3 %collective-permute-start.23 = (bf16[1,48,1024]{2,1,0:T(8,128)(2,1)S(1)}, bf16[1,48,1024]{2,1,0:T(8,128)(2,1)S(1)}, u32[]{:S(2)}, u32[]{:S(2)}) collective-permute-start(bf16[1,48,1024]{2,1,0:T(8,128)(2,1)S(1)} %slice.18.left_ref), channel_id=1, source_target_pairs={{0,1},{1,0},{2,3},{3,2},{4,5},{5,4},{6,7},{7,6},{8,9},{9,8},{10,11... | collective-permute-start | bytes 294920 | tf_op jit(solution)/shard_map/ppermute | solution.py:782
  167.3 8.1 %collective-permute-start.28 = (bf16[2,80,1024]{2,1,0:T(8,128)(2,1)S(1)}, bf16[2,80,1024]{2,1,0:T(8,128)(2,1)S(1)}, u32[]{:S(2)}, u32[]{:S(2)}) collective-permute-start(bf16[2,80,1024]{2,1,0:T(8,128)(2,1)S(1)} %shard_map.277.first_ref), channel_id=1, source_target_pairs={{0,8},{4,12},{8,0},{12,4},{16,24},{20,28},{24,16},{28,20},{1,9},{5... | collective-permute-start | bytes 983048 | tf_op jit(solution)/shard_map/ppermute | solution.py:786
  167.9 6.6 %collective-permute-start.26 = (bf16[1,48,1024]{2,1,0:T(8,128)(2,1)S(1)}, bf16[1,48,1024]{2,1,0:T(8,128)(2,1)S(1)}, u32[]{:S(2)}, u32[]{:S(2)}) collective-permute-start(bf16[1,48,1024]{2,1,0:T(8,128)(2,1)S(1)} %shard_map.276.shared_ref), channel_id=1, source_target_pairs={{0,2},{1,3},{2,0},{3,1},{4,6},{5,7},{6,4},{7,5},{8,10},{9,11},{10,... | collective-permute-start | bytes 294920 | tf_op jit(solution)/shard_map/ppermute | solution.py:782
  175.4 9.8 %collective-permute-start.30 = (bf16[4,80,1024]{2,1,0:T(8,128)(2,1)S(1)}, bf16[4,80,1024]{2,1,0:T(8,128)(2,1)S(1)}, u32[]{:S(2)}, u32[]{:S(2)}) collective-permute-start(bf16[4,80,1024]{2,1,0:T(8,128)(2,1)S(1)} %shard_map.280), channel_id=1, source_target_pairs={{0,4},{4,0},{8,12},{12,8},{16,20},{20,16},{24,28},{28,24},{1,5},{5... | collective-permute-start | bytes 1966088 | tf_op jit(solution)/shard_map/ppermute | solution.py:786
  175.5 5.9 %collective-permute-start.27 = (bf16[1,64,1024]{2,1,0:T(8,128)(2,1)S(1)}, bf16[1,64,1024]{2,1,0:T(8,128)(2,1)S(1)}, u32[]{:S(2)}, u32[]{:S(2)}) collective-permute-start(bf16[1,64,1024]{2,1,0:T(8,128)(2,1)S(1)} %shard_map.279.first_ref.refs_4_), channel_id=1, source_target_pairs={{0,16},{4,20},{8,24},{12,28},{16,0},{20,4},{24,8},{28,12},{1,17},{... | collective-permute-start | bytes 393224 | tf_op jit(solution)/shard_map/ppermute | solution.py:786
  181.4 7.8 %collective-permute-start.29 = (bf16[2,64,1024]{2,1,0:T(8,128)(2,1)S(1)}, bf16[2,64,1024]{2,1,0:T(8,128)(2,1)S(1)}, u32[]{:S(2)}, u32[]{:S(2)}) collective-permute-start(bf16[2,64,1024]{2,1,0:T(8,128)(2,1)S(1)} %shard_map.281.first_ref), channel_id=1, source_target_pairs={{0,8},{4,12},{8,0},{12,4},{16,24},{20,28},{24,16},{28,20},{1,9},{5... | collective-permute-start | bytes 786440 | tf_op jit(solution)/shard_map/ppermute | solution.py:786
  182.1 13.7 %collective-permute-start.24 = (bf16[256,1024]{1,0:T(8,128)(2,1)S(1)}, bf16[256,1024]{1,0:T(8,128)(2,1)S(1)}, u32[]{:S(2)}, u32[]{:S(2)}) collective-permute-start(bf16[256,1024]{1,0:T(8,128)(2,1)S(1)} %shard_map.269), channel_id=1, source_target_pairs={{0,1},{1,0},{2,3},{3,2},{4,5},{5,4},{6,7},{7,6},{8,9},{9,8},{10,11... | collective-permute-start | bytes 1572872 | tf_op jit(solution)/shard_map/ppermute | solution.py:895
  182.6 25.0 %collective-permute-start.25 = (bf16[256,1024]{1,0:T(8,128)(2,1)S(1)}, bf16[256,1024]{1,0:T(8,128)(2,1)S(1)}, u32[]{:S(2)}, u32[]{:S(2)}) collective-permute-start(bf16[256,1024]{1,0:T(8,128)(2,1)S(1)} %shard_map.273), channel_id=1, source_target_pairs={{0,3},{1,2},{2,1},{3,0},{4,7},{5,6},{6,5},{7,4},{8,11},{9,10},{10,... | collective-permute-start | bytes 1572872 | tf_op jit(solution)/shard_map/ppermute | solution.py:895
  189.3 20.1 %collective-permute-start.31 = (bf16[4,64,1024]{2,1,0:T(8,128)(2,1)S(1)}, bf16[4,64,1024]{2,1,0:T(8,128)(2,1)S(1)}, u32[]{:S(2)}, u32[]{:S(2)}) collective-permute-start(bf16[4,64,1024]{2,1,0:T(8,128)(2,1)S(1)} %shard_map.283), channel_id=1, source_target_pairs={{0,4},{4,0},{8,12},{12,8},{16,20},{20,16},{24,28},{28,24},{1,5},{5... | collective-permute-start | bytes 1572872 | tf_op jit(solution)/shard_map/ppermute | solution.py:786
  (26 other events, 69.9 us)
where the time goes:
time: 212 us; the launch traced here: 211 us
  waiting for transfers between devices  69.6 us (33%)
  Pallas kernels  67.6 us (32%)
  starting transfers between devices  57.2 us (27%)
  local copies, waits for them, and re-layouts  15.4 us (7%)
    pallas_call x45, Pallas kernels, call(): pl.pallas_call(kernel, in_specs=[pl.BlockSpec(memory_space=space) for spa...  64.7 us
    ppermute x16, starting transfers between devices, send(): return lax.ppermute(value, 'tensor', pairs)  39.4 us
    ppermute x16, waiting for transfers between devices, send(): return lax.ppermute(value, 'tensor', pairs)  31.1 us
    ppermute x4, waiting for transfers between devices, start(): self.moving = lax.ppermute(self.shared, 'tensor', pairs)  25.3 us
    unnamed x52, local copies, waits for them, and re-layouts  15.4 us
    ppermute x12, waiting for transfers between devices, start(): self.moving = lax.ppermute(sent, 'dp', pairs)  13.2 us
    ppermute x4, starting transfers between devices, start(): self.moving = lax.ppermute(self.shared, 'tensor', pairs)  9.65 us
    ppermute x12, starting transfers between devices, start(): self.moving = lax.ppermute(sent, 'dp', pairs)  8.13 us
  transfers between devices with their start and end apart: 32, of which 14 were waited for; matrix products, arithmetic and copies ran while one was open for 0% of the time, Pallas kernels for 24%

commit v1 on v0

--- a/solution.py
+++ b/solution.py
@@ -327,17 +327,18 @@
         outs[c][...] = mixed_all[:, :, lanes(places_ref[c], count)]
 
 
-def attend_backward(n, places_ref, start_ref, cos_ref, sin_ref, log_ref, *rest):
+def attend_backward(n, first, places_ref, start_ref, cos_ref, sin_ref, log_ref, *rest):
     chunks, outs, grads, results = (rest[k * n : (k + 1) * n] for k in range(4))
     qkv, mixed_all, grad_all, result = rest[4 * n :]
     seq_len = start_ref.shape[1]
     count = seq_len // n
     heads = qkv.shape[1]
+    mine = slice(first, first + heads)
     for c in range(n):
         at = lanes(places_ref[c], count)
-        qkv[:, :, :, at] = chunks[c][...]
-        mixed_all[:, :, at] = outs[c][...]
-        grad_all[:, :, at] = grads[c][...]
+        qkv[:, :, :, at] = chunks[c][:, mine]
+        mixed_all[:, :, at] = outs[c][mine]
+        grad_all[:, :, at] = grads[c][mine]
     cosine, sine = cos_ref[...], -sin_ref[...]
     blocks = seq_len // BLOCK
 
@@ -351,7 +352,11 @@
         grad_keys, grad_values = [0.0] * blocks, [0.0] * blocks
         for i in range(blocks):
             at = slice(i * BLOCK, (i + 1) * BLOCK)
-            start, log_total, inner_here = start_ref[:, at], log_ref[head, :, at], inner[:, at]
+            start, log_total, inner_here = (
+                start_ref[:, at],
+                log_ref[first + head, :, at],
+                inner[:, at],
+            )
             query, grad_here = queries[:, at], grad[:, at]
             grad_query = 0.0
             for j in key_blocks(i):
@@ -398,13 +403,15 @@
     return outs, log_total
 
 
-def backward_attention(places, start, cosine, sine, log_total, chunks, outs, grads):
+def backward_attention(part, places, start, cosine, sine, log_total, chunks, outs, grads):
     n = len(chunks)
     _, heads, _, count = chunks[0].shape
+    heads = heads // 2
+    first = part * heads
     seq_len = n * count
     pairs = heads * seq_len * seq_len // 2
     return call(
-        lambda *refs: attend_backward(n, *refs),
+        lambda *refs: attend_backward(n, first, *refs),
         [places, start, cosine, sine, log_total, *chunks, *outs, *grads],
         [((3, heads, HEAD_DIM, count), BF)] * n,
         [
@@ -498,40 +505,36 @@
     return sum(((slot >> b) & 1) << (bits - 1 - b) for b in range(bits))
 
 
-def part_sizes(members):
-    sizes = []
-    while members > 1:
+def part_slots(members):
+    halves = []
+    while members > 4:
         members //= 2
-        sizes.append(members)
-    return sizes + [1]
-
-
-def spread(me, members, fields, parts):
+        halves.append((members, members))
+    return halves + [(slot, 1) for slot in range(members - 1, -1, -1)]
+
+
+def move_slices(me, members, fields, parts, inward):
     bits = members.bit_length() - 1
-    for size, part in zip(part_sizes(members), parts):
+    for (first, size), part in zip(part_slots(members), parts):
         for k in range(size):
-            slot = k + (size if part is not parts[-1] else 0)
-            owner = me ^ slot_code(slot, bits)
+            owner = me ^ slot_code(first + k, bits)
             low = 0
             for field in fields:
                 rows = field.shape[0] // members
                 at = pl.ds(pl.multiple_of(owner * rows, rows), rows)
-                part[k, low : low + rows] = field[at]
+                if inward:
+                    part[k, low : low + rows] = field[at]
+                else:
+                    field[at] = part[k, low : low + rows]
                 low += rows
 
 
+def spread(me, members, fields, parts):
+    move_slices(me, members, fields, parts, True)
+
+
 def gather_spread(me, members, fields, parts):
-    bits = members.bit_length() - 1
-    for size, part in zip(part_sizes(members), parts):
-        for k in range(size):
-            slot = k + (size if part is not parts[-1] else 0)
-            owner = me ^ slot_code(slot, bits)
-            low = 0
-            for field in fields:
-                rows = field.shape[0] // members
-                at = pl.ds(pl.multiple_of(owner * rows, rows), rows)
-                field[at] = part[k, low : low + rows]
-                low += rows
+    move_slices(me, members, fields, parts, False)
 
 
 def early_kernel(chunks, packs, me_ref, up_second_ref, gain_ref, *rest):
@@ -539,7 +542,8 @@
     more = rest[fields * chunks :]
     before, more = (more[:3], more[3:]) if packs != 1 else (None, more)
     if packs > 1:
-        parts, more = more[: packs - 1], more[packs - 1 :]
+        count = len(part_slots(packs))
+        parts, more = more[:count], more[count:]
         out_ref, shared_ref, split_ref = more
     else:
         shared_ref, split_ref, out_ref = more
@@ -571,12 +575,11 @@
     split_ref[rank:] = down_a.astype(split_ref.dtype)
     out_ref[...] = out_a.astype(out_ref.dtype)
     if packs > 1:
-        members = 1 << (packs - 2)
-        spread(me_ref[0], members, (shared_ref, split_ref), parts)
+        spread(me_ref[0], packs, (shared_ref, split_ref), parts)
 
 
 def part_shapes(members, rows, width):
-    return [((size, rows, width), BF) for size in part_sizes(members)]
+    return [((size, rows, width), BF) for _, size in part_slots(members)]
 
 
 def early_sums(me, items, up_second, gain, before=None, members=0):
@@ -590,7 +593,7 @@
     elif not members:
         packs, outputs = 0, sums
     else:
-        packs = members.bit_length() + 1
+        packs = members
         outputs = part_shapes(members, 5 * rank // members, width) + [((rank, cols), BF)]
         scratch = [pltpu.VMEM((3 * rank, width), BF), pltpu.VMEM((2 * rank, hidden), BF)]
     return call(
@@ -603,9 +606,17 @@
     )
 
 
-def in_kernel(grad_pre_ref, grad_up_ref, in_full_ref, up_full_ref, *rest):
+def all_heads(first, second):
+    return jnp.concatenate(
+        [half.reshape(-1, half.shape[-1]) for half in (first, second)], axis=0
+    )
+
+
+def in_kernel(first_ref, second_ref, grad_up_ref, in_full_ref, up_full_ref, *rest):
     piece_ref = rest[-1]
-    grad_pre = grad_pre_ref[...].reshape(in_full_ref.shape[1], grad_up_ref.shape[0])
+    grad_pre = jnp.concatenate(
+        [all_heads(first_ref[i], second_ref[i]) for i in range(3)], axis=0
+    )
     total = mm(grad_pre, in_full_ref[...], 0, 1) + mm(grad_up_ref[...], up_full_ref[...], 1, 1)
     if len(rest) > 1:
         total = total + rest[0][...].astype(F32)
@@ -615,7 +626,7 @@
 def in_piece(grad_pre, grad_up, in_full, up_full, dtype, arrived=None):
     count, hidden = grad_up.shape
     width = up_full.shape[0]
-    operands = [grad_pre, grad_up, in_full, up_full]
+    operands = [*grad_pre, grad_up, in_full, up_full]
     (piece,) = call(
         in_kernel,
         operands + ([] if arrived is None else [arrived]),
@@ -626,7 +637,7 @@
 
 
 def late_kernel(chunks, packs, me_ref, second_ref, gain_ref, *rest):
-    fields = 3
+    fields = 4
     more = rest[fields * chunks :]
     rank, cols = second_ref.shape[1], second_ref.shape[2]
     out_ref, more = more[0], more[1:]
@@ -635,8 +646,8 @@
     def one_third(i, carry):
         shared, split = 0.0, 0.0
         for c in range(chunks):
-            grad_pre, low, hat = rest[c * fields : (c + 1) * fields]
-            part = grad_pre[i].reshape(cols, -1)
+            grad_first, grad_second, low, hat = rest[c * fields : (c + 1) * fields]
+            part = all_heads(grad_first[i], grad_second[i])
             low_grad = (ADAPTER_SCALE * mm(part, second_ref[i], 0, 1)).astype(BF)
             shared = shared + mm(low_grad, hat[...], 0, 0)
             split = split + mm(low[:, lanes(i, rank)], part, 0, 1)
@@ -649,28 +660,29 @@
     lax.fori_loop(0, 3, one_third, 0, unroll=True)
     split_ref[:, 3 * cols :] = out_ref[...].astype(BF)
     if packs:
-        spread(me_ref[0], 1 << (packs - 1), (shared_ref, split_ref), more[:packs])
+        spread(me_ref[0], packs, (shared_ref, split_ref), more[: len(part_slots(packs))])
 
 
 def late_sums(me, items, second, gain, out_a, members=0):
-    width, rank, cols = items[0][2].shape[1], second.shape[1], second.shape[2]
+    width, rank, cols = items[0][3].shape[1], second.shape[1], second.shape[2]
     sums = [((3 * rank, width), BF), ((rank, 4 * cols), BF)]
-    packs = members.bit_length() if members else 0
+    packs = members
     return call(
         lambda *refs: late_kernel(len(items), packs, *refs),
         [me, second, gain] + [array for item in items for array in item] + [out_a],
         part_shapes(members, 4 * rank // members, width) if packs else sums,
         [pltpu.VMEM(*spec) for spec in sums] if packs else [],
-        flops=2 * len(items) * items[0][1].shape[0] * rank * 3 * (width + 2 * cols),
+        flops=2 * len(items) * items[0][2].shape[0] * rank * 3 * (width + 2 * cols),
         scalars=1,
     )
 
 
 def early_unpack_kernel(packs, me_ref, *rest):
-    parts = rest[:packs]
-    up_a_ref, out_b_ref, down_b_ref, up_b_ref, down_a_ref, shared_ref, split_ref = rest[packs:]
+    count = len(part_slots(packs))
+    parts = rest[:count]
+    up_a_ref, out_b_ref, down_b_ref, up_b_ref, down_a_ref, shared_ref, split_ref = rest[count:]
     rank = out_b_ref.shape[0]
-    gather_spread(me_ref[0], 1 << (packs - 1), (shared_ref, split_ref), parts)
+    gather_spread(me_ref[0], packs, (shared_ref, split_ref), parts)
     up_a_ref[...] = shared_ref[:rank].astype(F32).T
     out_b_ref[...] = shared_ref[rank : 2 * rank].astype(F32)
     down_b_ref[...] = shared_ref[2 * rank :].astype(F32)
@@ -679,10 +691,11 @@
 
 
 def late_unpack_kernel(packs, me_ref, *rest):
-    parts = rest[:packs]
-    a_ref, b_ref, out_a_ref, shared_ref, split_ref = rest[packs:]
+    count = len(part_slots(packs))
+    parts = rest[:count]
+    a_ref, b_ref, out_a_ref, shared_ref, split_ref = rest[count:]
     rank, cols = b_ref.shape[1], b_ref.shape[2]
-    gather_spread(me_ref[0], 1 << (packs - 1), (shared_ref, split_ref), parts)
+    gather_spread(me_ref[0], packs, (shared_ref, split_ref), parts)
     for i in range(3):
         a_ref[i] = shared_ref[i * rank : (i + 1) * rank].astype(F32).T
         b_ref[i] = split_ref[:, i * cols : (i + 1) * cols].astype(F32)
@@ -714,14 +727,22 @@
     return call(add_kernel, [left, right], [(left.shape, BF)])[0]
 
 
-def fold_kernel(arrived_ref, *rest):
+def fold_kernel(firsts, arrived_ref, *rest):
     parts, results = rest[: len(rest) // 2], rest[len(rest) // 2 :]
-    for part, result in zip(parts, results):
-        size = part.shape[0]
-        low = size if part is not parts[-1] else 0
+    for first, part, result in zip(firsts, parts, results):
         result[...] = (
-            part[...].astype(F32) + arrived_ref[low : low + size].astype(F32)
+            part[...].astype(F32) + arrived_ref[first : first + part.shape[0]].astype(F32)
         ).astype(BF)
+
+
+def meet_kernel(count, *refs):
+    total = refs[0][...].astype(F32)
+    for ref in refs[1:count]:
+        total = total + ref[...].astype(F32)
+    shared_ref, split_ref = refs[count:]
+    rows = shared_ref.shape[1]
+    shared_ref[...] = total[:, :rows].astype(BF)
+    split_ref[...] = total[:, rows:].astype(BF)
 
 
 def close_kernel(shared_ref, arrived_ref, split_ref, both_ref):
@@ -732,10 +753,11 @@
     both_ref[:, rows:] = split_ref[...]
 
 
-def join_kernel(first_ref, second_ref, both_ref):
-    size = first_ref.shape[0]
-    both_ref[:size] = first_ref[...]
-    both_ref[size:] = second_ref[...]
+def join_kernel(*refs):
+    low = 0
+    for ref in refs[:-1]:
+        refs[-1][low : low + ref.shape[0]] = ref[...]
+        low += ref.shape[0]
 
 
 def swap_pairs(n):
@@ -766,54 +788,78 @@
     def __init__(self, parts, n_shared):
         self.parts, self.n_shared = list(parts), n_shared
         self.members, self.n = lax.axis_size("dp"), lax.axis_size("tensor")
-        self.bits = len(self.parts) - 1
-        self.steps = [("down", b) for b in range(self.bits)]
+        self.bits = self.members.bit_length() - 1
+        self.slots = part_slots(self.members)
+        halves = self.bits - 2
+        self.steps = [("down", b) for b in range(halves)] + [("meet", 0)]
         jump = 1
         while jump < self.n:
             self.steps.append(("across", jump))
             jump *= 2
-        self.steps += [("back", b) for b in reversed(range(self.bits))]
+        self.steps += [("part", 0)] + [("back", b) for b in reversed(range(halves))]
         self.moving, self.at, self.results = None, 0, []
+
+    def hop(self, value, code):
+        pairs = [(k, k ^ code) for k in range(self.members)]
+        return lax.ppermute(value, "dp", pairs)
 
     def start(self):
         kind, which = self.steps[self.at]
+        codes = [slot_code(slot, self.bits) for slot in (1, 2, 3)]
         if kind == "across":
             pairs = [(k, k ^ which) for k in range(self.n)]
             self.moving = lax.ppermute(self.shared, "tensor", pairs)
+        elif kind == "down":
+            self.moving = self.hop(self.parts[which], 1 << which)
+        elif kind == "meet":
+            self.moving = [
+                self.hop(self.parts[-1 - slot], code) for slot, code in zip((1, 2, 3), codes)
+            ]
+        elif kind == "part":
+            self.moving = [self.hop(self.have, code) for code in codes]
         else:
-            pairs = [(k, k ^ (1 << which)) for k in range(self.members)]
-            sent = self.parts[which] if kind == "down" else self.have
-            self.moving = lax.ppermute(sent, "dp", pairs)
+            self.moving = self.hop(self.have, 1 << which)
 
     def finish(self, *earlier):
         kind, which = self.steps[self.at]
         arrived = after(self.moving, *earlier) if earlier else self.moving
         if kind == "down":
             later = self.parts[which + 1 :]
+            firsts = [first for first, _ in self.slots[which + 1 :]]
             self.parts[which + 1 :] = call(
-                fold_kernel, [arrived, *later], [(part.shape, BF) for part in later]
+                lambda *refs: fold_kernel(firsts, *refs),
+                [arrived, *later],
+                [(part.shape, BF) for part in later],
             )
-            if which == self.bits - 1:
-                own = self.parts[-1]
-                self.shared, self.split = own[:, : self.n_shared], own[:, self.n_shared :]
             value = self.parts[-1]
+        elif kind == "meet":
+            _, rows, width = self.parts[-1].shape
+            self.shared, self.split = call(
+                lambda *refs: meet_kernel(4, *refs),
+                [self.parts[-1], *arrived],
+                [((1, self.n_shared, width), BF), ((1, rows - self.n_shared, width), BF)],
+            )
+            value = self.shared
         elif kind == "across":
-            if self.steps[self.at + 1][0] == "back":
+            if self.steps[self.at + 1][0] == "part":
                 (self.have,) = call(
                     close_kernel,
                     [self.shared, arrived, self.split],
                     [(self.parts[-1].shape, BF)],
                 )
-                self.results, value = [self.have], self.have
+                value = self.have
             else:
                 self.shared = value = added(self.shared, arrived)
         else:
-            self.results.append(arrived)
-            value = arrived
-            if which:
-                rows = self.have.shape
+            pieces = list(arrived) if kind == "part" else [arrived]
+            self.results = self.results or [self.have]
+            self.results += pieces
+            value = pieces[0]
+            if self.at + 1 < len(self.steps):
+                _, *rows = self.have.shape
+                total = sum(piece.shape[0] for piece in [self.have, *pieces])
                 (self.have,) = call(
-                    join_kernel, [self.have, arrived], [((2 * rows[0], *rows[1:]), BF)]
+                    join_kernel, [self.have, *pieces], [((total, *rows), BF)]
                 )
                 value = self.have
         self.at += 1
@@ -838,11 +884,7 @@
     )
     order = jnp.asarray([slot_code(slot, bits) for slot in range(members)], jnp.int32) ^ me
     both = both[order]
-    parts, top = [], members
-    for size in part_sizes(members)[:-1]:
-        parts.append(both[size:top])
-        top = size
-    return parts + [both[:1]]
+    return [both[first : first + size] for first, size in part_slots(members)]
 
 
 def slow_whole(me, parts, n_shared, members):
@@ -895,7 +937,6 @@
         return lax.ppermute(value, "tensor", pairs)
 
     members = lax.axis_size("dp")
-    bits = members.bit_length() - 1
     tidy = short and hidden == width and 4 * cols == width and rank % (16 * members) == 0
     if short:
         owners = [me, me ^ 1, n - 1 - me, (n - 1 - me) ^ 1]
@@ -962,9 +1003,10 @@
     mixed, log_total = forward_attention(places, start, qkv)
     low_out = [None] * n
 
-    def out_part(k, dtype, arrived=None, both=False):
+    def out_part(k, dtype, last=None, arrived=None, both=False):
+        rows = mixed[k] if last is None else after(mixed[k], last)
         piece, low_out[k], *more = out_piece(
-            mixed[k],
+            rows,
             act[k],
             out_full,
             down_full,
@@ -993,15 +1035,17 @@
         y_facing, y_facing_low = out_part(2, F32, both=True)
         y_far, y_far_low = out_part(3, F32, both=True)
         y_1, y_2 = send(y_facing_low, outward), send(y_far_low, outward)
-        g_near, g_mid = after((g_near, g_mid), y_facing, y_far)
+        g_near, g_mid = after((g_near, g_mid), mixed)
         g_mid_far, g_end_far = send(g_near, middle), send(g_mid, inward)
-        y_near, y_own = out_part(1, F32), out_part(0, F32)
-        backs = [pulled(0, own_g), pulled(1, g_near)]
-        g_mid_far, g_end_far = after((g_mid_far, g_end_far), backs, y_near, y_own)
+        backs = [pulled(0, own_g)]
+        g_mid_far, g_end_far = after((g_mid_far, g_end_far), y_far, backs)
         g_end = send(g_mid_far, inward)
         g_far = added(g_mid_far, g_end_far)
-        y_3 = send(added(y_far, after(y_1, g_far)), middle)
-        backs = backs + [None, pulled(3, g_far)]
+        backs.append(pulled(1, after(g_near, g_far)))
+        y_near, y_own = out_part(1, F32, g_far), out_part(0, F32, g_far)
+        pulled_far = pulled(3, g_far)
+        y_3 = send(added(y_far, after(y_1, backs, y_near, y_own, pulled_far)), middle)
+        backs = backs + [None, pulled_far]
         all_g = [own_g, g_near, None, g_far]
         before = early_sums(
             me_dp,
@@ -1021,10 +1065,10 @@
             before,
             members if tidy else 0,
         )
-        y_near = added(y_near, after(y_3, early))
-        y_4 = send(y_near, swap)
     else:
-        y_own = ring_scatter(lambda k, arrived: out_part(k, BF if k else F32, arrived), n)
+        y_own = ring_scatter(
+            lambda k, arrived: out_part(k, BF if k else F32, arrived=arrived), n
+        )
         backs, moving, all_g = [pulled(0, own_g)], own_g, [own_g]
         for k in range(1, n):
             moving = send(moving, up_ring)
@@ -1043,8 +1087,19 @@
     if short:
         last = early.finish()
         early.start()
-        grads_mixed = after(grads_mixed, y_near, last)
-    grad_pre = backward_attention(places, start, cosine, sine, log_total, qkv, mixed, grads_mixed)
+        grads_mixed = after(grads_mixed, last)
+    halves = []
+    for part in range(2):
+        halves.append(
+            backward_attention(
+                part, places, start, cosine, sine, log_total, qkv, mixed, grads_mixed
+            )
+        )
+        if short and not part:
+            y_near = added(y_near, after(y_3, halves[0]))
+            y_4 = send(y_near, swap)
+            grads_mixed = after(grads_mixed, y_near)
+    grad_pre = list(zip(*halves))
 
     def in_part(k, dtype, arrived=None, last=None):
         pre = grad_pre[k] if last is None else after(grad_pre[k], last)
@@ -1062,7 +1117,7 @@
                 early_b[rank:].T,
             )
         return call(
-            lambda *refs: early_unpack_kernel(bits + 1, *refs),
+            lambda *refs: early_unpack_kernel(members, *refs),
             [me_dp, *parts],
             [
                 ((width, rank), F32),
@@ -1078,7 +1133,7 @@
     def late_parts():
         late = late_sums(
             me_dp,
-            [(grad_pre[k], low[k], hat[k]) for k in range(n)],
+            [(*grad_pre[k], low[k], hat[k]) for k in range(n)],
             adapter_query_key_value_second,
             gain_a,
             out_a,
@@ -1094,22 +1149,19 @@
         late = late_parts()
         late.start()
         dx_far = in_part(3, BF)
-        last = late.finish(dx_far)
-        late.start()
-        last = early.finish(last)
+        last = early.finish(dx_far)
         early.start()
         dx_swap = send(dx_far, swap)
-        dx_near, dx_own = in_part(1, BF, last=last), in_part(0, F32, last=last)
-        last = early.finish(dx_near, dx_own)
+        last = late.finish(last)
+        late.start()
+        dx_near = in_part(1, BF, last=last)
+        last = early.finish(dx_near)
         early.start()
         last = late.finish(last)
         late.start()
-        dx_facing = in_part(2, BF, after(dx_swap, last))
+        dx_own = in_part(0, F32, last=last)
+        dx_facing = in_part(2, BF, after(dx_swap, dx_own))
         last = late.finish(dx_facing)
-        late.start()
-        last = early.finish(last)
-        early.start()
-        last = late.finish(last)
         late.start()
         dx_a = send(dx_near, swap)
         dx_b = send(dx_facing, mirror)
@@ -1122,15 +1174,11 @@
         )
         last = late.finish(last, layer_output)
         late.start()
-        last = early.finish(last)
-        early.start()
-        last = late.finish(last)
-        late.start()
         early.finish(last)
         early_done = early_whole(early.rest())
         last = late.finish(early_done)
         late.start()
-        dx_parts = [dx_own, *after((dx_a, dx_b), last)]
+        dx_parts = [dx_own, dx_a, dx_b]
     else:
         (layer_output,) = call(output_kernel, [own_x, y_own], [((shard_len, width), BF)])
         dx_parts = [
@@ -1139,15 +1187,11 @@
         early.finish()
         late = late_parts()
         early_done = early_whole(early.rest())
-    (grad_in,) = call(
-        input_grad_kernel, [own_x, own_g, *dx_parts], [((shard_len, width), F32)]
-    )
-
     up_a, out_b, down_b, up_b, down_a = early_done
     late = late.rest()
     if tidy:
         a_qkv, b_qkv, out_a = call(
-            lambda *refs: late_unpack_kernel(bits + 1, *refs),
+            lambda *refs: late_unpack_kernel(members, *refs),
             [me_dp, *late],
             [((3, width, rank), F32), ((3, rank, cols), F32), ((cols, rank), F32)],
             [pltpu.VMEM((3 * rank, width), BF), pltpu.VMEM((rank, width), BF)],
@@ -1159,6 +1203,10 @@
         a_qkv = jnp.swapaxes(late_a.reshape(3, rank, width), 1, 2)
         b_qkv = jnp.stack([late_b[:, i * cols : (i + 1) * cols] for i in range(3)])
         out_a = late_b[:, 3 * cols :].T
+    dx_parts = [dx_parts[0], *after(dx_parts[1:], a_qkv)]
+    (grad_in,) = call(
+        input_grad_kernel, [own_x, own_g, *dx_parts], [((shard_len, width), F32)]
+    )
     return (
         layer_output[None],
         grad_in[None],

time: 212 us -> 210 us (level)
  waiting for transfers between devices: 69.6 us -> 67.4 us
    ppermute x16, waiting for transfers between devices: 31.1 us -> 43.1 us  [send(): return lax.ppermute(value, 'tensor', pairs)]
    ppermute x4, waiting for transfers between devices: 25.3 us -> 13.6 us  [start(): self.moving = lax.ppermute(self.shared, 'tensor', pairs)]
    ppermute x12 -> x16, starting transfers between devices: 8.13 us -> 16.7 us  [hop(): return lax.ppermute(value, 'dp', pairs)]
    ppermute x16, starting transfers between devices: 39.4 us -> 34 us  [send(): return lax.ppermute(value, 'tensor', pairs)]
    ppermute x4, starting transfers between devices: 9.65 us -> 6.6 us  [start(): self.moving = lax.ppermute(self.shared, 'tensor', pairs)]
    ppermute x12 -> x16, waiting for transfers between devices: 13.2 us -> 10.7 us  [hop(): return lax.ppermute(value, 'dp', pairs)]
    pallas_call x45 -> x42, Pallas kernels: 64.7 us -> 65.2 us  [call(): pl.pallas_call(kernel, in_specs=[pl.BlockSpec(memory_space=space) for spa...]
  transfers between devices with their start and end apart: 32 -> 36, of which waited for: 14 -> 14; matrix products, arithmetic and copies ran while one was open for 0% -> 0% of each run, Pallas kernels for 24% -> 27%
where the time goes in v1:
time: 210 us; the launch traced here: 209 us
  Pallas kernels  68 us (32%)
  waiting for transfers between devices  67.4 us (32%)
  starting transfers between devices  57.2 us (27%)
  local copies, waits for them, and re-layouts  15.4 us (7%)
    pallas_call x42, Pallas kernels, call(): pl.pallas_call(kernel, in_specs=[pl.BlockSpec(memory_space=space) for spa...  65.2 us
    ppermute x16, waiting for transfers between devices, send(): return lax.ppermute(value, 'tensor', pairs)  43.1 us
    ppermute x16, starting transfers between devices, send(): return lax.ppermute(value, 'tensor', pairs)  34 us
    ppermute x16, starting transfers between devices, hop(): return lax.ppermute(value, 'dp', pairs)  16.7 us
    unnamed x52, local copies, waits for them, and re-layouts  15.4 us
    ppermute x4, waiting for transfers between devices, start(): self.moving = lax.ppermute(self.shared, 'tensor', pairs)  13.6 us
    ppermute x16, waiting for transfers between devices, hop(): return lax.ppermute(value, 'dp', pairs)  10.7 us
    ppermute x4, starting transfers between devices, start(): self.moving = lax.ppermute(self.shared, 'tensor', pairs)  6.6 us
  transfers between devices with their start and end apart: 36, of which 14 were waited for; matrix products, arithmetic and copies ran while one was open for 0% of the time, Pallas kernels for 27%

profile of v1, /device:TPU:0, one launch (start us, length us, event | category | flops | bytes accessed | tf_op | source)
XLA Modules:
  0.0 209.3 jit_solution(5492280762703517260)
XLA Ops:
  0.7 3.1 %collective-permute-start = (bf16[256,1024]{1,0:T(8,128)(2,1)}, bf16[256,1024]{1,0:T(8,128)(2,1)S(1)}, u32[]{:S(2)}, u32[]{:S(2)}) collective-permute-start(bf16[256,1024]{1,0:T(8,128)(2,1)} %bitcast.11), channel_id=1, source_target_pairs={{0,1},{1,0},{2,3},{3,2},{4,5},{5,4},{6,7},{7,6},{8,9},{9,8},{10,11... | collective-permute-start | bytes 1572872 | tf_op jit(solution)/shard_map/ppermute | solution.py:937
  3.8 2.5 %collective-permute-start.1 = (bf16[256,1024]{1,0:T(8,128)(2,1)}, bf16[256,1024]{1,0:T(8,128)(2,1)S(1)}, u32[]{:S(2)}, u32[]{:S(2)}) collective-permute-start(bf16[256,1024]{1,0:T(8,128)(2,1)} %bitcast.12), channel_id=1, source_target_pairs={{0,3},{1,2},{2,1},{3,0},{4,7},{5,6},{6,5},{7,4},{8,11},{9,10},{10,... | collective-permute-start | bytes 1572872 | tf_op jit(solution)/shard_map/ppermute | solution.py:937
  22.3 2.8 %shard_map.242 = (bf16[1024,768]{1,0:T(8,128)(2,1)S(1)}, bf16[1024,1024]{1,0:T(8,128)(2,1)S(1)}, bf16[256,1024]{1,0:T(8,128)(2,1)S(1)}, bf16[1024,1024]{1,0:T(8,128)(2,1)S(1)}) custom-call(bf16[3,1024,256]{2,1,0:T(8,128)(2,1)S(1)} %copy-done.2, bf16[3,1024,128]{2,1,0:T(8,128)(2,1)S(1)} %copy-done.4, bf16[3,128,256]{2,1,0:T(8,128)(2,1)S(1)} %copy-done.7, ...), custom_call_target="tpu_custom_call" | custom-call | flops 805306368 | bytes 12582912 | tf_op jit(solution)/shard_map/pallas_call | solution.py:140
  25.2 4.3 %shard_map.241 = (bf16[3,4,64,256]{3,2,1,0:T(8,128)(2,1)S(1)}, bf16[256,512]{1,0:T(8,128)(2,1)S(1)}, bf16[256,1024]{1,0:T(8,128)(2,1)S(1)}, bf16[256,1024]{1,0:T(8,128)(2,1)S(1)}, bf16[256,1024]{1,0:T(8,128)(2,1)S(1)}) custom-call(bf16[256,1024]{1,0:T(8,128)(2,1)S(1)} %bitcast.13, f32[1,1024]{1,0:T(1,128)S(1)} %bitcast.29, f32[1,1024]{1,0:T(1,128)S(1)} %bitcast.22, ...), custom_call_target="tpu_custom_call" | custom-call | flops 1207959552 | bytes 4456448 | tf_op jit(solution)/shard_map/pallas_call | solution.py:33
  32.3 4.3 %shard_map.244 = (bf16[3,4,64,256]{3,2,1,0:T(8,128)(2,1)S(1)}, bf16[256,512]{1,0:T(8,128)(2,1)S(1)}, bf16[256,1024]{1,0:T(8,128)(2,1)S(1)}, bf16[256,1024]{1,0:T(8,128)(2,1)S(1)}, bf16[256,1024]{1,0:T(8,128)(2,1)S(1)}) custom-call(bf16[256,1024]{1,0:T(8,128)(2,1)S(1)} %collective-permute-done.1.x_ref, f32[1,1024]{1,0:T(1,128)S(1)} %bitcast.30, ...), custom_call_target="tpu_custom_call" | custom-call | flops 1207959552 | bytes 4456448 | tf_op jit(solution)/shard_map/pallas_call | solution.py:33
  36.6 4.3 %shard_map.243 = (bf16[3,4,64,256]{3,2,1,0:T(8,128)(2,1)S(1)}, bf16[256,512]{1,0:T(8,128)(2,1)S(1)}, bf16[256,1024]{1,0:T(8,128)(2,1)S(1)}, bf16[256,1024]{1,0:T(8,128)(2,1)S(1)}, bf16[256,1024]{1,0:T(8,128)(2,1)S(1)}) custom-call(bf16[256,1024]{1,0:T(8,128)(2,1)S(1)} %collective-permute-done.x_ref, f32[1,1024]{1,0:T(1,128)S(1)} %bitcast.31, ...), custom_call_target="tpu_custom_call" | custom-call | flops 1207959552 | bytes 4456448 | tf_op jit(solution)/shard_map/pallas_call | solution.py:33
  40.8 3.5 %collective-permute-done.2.x_ref = bf16[256,1024]{1,0:T(8,128)(2,1)S(1)} collective-permute-done((bf16[256,1024]{1,0:T(8,128)(2,1)S(1)}, bf16[256,1024]{1,0:T(8,128)(2,1)S(1)}, u32[]{:S(2)}, u32[]{:S(2)}) %collective-permute-start.2) | collective-permute-done | bytes 524320 | tf_op jit(solution)/shard_map/ppermute | solution.py:937
  44.4 4.3 %shard_map.245 = (bf16[3,4,64,256]{3,2,1,0:T(8,128)(2,1)S(1)}, bf16[256,512]{1,0:T(8,128)(2,1)S(1)}, bf16[256,1024]{1,0:T(8,128)(2,1)S(1)}, bf16[256,1024]{1,0:T(8,128)(2,1)S(1)}, bf16[256,1024]{1,0:T(8,128)(2,1)S(1)}) custom-call(bf16[256,1024]{1,0:T(8,128)(2,1)S(1)} %collective-permute-done.2.x_ref, f32[1,1024]{1,0:T(1,128)S(1)} %bitcast.32, ...), custom_call_target="tpu_custom_call" | custom-call | flops 1207959552 | bytes 4456448 | tf_op jit(solution)/shard_map/pallas_call | solution.py:33
  48.6 7.2 %shard_map.246 = (bf16[4,64,256]{2,1,0:T(8,128)(2,1)S(1)}, bf16[4,64,256]{2,1,0:T(8,128)(2,1)S(1)}, bf16[4,64,256]{2,1,0:T(8,128)(2,1)S(1)}, bf16[4,64,256]{2,1,0:T(8,128)(2,1)S(1)}, f32[4,1,1024]{2,1,0:T(1,128)S(1)}) custom-call(s32[4]{0:T(128)S(1)} %pad_add_fusion.places_ref.refs_0_, s32[1,1024]{1,0:T(1,128)S(1)} %get-tuple-element.193.refs_1_, ...), custom_call_target="tpu_custom_call" | custom-call | flops 2147483648 | bytes 1081344 | tf_op jit(solution)/shard_map/pallas_call | solution.py:33
  60.7 9.2 %collective-permute-done.6.right_ref = bf16[256,1024]{1,0:T(8,128)(2,1)S(1)} collective-permute-done((bf16[256,1024]{1,0:T(8,128)(2,1)S(1)}, bf16[256,1024]{1,0:T(8,128)(2,1)S(1)}, u32[]{:S(2)}, u32[]{:S(2)}) %collective-permute-start.6) | collective-permute-done | bytes 524320 | tf_op jit(solution)/shard_map/ppermute | solution.py:937
  72.9 4.6 %collective-permute-start.7 = (bf16[256,1024]{1,0:T(8,128)(2,1)S(1)}, bf16[256,1024]{1,0:T(8,128)(2,1)S(1)}, u32[]{:S(2)}, u32[]{:S(2)}) collective-permute-start(bf16[256,1024]{1,0:T(8,128)(2,1)S(1)} %get-tuple-element.257), channel_id=1, source_target_pairs={{0,1},{3,2},{4,5},{7,6},{8,9},{11,10},{12,13},{15,14},{16,17},{19,... | collective-permute-start | bytes 1572872 | tf_op jit(solution)/shard_map/ppermute | solution.py:937
  82.0 2.2 %shard_map.256 = (f32[384,1024]{1,0:T(8,128)S(1)}, f32[256,1024]{1,0:T(8,128)S(1)}, f32[128,256]{1,0:T(8,128)S(1)}) custom-call(s32[1]{0:T(128)} %bitcast.4.refs_0_, bf16[128,1024]{1,0:T(8,128)(2,1)S(1)} %copy-done.6, f32[1,1024]{1,0:T(1,128)S(1)} %bitcast.26, bf16[256,1024]{1,0:T(8,128)(2,1)S(1)} %bitcast.19, ...), custom_call_target="tpu_custom_call" | custom-call | flops 1207959552 | bytes 5505024 | tf_op jit(solution)/shard_map/pallas_call | solution.py:33
  89.0 5.9 %shard_map.261 = (bf16[3,2,64,256]{3,2,1,0:T(8,128)(2,1)S(1)}, bf16[3,2,64,256]{3,2,1,0:T(8,128)(2,1)S(1)}, bf16[3,2,64,256]{3,2,1,0:T(8,128)(2,1)S(1)}, bf16[3,2,64,256]{3,2,1,0:T(8,128)(2,1)S(1)}) custom-call(s32[4]{0:T(128)S(1)} %pad_add_fusion.places_ref.refs_0_, s32[1,1024]{1,0:T(1,128)S(1)} %get-tuple-element.193.refs_1_, ...), custom_call_target="tpu_custom_call" | custom-call | flops 2684354560 | bytes 1572864 | tf_op jit(solution)/shard_map/pallas_call | solution.py:33
  95.0 5.9 %shard_map.264 = (bf16[3,2,64,256]{3,2,1,0:T(8,128)(2,1)S(1)}, bf16[3,2,64,256]{3,2,1,0:T(8,128)(2,1)S(1)}, bf16[3,2,64,256]{3,2,1,0:T(8,128)(2,1)S(1)}, bf16[3,2,64,256]{3,2,1,0:T(8,128)(2,1)S(1)}) custom-call(s32[4]{0:T(128)S(1)} %pad_add_fusion.places_ref.refs_0_, s32[1,1024]{1,0:T(1,128)S(1)} %get-tuple-element.193.refs_1_, ...), custom_call_target="tpu_custom_call" | custom-call | flops 2684354560 | bytes 1572864 | tf_op jit(solution)/shard_map/pallas_call | solution.py:33
  100.9 3.5 %shard_map.268 = (bf16[4,64,1024]{2,1,0:T(8,128)(2,1)S(1)}, bf16[1,64,1024]{2,1,0:T(8,128)(2,1)S(1)}, bf16[1,64,1024]{2,1,0:T(8,128)(2,1)S(1)}, bf16[1,64,1024]{2,1,0:T(8,128)(2,1)S(1)}, bf16[1,64,1024]{2,1,0:T(8,128)(2,1)S(1)}) custom-call(s32[1]{0:T(128)} %bitcast.4.refs_0_, bf16[3,128,256]{2,1,0:T(8,128)(2,1)S(1)} %copy-done.8, f32[1,1024]{1,0:T(1,128)S(1)} %bitcast.33, ...), custom_call_target="tpu_custom_call" | custom-call | flops 1207959552 | bytes 2097152 | tf_op jit(solution)/shard_map/pallas_call | solution.py:33
  104.6 9.4 %collective-permute-start.12 = (bf16[256,1024]{1,0:T(8,128)(2,1)S(1)}, bf16[256,1024]{1,0:T(8,128)(2,1)S(1)}, u32[]{:S(2)}, u32[]{:S(2)}) collective-permute-start(bf16[256,1024]{1,0:T(8,128)(2,1)S(1)} %get-tuple-element.308), channel_id=1, source_target_pairs={{0,1},{3,2},{4,5},{7,6},{8,9},{11,10},{12,13},{15,14},{16,17},{19,... | collective-permute-start | bytes 1572872 | tf_op jit(solution)/shard_map/ppermute | solution.py:937
  118.4 2.0 collective-permute-done.14.refs_1_
  120.4 2.4 %collective-permute-start.16 = (bf16[1,80,1024]{2,1,0:T(8,128)(2,1)S(1)}, bf16[1,80,1024]{2,1,0:T(8,128)(2,1)S(1)}, u32[]{:S(2)}, u32[]{:S(2)}) collective-permute-start(bf16[1,80,1024]{2,1,0:T(8,128)(2,1)S(1)} %get-tuple-element.312), channel_id=1, source_target_pairs={{0,24},{4,28},{8,16},{12,20},{16,8},{20,12},{24,0},{28,4},{1,25},{... | collective-permute-start | bytes 491528 | tf_op jit(solution)/shard_map/ppermute | solution.py:804
  122.9 3.8 %collective-permute-done.16.refs_3_ = bf16[1,80,1024]{2,1,0:T(8,128)(2,1)S(1)} collective-permute-done((bf16[1,80,1024]{2,1,0:T(8,128)(2,1)S(1)}, bf16[1,80,1024]{2,1,0:T(8,128)(2,1)S(1)}, u32[]{:S(2)}, u32[]{:S(2)}) %collective-permute-start.16) | collective-permute-done | bytes 163872 | tf_op jit(solution)/shard_map/ppermute | solution.py:804
  128.2 10.9 %collective-permute-done.17.right_ref = bf16[1,48,1024]{2,1,0:T(8,128)(2,1)S(1)} collective-permute-done((bf16[1,48,1024]{2,1,0:T(8,128)(2,1)S(1)}, bf16[1,48,1024]{2,1,0:T(8,128)(2,1)S(1)}, u32[]{:S(2)}, u32[]{:S(2)}) %collective-permute-start.17) | collective-permute-done | bytes 98336 | tf_op jit(solution)/shard_map/ppermute | solution.py:811
  142.8 2.5 %collective-permute-start.18 = (bf16[1,48,1024]{2,1,0:T(8,128)(2,1)S(1)}, bf16[1,48,1024]{2,1,0:T(8,128)(2,1)S(1)}, u32[]{:S(2)}, u32[]{:S(2)}) collective-permute-start(bf16[1,48,1024]{2,1,0:T(8,128)(2,1)S(1)} %shard_map.267.shared_ref), channel_id=1, source_target_pairs={{0,2},{1,3},{2,0},{3,1},{4,6},{5,7},{6,4},{7,5},{8,10},{9,11},{10,... | collective-permute-start | bytes 294920 | tf_op jit(solution)/shard_map/ppermute | solution.py:811
  146.6 2.6 %collective-permute-done.18.arrived_ref = bf16[1,48,1024]{2,1,0:T(8,128)(2,1)S(1)} collective-permute-done((bf16[1,48,1024]{2,1,0:T(8,128)(2,1)S(1)}, bf16[1,48,1024]{2,1,0:T(8,128)(2,1)S(1)}, u32[]{:S(2)}, u32[]{:S(2)}) %collective-permute-start.18) | collective-permute-done | bytes 98336 | tf_op jit(solution)/shard_map/ppermute | solution.py:811
  152.8 1.8 collective-permute-start.26
  157.9 2.2 %collective-permute-start.11 = (bf16[256,1024]{1,0:T(8,128)(2,1)S(1)}, bf16[256,1024]{1,0:T(8,128)(2,1)S(1)}, u32[]{:S(2)}, u32[]{:S(2)}) collective-permute-start(bf16[256,1024]{1,0:T(8,128)(2,1)S(1)} %shard_map.262), channel_id=1, source_target_pairs={{0,1},{1,0},{2,3},{3,2},{4,5},{5,4},{6,7},{7,6},{8,9},{9,8},{10,11... | collective-permute-start | bytes 1572872 | tf_op jit(solution)/shard_map/ppermute | solution.py:937
  161.2 8.5 %collective-permute-done.11.rest_0_ = bf16[256,1024]{1,0:T(8,128)(2,1)S(1)} collective-permute-done((bf16[256,1024]{1,0:T(8,128)(2,1)S(1)}, bf16[256,1024]{1,0:T(8,128)(2,1)S(1)}, u32[]{:S(2)}, u32[]{:S(2)}) %collective-permute-start.11) | collective-permute-done | bytes 524320 | tf_op jit(solution)/shard_map/ppermute | solution.py:937
  174.5 1.7 shard_map.279
  177.5 2.4 %collective-permute-done.33.refs_3_.refs_2_ = bf16[1,64,1024]{2,1,0:T(8,128)(2,1)S(1)} collective-permute-done((bf16[1,64,1024]{2,1,0:T(8,128)(2,1)S(1)}, bf16[1,64,1024]{2,1,0:T(8,128)(2,1)S(1)}, u32[]{:S(2)}, u32[]{:S(2)}) %collective-permute-start.33) | collective-permute-done | bytes 131104 | tf_op jit(solution)/shard_map/ppermute | solution.py:804
  180.0 2.3 %collective-permute-start.28 = (bf16[256,1024]{1,0:T(8,128)(2,1)S(1)}, bf16[256,1024]{1,0:T(8,128)(2,1)S(1)}, u32[]{:S(2)}, u32[]{:S(2)}) collective-permute-start(bf16[256,1024]{1,0:T(8,128)(2,1)S(1)} %shard_map.270), channel_id=1, source_target_pairs={{0,1},{1,0},{2,3},{3,2},{4,5},{5,4},{6,7},{7,6},{8,9},{9,8},{10,11... | collective-permute-start | bytes 1572872 | tf_op jit(solution)/shard_map/ppermute | solution.py:937
  182.3 1.7 collective-permute-start.29
  185.7 9.2 %collective-permute-done.28.rest_0_ = bf16[256,1024]{1,0:T(8,128)(2,1)S(1)} collective-permute-done((bf16[256,1024]{1,0:T(8,128)(2,1)S(1)}, bf16[256,1024]{1,0:T(8,128)(2,1)S(1)}, u32[]{:S(2)}, u32[]{:S(2)}) %collective-permute-start.28) | collective-permute-done | bytes 524320 | tf_op jit(solution)/shard_map/ppermute | solution.py:937
  194.8 12.7 %collective-permute-done.29.rest_1_ = bf16[256,1024]{1,0:T(8,128)(2,1)S(1)} collective-permute-done((bf16[256,1024]{1,0:T(8,128)(2,1)S(1)}, bf16[256,1024]{1,0:T(8,128)(2,1)S(1)}, u32[]{:S(2)}, u32[]{:S(2)}) %collective-permute-start.29) | collective-permute-done | bytes 524320 | tf_op jit(solution)/shard_map/ppermute | solution.py:937
  207.5 1.8 shard_map.282
  (136 shorter events, 62.8 us)
Async XLA Ops:
  0.7 28.8 %collective-permute-start = (bf16[256,1024]{1,0:T(8,128)(2,1)}, bf16[256,1024]{1,0:T(8,128)(2,1)S(1)}, u32[]{:S(2)}, u32[]{:S(2)}) collective-permute-start(bf16[256,1024]{1,0:T(8,128)(2,1)} %bitcast.11), channel_id=1, source_target_pairs={{0,1},{1,0},{2,3},{3,2},{4,5},{5,4},{6,7},{7,6},{8,9},{9,8},{10,11... | collective-permute-start | bytes 1572872 | tf_op jit(solution)/shard_map/ppermute | solution.py:937
  3.8 25.7 %collective-permute-start.1 = (bf16[256,1024]{1,0:T(8,128)(2,1)}, bf16[256,1024]{1,0:T(8,128)(2,1)S(1)}, u32[]{:S(2)}, u32[]{:S(2)}) collective-permute-start(bf16[256,1024]{1,0:T(8,128)(2,1)} %bitcast.12), channel_id=1, source_target_pairs={{0,3},{1,2},{2,1},{3,0},{4,7},{5,6},{6,5},{7,4},{8,11},{9,10},{10,... | collective-permute-start | bytes 1572872 | tf_op jit(solution)/shard_map/ppermute | solution.py:937
  29.5 14.9 %collective-permute-start.2 = (bf16[256,1024]{1,0:T(8,128)(2,1)S(1)}, bf16[256,1024]{1,0:T(8,128)(2,1)S(1)}, u32[]{:S(2)}, u32[]{:S(2)}) collective-permute-start(bf16[256,1024]{1,0:T(8,128)(2,1)S(1)} %collective-permute-done.1.x_ref), channel_id=1, source_target_pairs={{0,1},{1,0},{2,3},{3,2},{4,5},{5,4},{6,7},{7,6},{8,9},{9,8},{10,11... | collective-permute-start | bytes 1572872 | tf_op jit(solution)/shard_map/ppermute | solution.py:937
  30.3 25.6 %collective-permute-start.3 = (bf16[256,1024]{1,0:T(8,128)(2,1)S(1)}, bf16[256,1024]{1,0:T(8,128)(2,1)S(1)}, u32[]{:S(2)}, u32[]{:S(2)}) collective-permute-start(bf16[256,1024]{1,0:T(8,128)(2,1)S(1)} %bitcast.16), channel_id=1, source_target_pairs={{0,1},{1,0},{2,3},{3,2},{4,5},{5,4},{6,7},{7,6},{8,9},{9,8},{10,11... | collective-permute-start | bytes 1572872 | tf_op jit(solution)/shard_map/ppermute | solution.py:937
  31.6 24.3 %collective-permute-start.4 = (bf16[256,1024]{1,0:T(8,128)(2,1)S(1)}, bf16[256,1024]{1,0:T(8,128)(2,1)S(1)}, u32[]{:S(2)}, u32[]{:S(2)}) collective-permute-start(bf16[256,1024]{1,0:T(8,128)(2,1)S(1)} %bitcast.17), channel_id=1, source_target_pairs={{1,2},{2,1},{5,6},{6,5},{9,10},{10,9},{13,14},{14,13},{17,18},{18,... | collective-permute-start | bytes 1572872 | tf_op jit(solution)/shard_map/ppermute | solution.py:937
  56.7 13.2 %collective-permute-start.6 = (bf16[256,1024]{1,0:T(8,128)(2,1)S(1)}, bf16[256,1024]{1,0:T(8,128)(2,1)S(1)}, u32[]{:S(2)}, u32[]{:S(2)}) collective-permute-start(bf16[256,1024]{1,0:T(8,128)(2,1)S(1)} %collective-permute-done.4.left_ref), channel_id=1, source_target_pairs={{1,0},{2,3},{5,4},{6,7},{9,8},{10,11},{13,12},{14,15},{17,16},{18,... | collective-permute-start | bytes 1572872 | tf_op jit(solution)/shard_map/ppermute | solution.py:937
  69.9 14.4 %collective-permute-start.9 = (bf16[256,1024]{1,0:T(8,128)(2,1)S(1)}, bf16[256,1024]{1,0:T(8,128)(2,1)S(1)}, u32[]{:S(2)}, u32[]{:S(2)}) collective-permute-start(bf16[256,1024]{1,0:T(8,128)(2,1)S(1)} %collective-permute-done.5.left_ref), channel_id=1, source_target_pairs={{1,0},{2,3},{5,4},{6,7},{9,8},{10,11},{13,12},{14,15},{17,16},{18,... | collective-permute-start | bytes 1572872 | tf_op jit(solution)/shard_map/ppermute | solution.py:937
  72.9 13.8 %collective-permute-start.7 = (bf16[256,1024]{1,0:T(8,128)(2,1)S(1)}, bf16[256,1024]{1,0:T(8,128)(2,1)S(1)}, u32[]{:S(2)}, u32[]{:S(2)}) collective-permute-start(bf16[256,1024]{1,0:T(8,128)(2,1)S(1)} %get-tuple-element.257), channel_id=1, source_target_pairs={{0,1},{3,2},{4,5},{7,6},{8,9},{11,10},{12,13},{15,14},{16,17},{19,... | collective-permute-start | bytes 1572872 | tf_op jit(solution)/shard_map/ppermute | solution.py:937
  86.9 8.0 %collective-permute-start.8 = (bf16[256,1024]{1,0:T(8,128)(2,1)S(1)}, bf16[256,1024]{1,0:T(8,128)(2,1)S(1)}, u32[]{:S(2)}, u32[]{:S(2)}) collective-permute-start(bf16[256,1024]{1,0:T(8,128)(2,1)S(1)} %shard_map.255), channel_id=1, source_target_pairs={{1,2},{2,1},{5,6},{6,5},{9,10},{10,9},{13,14},{14,13},{17,18},{18,... | collective-permute-start | bytes 1572872 | tf_op jit(solution)/shard_map/ppermute | solution.py:937
  104.4 34.7 %collective-permute-start.19 = (bf16[4,64,1024]{2,1,0:T(8,128)(2,1)S(1)}, bf16[4,64,1024]{2,1,0:T(8,128)(2,1)S(1)}, u32[]{:S(2)}, u32[]{:S(2)}) collective-permute-start(bf16[4,64,1024]{2,1,0:T(8,128)(2,1)S(1)} %get-tuple-element.329), channel_id=1, source_target_pairs={{0,4},{4,0},{8,12},{12,8},{16,20},{20,16},{24,28},{28,24},{1,5},{5... | collective-permute-start | bytes 1572872 | tf_op jit(solution)/shard_map/ppermute | solution.py:804
  104.6 38.2 %collective-permute-start.12 = (bf16[256,1024]{1,0:T(8,128)(2,1)S(1)}, bf16[256,1024]{1,0:T(8,128)(2,1)S(1)}, u32[]{:S(2)}, u32[]{:S(2)}) collective-permute-start(bf16[256,1024]{1,0:T(8,128)(2,1)S(1)} %get-tuple-element.308), channel_id=1, source_target_pairs={{0,1},{3,2},{4,5},{7,6},{8,9},{11,10},{12,13},{15,14},{16,17},{19,... | collective-permute-start | bytes 1572872 | tf_op jit(solution)/shard_map/ppermute | solution.py:937
  114.0 6.4 %collective-permute-start.14 = (bf16[1,80,1024]{2,1,0:T(8,128)(2,1)S(1)}, bf16[1,80,1024]{2,1,0:T(8,128)(2,1)S(1)}, u32[]{:S(2)}, u32[]{:S(2)}) collective-permute-start(bf16[1,80,1024]{2,1,0:T(8,128)(2,1)S(1)} %get-tuple-element.310), channel_id=1, source_target_pairs={{0,16},{4,20},{8,24},{12,28},{16,0},{20,4},{24,8},{28,12},{1,17},{... | collective-permute-start | bytes 491528 | tf_op jit(solution)/shard_map/ppermute | solution.py:804
  116.7 39.0 %collective-permute-start.27 = (bf16[256,1024]{1,0:T(8,128)(2,1)S(1)}, bf16[256,1024]{1,0:T(8,128)(2,1)S(1)}, u32[]{:S(2)}, u32[]{:S(2)}) collective-permute-start(bf16[256,1024]{1,0:T(8,128)(2,1)S(1)} %shard_map.266), channel_id=1, source_target_pairs={{0,1},{1,0},{2,3},{3,2},{4,5},{5,4},{6,7},{7,6},{8,9},{9,8},{10,11... | collective-permute-start | bytes 1572872 | tf_op jit(solution)/shard_map/ppermute | solution.py:937
  116.8 6.1 %collective-permute-start.15 = (bf16[1,80,1024]{2,1,0:T(8,128)(2,1)S(1)}, bf16[1,80,1024]{2,1,0:T(8,128)(2,1)S(1)}, u32[]{:S(2)}, u32[]{:S(2)}) collective-permute-start(bf16[1,80,1024]{2,1,0:T(8,128)(2,1)S(1)} %get-tuple-element.311), channel_id=1, source_target_pairs={{0,8},{4,12},{8,0},{12,4},{16,24},{20,28},{24,16},{28,20},{1,9},{5... | collective-permute-start | bytes 491528 | tf_op jit(solution)/shard_map/ppermute | solution.py:804
  120.4 6.4 %collective-permute-start.16 = (bf16[1,80,1024]{2,1,0:T(8,128)(2,1)S(1)}, bf16[1,80,1024]{2,1,0:T(8,128)(2,1)S(1)}, u32[]{:S(2)}, u32[]{:S(2)}) collective-permute-start(bf16[1,80,1024]{2,1,0:T(8,128)(2,1)S(1)} %get-tuple-element.312), channel_id=1, source_target_pairs={{0,24},{4,28},{8,16},{12,20},{16,8},{20,12},{24,0},{28,4},{1,25},{... | collective-permute-start | bytes 491528 | tf_op jit(solution)/shard_map/ppermute | solution.py:804
  126.8 12.3 %collective-permute-start.17 = (bf16[1,48,1024]{2,1,0:T(8,128)(2,1)S(1)}, bf16[1,48,1024]{2,1,0:T(8,128)(2,1)S(1)}, u32[]{:S(2)}, u32[]{:S(2)}) collective-permute-start(bf16[1,48,1024]{2,1,0:T(8,128)(2,1)S(1)} %get-tuple-element.324.left_ref), channel_id=1, source_target_pairs={{0,1},{1,0},{2,3},{3,2},{4,5},{5,4},{6,7},{7,6},{8,9},{9,8},{10,11... | collective-permute-start | bytes 294920 | tf_op jit(solution)/shard_map/ppermute | solution.py:811
  139.3 11.5 %collective-permute-start.23 = (bf16[1,64,1024]{2,1,0:T(8,128)(2,1)S(1)}, bf16[1,64,1024]{2,1,0:T(8,128)(2,1)S(1)}, u32[]{:S(2)}, u32[]{:S(2)}) collective-permute-start(bf16[1,64,1024]{2,1,0:T(8,128)(2,1)S(1)} %get-tuple-element.340), channel_id=1, source_target_pairs={{0,16},{4,20},{8,24},{12,28},{16,0},{20,4},{24,8},{28,12},{1,17},{... | collective-permute-start | bytes 393224 | tf_op jit(solution)/shard_map/ppermute | solution.py:804
  140.9 11.4 %collective-permute-start.24 = (bf16[1,64,1024]{2,1,0:T(8,128)(2,1)S(1)}, bf16[1,64,1024]{2,1,0:T(8,128)(2,1)S(1)}, u32[]{:S(2)}, u32[]{:S(2)}) collective-permute-start(bf16[1,64,1024]{2,1,0:T(8,128)(2,1)S(1)} %get-tuple-element.341), channel_id=1, source_target_pairs={{0,8},{4,12},{8,0},{12,4},{16,24},{20,28},{24,16},{28,20},{1,9},{5... | collective-permute-start | bytes 393224 | tf_op jit(solution)/shard_map/ppermute | solution.py:804
  142.4 10.4 %collective-permute-start.25 = (bf16[1,64,1024]{2,1,0:T(8,128)(2,1)S(1)}, bf16[1,64,1024]{2,1,0:T(8,128)(2,1)S(1)}, u32[]{:S(2)}, u32[]{:S(2)}) collective-permute-start(bf16[1,64,1024]{2,1,0:T(8,128)(2,1)S(1)} %get-tuple-element.342), channel_id=1, source_target_pairs={{0,24},{4,28},{8,16},{12,20},{16,8},{20,12},{24,0},{28,4},{1,25},{... | collective-permute-start | bytes 393224 | tf_op jit(solution)/shard_map/ppermute | solution.py:804
  142.8 6.3 %collective-permute-start.18 = (bf16[1,48,1024]{2,1,0:T(8,128)(2,1)S(1)}, bf16[1,48,1024]{2,1,0:T(8,128)(2,1)S(1)}, u32[]{:S(2)}, u32[]{:S(2)}) collective-permute-start(bf16[1,48,1024]{2,1,0:T(8,128)(2,1)S(1)} %shard_map.267.shared_ref), channel_id=1, source_target_pairs={{0,2},{1,3},{2,0},{3,1},{4,6},{5,7},{6,4},{7,5},{8,10},{9,11},{10,... | collective-permute-start | bytes 294920 | tf_op jit(solution)/shard_map/ppermute | solution.py:811
  149.2 10.9 %collective-permute-start.20 = (bf16[1,80,1024]{2,1,0:T(8,128)(2,1)S(1)}, bf16[1,80,1024]{2,1,0:T(8,128)(2,1)S(1)}, u32[]{:S(2)}, u32[]{:S(2)}) collective-permute-start(bf16[1,80,1024]{2,1,0:T(8,128)(2,1)S(1)} %shard_map.271.refs_0_.refs_5_), channel_id=1, source_target_pairs={{0,16},{4,20},{8,24},{12,28},{16,0},{20,4},{24,8},{28,12},{1,17},{... | collective-permute-start | bytes 491528 | tf_op jit(solution)/shard_map/ppermute | solution.py:804
  150.8 9.4 %collective-permute-start.21 = (bf16[1,80,1024]{2,1,0:T(8,128)(2,1)S(1)}, bf16[1,80,1024]{2,1,0:T(8,128)(2,1)S(1)}, u32[]{:S(2)}, u32[]{:S(2)}) collective-permute-start(bf16[1,80,1024]{2,1,0:T(8,128)(2,1)S(1)} %shard_map.271.refs_0_.refs_5_), channel_id=1, source_target_pairs={{0,8},{4,12},{8,0},{12,4},{16,24},{20,28},{24,16},{28,20},{1,9},{5... | collective-permute-start | bytes 491528 | tf_op jit(solution)/shard_map/ppermute | solution.py:804
  152.3 7.9 %collective-permute-start.22 = (bf16[1,80,1024]{2,1,0:T(8,128)(2,1)S(1)}, bf16[1,80,1024]{2,1,0:T(8,128)(2,1)S(1)}, u32[]{:S(2)}, u32[]{:S(2)}) collective-permute-start(bf16[1,80,1024]{2,1,0:T(8,128)(2,1)S(1)} %shard_map.271.refs_0_.refs_5_), channel_id=1, source_target_pairs={{0,24},{4,28},{8,16},{12,20},{16,8},{20,12},{24,0},{28,4},{1,25},{... | collective-permute-start | bytes 491528 | tf_op jit(solution)/shard_map/ppermute | solution.py:804
  152.8 5.1 %collective-permute-start.26 = (bf16[1,48,1024]{2,1,0:T(8,128)(2,1)S(1)}, bf16[1,48,1024]{2,1,0:T(8,128)(2,1)S(1)}, u32[]{:S(2)}, u32[]{:S(2)}) collective-permute-start(bf16[1,48,1024]{2,1,0:T(8,128)(2,1)S(1)} %get-tuple-element.346.left_ref), channel_id=1, source_target_pairs={{0,1},{1,0},{2,3},{3,2},{4,5},{5,4},{6,7},{7,6},{8,9},{9,8},{10,11... | collective-permute-start | bytes 294920 | tf_op jit(solution)/shard_map/ppermute | solution.py:811
  155.7 5.5 %collective-permute-start.13 = (bf16[256,1024]{1,0:T(8,128)(2,1)S(1)}, bf16[256,1024]{1,0:T(8,128)(2,1)S(1)}, u32[]{:S(2)}, u32[]{:S(2)}) collective-permute-start(bf16[256,1024]{1,0:T(8,128)(2,1)S(1)} %shard_map.263), channel_id=1, source_target_pairs={{1,2},{2,1},{5,6},{6,5},{9,10},{10,9},{13,14},{14,13},{17,18},{18,... | collective-permute-start | bytes 1572872 | tf_op jit(solution)/shard_map/ppermute | solution.py:937
  157.9 11.9 %collective-permute-start.11 = (bf16[256,1024]{1,0:T(8,128)(2,1)S(1)}, bf16[256,1024]{1,0:T(8,128)(2,1)S(1)}, u32[]{:S(2)}, u32[]{:S(2)}) collective-permute-start(bf16[256,1024]{1,0:T(8,128)(2,1)S(1)} %shard_map.262), channel_id=1, source_target_pairs={{0,1},{1,0},{2,3},{3,2},{4,5},{5,4},{6,7},{7,6},{8,9},{9,8},{10,11... | collective-permute-start | bytes 1572872 | tf_op jit(solution)/shard_map/ppermute | solution.py:937
  160.2 14.4 %collective-permute-start.34 = (bf16[4,80,1024]{2,1,0:T(8,128)(2,1)S(1)}, bf16[4,80,1024]{2,1,0:T(8,128)(2,1)S(1)}, u32[]{:S(2)}, u32[]{:S(2)}) collective-permute-start(bf16[4,80,1024]{2,1,0:T(8,128)(2,1)S(1)} %shard_map.276), channel_id=1, source_target_pairs={{0,4},{4,0},{8,12},{12,8},{16,20},{20,16},{24,28},{28,24},{1,5},{5... | collective-permute-start | bytes 1966088 | tf_op jit(solution)/shard_map/ppermute | solution.py:804
  160.3 10.7 %collective-permute-start.30 = (bf16[1,48,1024]{2,1,0:T(8,128)(2,1)S(1)}, bf16[1,48,1024]{2,1,0:T(8,128)(2,1)S(1)}, u32[]{:S(2)}, u32[]{:S(2)}) collective-permute-start(bf16[1,48,1024]{2,1,0:T(8,128)(2,1)S(1)} %shard_map.275.shared_ref), channel_id=1, source_target_pairs={{0,2},{1,3},{2,0},{3,1},{4,6},{5,7},{6,4},{7,5},{8,10},{9,11},{10,... | collective-permute-start | bytes 294920 | tf_op jit(solution)/shard_map/ppermute | solution.py:811
  171.0 5.2 %collective-permute-start.31 = (bf16[1,64,1024]{2,1,0:T(8,128)(2,1)S(1)}, bf16[1,64,1024]{2,1,0:T(8,128)(2,1)S(1)}, u32[]{:S(2)}, u32[]{:S(2)}) collective-permute-start(bf16[1,64,1024]{2,1,0:T(8,128)(2,1)S(1)} %shard_map.278.refs_0_.refs_5_), channel_id=1, source_target_pairs={{0,16},{4,20},{8,24},{12,28},{16,0},{20,4},{24,8},{28,12},{1,17},{... | collective-permute-start | bytes 393224 | tf_op jit(solution)/shard_map/ppermute | solution.py:804
  174.1 5.9 %collective-permute-start.33 = (bf16[1,64,1024]{2,1,0:T(8,128)(2,1)S(1)}, bf16[1,64,1024]{2,1,0:T(8,128)(2,1)S(1)}, u32[]{:S(2)}, u32[]{:S(2)}) collective-permute-start(bf16[1,64,1024]{2,1,0:T(8,128)(2,1)S(1)} %shard_map.278.refs_0_.refs_5_), channel_id=1, source_target_pairs={{0,24},{4,28},{8,16},{12,20},{16,8},{20,12},{24,0},{28,4},{1,25},{... | collective-permute-start | bytes 393224 | tf_op jit(solution)/shard_map/ppermute | solution.py:804
  180.0 14.8 %collective-permute-start.28 = (bf16[256,1024]{1,0:T(8,128)(2,1)S(1)}, bf16[256,1024]{1,0:T(8,128)(2,1)S(1)}, u32[]{:S(2)}, u32[]{:S(2)}) collective-permute-start(bf16[256,1024]{1,0:T(8,128)(2,1)S(1)} %shard_map.270), channel_id=1, source_target_pairs={{0,1},{1,0},{2,3},{3,2},{4,5},{5,4},{6,7},{7,6},{8,9},{9,8},{10,11... | collective-permute-start | bytes 1572872 | tf_op jit(solution)/shard_map/ppermute | solution.py:937
  182.3 25.2 %collective-permute-start.29 = (bf16[256,1024]{1,0:T(8,128)(2,1)S(1)}, bf16[256,1024]{1,0:T(8,128)(2,1)S(1)}, u32[]{:S(2)}, u32[]{:S(2)}) collective-permute-start(bf16[256,1024]{1,0:T(8,128)(2,1)S(1)} %shard_map.274), channel_id=1, source_target_pairs={{0,3},{1,2},{2,1},{3,0},{4,7},{5,6},{6,5},{7,4},{8,11},{9,10},{10,... | collective-permute-start | bytes 1572872 | tf_op jit(solution)/shard_map/ppermute | solution.py:937
  (30 other events, 72.1 us)

commit v2 on v1

--- a/solution.py
+++ b/solution.py
@@ -1053,7 +1053,6 @@
             adapter_up_second,
             gain_m,
         )
-        y_5 = send(added(y_facing, after(y_2, before)), middle)
         g_end = after(g_end, before)
         g_facing = added(g_mid, g_end)
         backs[2] = pulled(2, g_facing)
@@ -1084,10 +1083,6 @@
     early = GroupSum(early, 3 * rank // members)
     early.start()
     grads_mixed = [back[0] for back in backs]
-    if short:
-        last = early.finish()
-        early.start()
-        grads_mixed = after(grads_mixed, last)
     halves = []
     for part in range(2):
         halves.append(
@@ -1096,7 +1091,10 @@
             )
         )
         if short and not part:
-            y_near = added(y_near, after(y_3, halves[0]))
+            last = early.finish(halves[0])
+            early.start()
+            y_5 = send(added(y_facing, after(y_2, last)), middle)
+            y_near = added(y_near, after(y_3, last))
             y_4 = send(y_near, swap)
             grads_mixed = after(grads_mixed, y_near)
     grad_pre = list(zip(*halves))

time: 210 us -> 212 us (level)
    ppermute x4, waiting for transfers between devices: 13.6 us -> 20.1 us  [start(): self.moving = lax.ppermute(self.shared, 'tensor', pairs)]
    ppermute x16, waiting for transfers between devices: 43.1 us -> 39.1 us  [send(): return lax.ppermute(value, 'tensor', pairs)]
    ppermute x4, starting transfers between devices: 6.6 us -> 10.1 us  [start(): self.moving = lax.ppermute(self.shared, 'tensor', pairs)]
    ppermute x16, starting transfers between devices: 34 us -> 30.9 us  [send(): return lax.ppermute(value, 'tensor', pairs)]
where the time goes in v2:
time: 212 us; the launch traced here: 211 us
  waiting for transfers between devices  68.8 us (32%)
  Pallas kernels  68 us (32%)
  starting transfers between devices  58 us (27%)
  local copies, waits for them, and re-layouts  15.4 us (7%)
    pallas_call x42, Pallas kernels, call(): pl.pallas_call(kernel, in_specs=[pl.BlockSpec(memory_space=space) for spa...  65.1 us
    ppermute x16, waiting for transfers between devices, send(): return lax.ppermute(value, 'tensor', pairs)  39.1 us
    ppermute x16, starting transfers between devices, send(): return lax.ppermute(value, 'tensor', pairs)  30.9 us
    ppermute x4, waiting for transfers between devices, start(): self.moving = lax.ppermute(self.shared, 'tensor', pairs)  20.1 us
    ppermute x16, starting transfers between devices, hop(): return lax.ppermute(value, 'dp', pairs)  17 us
    unnamed x52, local copies, waits for them, and re-layouts  15.4 us
    ppermute x4, starting transfers between devices, start(): self.moving = lax.ppermute(self.shared, 'tensor', pairs)  10.1 us
    ppermute x16, waiting for transfers between devices, hop(): return lax.ppermute(value, 'dp', pairs)  9.61 us
  transfers between devices with their start and end apart: 36, of which 14 were waited for; matrix products, arithmetic and copies ran while one was open for 0% of the time, Pallas kernels for 27%

profile of v2, /device:TPU:0, one launch (start us, length us, event | category | flops | bytes accessed | tf_op | source)
XLA Modules:
  0.0 211.4 jit_solution(81654845856569700)
XLA Ops:
  0.7 3.1 %collective-permute-start = (bf16[256,1024]{1,0:T(8,128)(2,1)}, bf16[256,1024]{1,0:T(8,128)(2,1)S(1)}, u32[]{:S(2)}, u32[]{:S(2)}) collective-permute-start(bf16[256,1024]{1,0:T(8,128)(2,1)} %bitcast.11), channel_id=1, source_target_pairs={{0,1},{1,0},{2,3},{3,2},{4,5},{5,4},{6,7},{7,6},{8,9},{9,8},{10,11... | collective-permute-start | bytes 1572872 | tf_op jit(solution)/shard_map/ppermute | solution.py:937
  3.8 2.5 %collective-permute-start.1 = (bf16[256,1024]{1,0:T(8,128)(2,1)}, bf16[256,1024]{1,0:T(8,128)(2,1)S(1)}, u32[]{:S(2)}, u32[]{:S(2)}) collective-permute-start(bf16[256,1024]{1,0:T(8,128)(2,1)} %bitcast.12), channel_id=1, source_target_pairs={{0,3},{1,2},{2,1},{3,0},{4,7},{5,6},{6,5},{7,4},{8,11},{9,10},{10,... | collective-permute-start | bytes 1572872 | tf_op jit(solution)/shard_map/ppermute | solution.py:937
  22.3 2.8 %shard_map.242 = (bf16[1024,768]{1,0:T(8,128)(2,1)S(1)}, bf16[1024,1024]{1,0:T(8,128)(2,1)S(1)}, bf16[256,1024]{1,0:T(8,128)(2,1)S(1)}, bf16[1024,1024]{1,0:T(8,128)(2,1)S(1)}) custom-call(bf16[3,1024,256]{2,1,0:T(8,128)(2,1)S(1)} %copy-done.2, bf16[3,1024,128]{2,1,0:T(8,128)(2,1)S(1)} %copy-done.4, bf16[3,128,256]{2,1,0:T(8,128)(2,1)S(1)} %copy-done.7, ...), custom_call_target="tpu_custom_call" | custom-call | flops 805306368 | bytes 12582912 | tf_op jit(solution)/shard_map/pallas_call | solution.py:140
  25.2 4.3 %shard_map.241 = (bf16[3,4,64,256]{3,2,1,0:T(8,128)(2,1)S(1)}, bf16[256,512]{1,0:T(8,128)(2,1)S(1)}, bf16[256,1024]{1,0:T(8,128)(2,1)S(1)}, bf16[256,1024]{1,0:T(8,128)(2,1)S(1)}, bf16[256,1024]{1,0:T(8,128)(2,1)S(1)}) custom-call(bf16[256,1024]{1,0:T(8,128)(2,1)S(1)} %bitcast.13, f32[1,1024]{1,0:T(1,128)S(1)} %bitcast.29, f32[1,1024]{1,0:T(1,128)S(1)} %bitcast.22, ...), custom_call_target="tpu_custom_call" | custom-call | flops 1207959552 | bytes 4456448 | tf_op jit(solution)/shard_map/pallas_call | solution.py:33
  32.3 4.3 %shard_map.244 = (bf16[3,4,64,256]{3,2,1,0:T(8,128)(2,1)S(1)}, bf16[256,512]{1,0:T(8,128)(2,1)S(1)}, bf16[256,1024]{1,0:T(8,128)(2,1)S(1)}, bf16[256,1024]{1,0:T(8,128)(2,1)S(1)}, bf16[256,1024]{1,0:T(8,128)(2,1)S(1)}) custom-call(bf16[256,1024]{1,0:T(8,128)(2,1)S(1)} %collective-permute-done.1.x_ref, f32[1,1024]{1,0:T(1,128)S(1)} %bitcast.30, ...), custom_call_target="tpu_custom_call" | custom-call | flops 1207959552 | bytes 4456448 | tf_op jit(solution)/shard_map/pallas_call | solution.py:33
  36.6 4.3 %shard_map.243 = (bf16[3,4,64,256]{3,2,1,0:T(8,128)(2,1)S(1)}, bf16[256,512]{1,0:T(8,128)(2,1)S(1)}, bf16[256,1024]{1,0:T(8,128)(2,1)S(1)}, bf16[256,1024]{1,0:T(8,128)(2,1)S(1)}, bf16[256,1024]{1,0:T(8,128)(2,1)S(1)}) custom-call(bf16[256,1024]{1,0:T(8,128)(2,1)S(1)} %collective-permute-done.x_ref, f32[1,1024]{1,0:T(1,128)S(1)} %bitcast.31, ...), custom_call_target="tpu_custom_call" | custom-call | flops 1207959552 | bytes 4456448 | tf_op jit(solution)/shard_map/pallas_call | solution.py:33
  40.8 3.5 %collective-permute-done.2.x_ref = bf16[256,1024]{1,0:T(8,128)(2,1)S(1)} collective-permute-done((bf16[256,1024]{1,0:T(8,128)(2,1)S(1)}, bf16[256,1024]{1,0:T(8,128)(2,1)S(1)}, u32[]{:S(2)}, u32[]{:S(2)}) %collective-permute-start.2) | collective-permute-done | bytes 524320 | tf_op jit(solution)/shard_map/ppermute | solution.py:937
  44.4 4.3 %shard_map.245 = (bf16[3,4,64,256]{3,2,1,0:T(8,128)(2,1)S(1)}, bf16[256,512]{1,0:T(8,128)(2,1)S(1)}, bf16[256,1024]{1,0:T(8,128)(2,1)S(1)}, bf16[256,1024]{1,0:T(8,128)(2,1)S(1)}, bf16[256,1024]{1,0:T(8,128)(2,1)S(1)}) custom-call(bf16[256,1024]{1,0:T(8,128)(2,1)S(1)} %collective-permute-done.2.x_ref, f32[1,1024]{1,0:T(1,128)S(1)} %bitcast.32, ...), custom_call_target="tpu_custom_call" | custom-call | flops 1207959552 | bytes 4456448 | tf_op jit(solution)/shard_map/pallas_call | solution.py:33
  48.6 7.2 %shard_map.246 = (bf16[4,64,256]{2,1,0:T(8,128)(2,1)S(1)}, bf16[4,64,256]{2,1,0:T(8,128)(2,1)S(1)}, bf16[4,64,256]{2,1,0:T(8,128)(2,1)S(1)}, bf16[4,64,256]{2,1,0:T(8,128)(2,1)S(1)}, f32[4,1,1024]{2,1,0:T(1,128)S(1)}) custom-call(s32[4]{0:T(128)S(1)} %pad_add_fusion.places_ref.refs_0_, s32[1,1024]{1,0:T(1,128)S(1)} %get-tuple-element.190.refs_1_, ...), custom_call_target="tpu_custom_call" | custom-call | flops 2147483648 | bytes 1081344 | tf_op jit(solution)/shard_map/pallas_call | solution.py:33
  60.7 9.2 %collective-permute-done.6.right_ref = bf16[256,1024]{1,0:T(8,128)(2,1)S(1)} collective-permute-done((bf16[256,1024]{1,0:T(8,128)(2,1)S(1)}, bf16[256,1024]{1,0:T(8,128)(2,1)S(1)}, u32[]{:S(2)}, u32[]{:S(2)}) %collective-permute-start.6) | collective-permute-done | bytes 524320 | tf_op jit(solution)/shard_map/ppermute | solution.py:937
  72.9 4.6 %collective-permute-start.7 = (bf16[256,1024]{1,0:T(8,128)(2,1)S(1)}, bf16[256,1024]{1,0:T(8,128)(2,1)S(1)}, u32[]{:S(2)}, u32[]{:S(2)}) collective-permute-start(bf16[256,1024]{1,0:T(8,128)(2,1)S(1)} %get-tuple-element.254), channel_id=1, source_target_pairs={{0,1},{3,2},{4,5},{7,6},{8,9},{11,10},{12,13},{15,14},{16,17},{19,... | collective-permute-start | bytes 1572872 | tf_op jit(solution)/shard_map/ppermute | solution.py:937
  82.0 2.2 %shard_map.256 = (f32[384,1024]{1,0:T(8,128)S(1)}, f32[256,1024]{1,0:T(8,128)S(1)}, f32[128,256]{1,0:T(8,128)S(1)}) custom-call(s32[1]{0:T(128)} %bitcast.4.refs_0_, bf16[128,1024]{1,0:T(8,128)(2,1)S(1)} %copy-done.6, f32[1,1024]{1,0:T(1,128)S(1)} %bitcast.26, bf16[256,1024]{1,0:T(8,128)(2,1)S(1)} %bitcast.19, ...), custom_call_target="tpu_custom_call" | custom-call | flops 1207959552 | bytes 5505024 | tf_op jit(solution)/shard_map/pallas_call | solution.py:33
  87.8 5.9 %shard_map.260 = (bf16[3,2,64,256]{3,2,1,0:T(8,128)(2,1)S(1)}, bf16[3,2,64,256]{3,2,1,0:T(8,128)(2,1)S(1)}, bf16[3,2,64,256]{3,2,1,0:T(8,128)(2,1)S(1)}, bf16[3,2,64,256]{3,2,1,0:T(8,128)(2,1)S(1)}) custom-call(s32[4]{0:T(128)S(1)} %pad_add_fusion.places_ref.refs_0_, s32[1,1024]{1,0:T(1,128)S(1)} %get-tuple-element.190.refs_1_, ...), custom_call_target="tpu_custom_call" | custom-call | flops 2684354560 | bytes 1572864 | tf_op jit(solution)/shard_map/pallas_call | solution.py:33
  94.0 5.9 %shard_map.264 = (bf16[3,2,64,256]{3,2,1,0:T(8,128)(2,1)S(1)}, bf16[3,2,64,256]{3,2,1,0:T(8,128)(2,1)S(1)}, bf16[3,2,64,256]{3,2,1,0:T(8,128)(2,1)S(1)}, bf16[3,2,64,256]{3,2,1,0:T(8,128)(2,1)S(1)}) custom-call(s32[4]{0:T(128)S(1)} %pad_add_fusion.places_ref.refs_0_, s32[1,1024]{1,0:T(1,128)S(1)} %get-tuple-element.190.refs_1_, ...), custom_call_target="tpu_custom_call" | custom-call | flops 2684354560 | bytes 1572864 | tf_op jit(solution)/shard_map/pallas_call | solution.py:33
  99.9 3.5 %shard_map.268 = (bf16[4,64,1024]{2,1,0:T(8,128)(2,1)S(1)}, bf16[1,64,1024]{2,1,0:T(8,128)(2,1)S(1)}, bf16[1,64,1024]{2,1,0:T(8,128)(2,1)S(1)}, bf16[1,64,1024]{2,1,0:T(8,128)(2,1)S(1)}, bf16[1,64,1024]{2,1,0:T(8,128)(2,1)S(1)}) custom-call(s32[1]{0:T(128)} %bitcast.4.refs_0_, bf16[3,128,256]{2,1,0:T(8,128)(2,1)S(1)} %copy-done.8, f32[1,1024]{1,0:T(1,128)S(1)} %bitcast.33, ...), custom_call_target="tpu_custom_call" | custom-call | flops 1207959552 | bytes 2097152 | tf_op jit(solution)/shard_map/pallas_call | solution.py:33
  104.0 10.3 %collective-permute-start.12 = (bf16[256,1024]{1,0:T(8,128)(2,1)S(1)}, bf16[256,1024]{1,0:T(8,128)(2,1)S(1)}, u32[]{:S(2)}, u32[]{:S(2)}) collective-permute-start(bf16[256,1024]{1,0:T(8,128)(2,1)S(1)} %get-tuple-element.302), channel_id=1, source_target_pairs={{0,1},{3,2},{4,5},{7,6},{8,9},{11,10},{12,13},{15,14},{16,17},{19,... | collective-permute-start | bytes 1572872 | tf_op jit(solution)/shard_map/ppermute | solution.py:937
  118.6 2.0 collective-permute-done.14.refs_1_
  120.6 2.5 %collective-permute-start.16 = (bf16[1,80,1024]{2,1,0:T(8,128)(2,1)S(1)}, bf16[1,80,1024]{2,1,0:T(8,128)(2,1)S(1)}, u32[]{:S(2)}, u32[]{:S(2)}) collective-permute-start(bf16[1,80,1024]{2,1,0:T(8,128)(2,1)S(1)} %get-tuple-element.306), channel_id=1, source_target_pairs={{0,24},{4,28},{8,16},{12,20},{16,8},{20,12},{24,0},{28,4},{1,25},{... | collective-permute-start | bytes 491528 | tf_op jit(solution)/shard_map/ppermute | solution.py:804
  123.2 3.8 %collective-permute-done.16.refs_3_ = bf16[1,80,1024]{2,1,0:T(8,128)(2,1)S(1)} collective-permute-done((bf16[1,80,1024]{2,1,0:T(8,128)(2,1)S(1)}, bf16[1,80,1024]{2,1,0:T(8,128)(2,1)S(1)}, u32[]{:S(2)}, u32[]{:S(2)}) %collective-permute-start.16) | collective-permute-done | bytes 163872 | tf_op jit(solution)/shard_map/ppermute | solution.py:804
  128.4 10.7 %collective-permute-done.17.right_ref = bf16[1,48,1024]{2,1,0:T(8,128)(2,1)S(1)} collective-permute-done((bf16[1,48,1024]{2,1,0:T(8,128)(2,1)S(1)}, bf16[1,48,1024]{2,1,0:T(8,128)(2,1)S(1)}, u32[]{:S(2)}, u32[]{:S(2)}) %collective-permute-start.17) | collective-permute-done | bytes 98336 | tf_op jit(solution)/shard_map/ppermute | solution.py:811
  142.8 2.5 %collective-permute-start.18 = (bf16[1,48,1024]{2,1,0:T(8,128)(2,1)S(1)}, bf16[1,48,1024]{2,1,0:T(8,128)(2,1)S(1)}, u32[]{:S(2)}, u32[]{:S(2)}) collective-permute-start(bf16[1,48,1024]{2,1,0:T(8,128)(2,1)S(1)} %shard_map.267.shared_ref), channel_id=1, source_target_pairs={{0,2},{1,3},{2,0},{3,1},{4,6},{5,7},{6,4},{7,5},{8,10},{9,11},{10,... | collective-permute-start | bytes 294920 | tf_op jit(solution)/shard_map/ppermute | solution.py:811
  146.6 2.6 %collective-permute-done.18.arrived_ref = bf16[1,48,1024]{2,1,0:T(8,128)(2,1)S(1)} collective-permute-done((bf16[1,48,1024]{2,1,0:T(8,128)(2,1)S(1)}, bf16[1,48,1024]{2,1,0:T(8,128)(2,1)S(1)}, u32[]{:S(2)}, u32[]{:S(2)}) %collective-permute-start.18) | collective-permute-done | bytes 98336 | tf_op jit(solution)/shard_map/ppermute | solution.py:811
  152.8 1.8 collective-permute-start.26
  159.4 4.4 %collective-permute-start.30 = (bf16[1,48,1024]{2,1,0:T(8,128)(2,1)S(1)}, bf16[1,48,1024]{2,1,0:T(8,128)(2,1)S(1)}, u32[]{:S(2)}, u32[]{:S(2)}) collective-permute-start(bf16[1,48,1024]{2,1,0:T(8,128)(2,1)S(1)} %shard_map.275.shared_ref), channel_id=1, source_target_pairs={{0,2},{1,3},{2,0},{3,1},{4,6},{5,7},{6,4},{7,5},{8,10},{9,11},{10,... | collective-permute-start | bytes 294920 | tf_op jit(solution)/shard_map/ppermute | solution.py:811
  163.9 4.5 %collective-permute-done.11.rest_0_ = bf16[256,1024]{1,0:T(8,128)(2,1)S(1)} collective-permute-done((bf16[256,1024]{1,0:T(8,128)(2,1)S(1)}, bf16[256,1024]{1,0:T(8,128)(2,1)S(1)}, u32[]{:S(2)}, u32[]{:S(2)}) %collective-permute-start.11) | collective-permute-done | bytes 524320 | tf_op jit(solution)/shard_map/ppermute | solution.py:937
  169.3 5.6 %collective-permute-done.30.arrived_ref = bf16[1,48,1024]{2,1,0:T(8,128)(2,1)S(1)} collective-permute-done((bf16[1,48,1024]{2,1,0:T(8,128)(2,1)S(1)}, bf16[1,48,1024]{2,1,0:T(8,128)(2,1)S(1)}, u32[]{:S(2)}, u32[]{:S(2)}) %collective-permute-start.30) | collective-permute-done | bytes 98336 | tf_op jit(solution)/shard_map/ppermute | solution.py:811
  178.5 1.7 shard_map.279
  181.5 2.4 %collective-permute-done.33.refs_3_.refs_2_ = bf16[1,64,1024]{2,1,0:T(8,128)(2,1)S(1)} collective-permute-done((bf16[1,64,1024]{2,1,0:T(8,128)(2,1)S(1)}, bf16[1,64,1024]{2,1,0:T(8,128)(2,1)S(1)}, u32[]{:S(2)}, u32[]{:S(2)}) %collective-permute-start.33) | collective-permute-done | bytes 131104 | tf_op jit(solution)/shard_map/ppermute | solution.py:804
  186.1 1.6 shard_map.281
  187.7 11.2 %collective-permute-done.28.rest_0_ = bf16[256,1024]{1,0:T(8,128)(2,1)S(1)} collective-permute-done((bf16[256,1024]{1,0:T(8,128)(2,1)S(1)}, bf16[256,1024]{1,0:T(8,128)(2,1)S(1)}, u32[]{:S(2)}, u32[]{:S(2)}) %collective-permute-start.28) | collective-permute-done | bytes 524320 | tf_op jit(solution)/shard_map/ppermute | solution.py:937
  198.9 10.8 %collective-permute-done.29.rest_1_ = bf16[256,1024]{1,0:T(8,128)(2,1)S(1)} collective-permute-done((bf16[256,1024]{1,0:T(8,128)(2,1)S(1)}, bf16[256,1024]{1,0:T(8,128)(2,1)S(1)}, u32[]{:S(2)}, u32[]{:S(2)}) %collective-permute-start.29) | collective-permute-done | bytes 524320 | tf_op jit(solution)/shard_map/ppermute | solution.py:937
  209.7 1.7 shard_map.282
  (136 shorter events, 62.8 us)
Async XLA Ops:
  0.7 28.8 %collective-permute-start = (bf16[256,1024]{1,0:T(8,128)(2,1)}, bf16[256,1024]{1,0:T(8,128)(2,1)S(1)}, u32[]{:S(2)}, u32[]{:S(2)}) collective-permute-start(bf16[256,1024]{1,0:T(8,128)(2,1)} %bitcast.11), channel_id=1, source_target_pairs={{0,1},{1,0},{2,3},{3,2},{4,5},{5,4},{6,7},{7,6},{8,9},{9,8},{10,11... | collective-permute-start | bytes 1572872 | tf_op jit(solution)/shard_map/ppermute | solution.py:937
  3.8 25.7 %collective-permute-start.1 = (bf16[256,1024]{1,0:T(8,128)(2,1)}, bf16[256,1024]{1,0:T(8,128)(2,1)S(1)}, u32[]{:S(2)}, u32[]{:S(2)}) collective-permute-start(bf16[256,1024]{1,0:T(8,128)(2,1)} %bitcast.12), channel_id=1, source_target_pairs={{0,3},{1,2},{2,1},{3,0},{4,7},{5,6},{6,5},{7,4},{8,11},{9,10},{10,... | collective-permute-start | bytes 1572872 | tf_op jit(solution)/shard_map/ppermute | solution.py:937
  29.5 14.9 %collective-permute-start.2 = (bf16[256,1024]{1,0:T(8,128)(2,1)S(1)}, bf16[256,1024]{1,0:T(8,128)(2,1)S(1)}, u32[]{:S(2)}, u32[]{:S(2)}) collective-permute-start(bf16[256,1024]{1,0:T(8,128)(2,1)S(1)} %collective-permute-done.1.x_ref), channel_id=1, source_target_pairs={{0,1},{1,0},{2,3},{3,2},{4,5},{5,4},{6,7},{7,6},{8,9},{9,8},{10,11... | collective-permute-start | bytes 1572872 | tf_op jit(solution)/shard_map/ppermute | solution.py:937
  30.3 25.6 %collective-permute-start.3 = (bf16[256,1024]{1,0:T(8,128)(2,1)S(1)}, bf16[256,1024]{1,0:T(8,128)(2,1)S(1)}, u32[]{:S(2)}, u32[]{:S(2)}) collective-permute-start(bf16[256,1024]{1,0:T(8,128)(2,1)S(1)} %bitcast.16), channel_id=1, source_target_pairs={{0,1},{1,0},{2,3},{3,2},{4,5},{5,4},{6,7},{7,6},{8,9},{9,8},{10,11... | collective-permute-start | bytes 1572872 | tf_op jit(solution)/shard_map/ppermute | solution.py:937
  31.6 24.3 %collective-permute-start.4 = (bf16[256,1024]{1,0:T(8,128)(2,1)S(1)}, bf16[256,1024]{1,0:T(8,128)(2,1)S(1)}, u32[]{:S(2)}, u32[]{:S(2)}) collective-permute-start(bf16[256,1024]{1,0:T(8,128)(2,1)S(1)} %bitcast.17), channel_id=1, source_target_pairs={{1,2},{2,1},{5,6},{6,5},{9,10},{10,9},{13,14},{14,13},{17,18},{18,... | collective-permute-start | bytes 1572872 | tf_op jit(solution)/shard_map/ppermute | solution.py:937
  56.7 13.2 %collective-permute-start.6 = (bf16[256,1024]{1,0:T(8,128)(2,1)S(1)}, bf16[256,1024]{1,0:T(8,128)(2,1)S(1)}, u32[]{:S(2)}, u32[]{:S(2)}) collective-permute-start(bf16[256,1024]{1,0:T(8,128)(2,1)S(1)} %collective-permute-done.4.left_ref), channel_id=1, source_target_pairs={{1,0},{2,3},{5,4},{6,7},{9,8},{10,11},{13,12},{14,15},{17,16},{18,... | collective-permute-start | bytes 1572872 | tf_op jit(solution)/shard_map/ppermute | solution.py:937
  69.9 14.4 %collective-permute-start.9 = (bf16[256,1024]{1,0:T(8,128)(2,1)S(1)}, bf16[256,1024]{1,0:T(8,128)(2,1)S(1)}, u32[]{:S(2)}, u32[]{:S(2)}) collective-permute-start(bf16[256,1024]{1,0:T(8,128)(2,1)S(1)} %collective-permute-done.5.left_ref), channel_id=1, source_target_pairs={{1,0},{2,3},{5,4},{6,7},{9,8},{10,11},{13,12},{14,15},{17,16},{18,... | collective-permute-start | bytes 1572872 | tf_op jit(solution)/shard_map/ppermute | solution.py:937
  72.9 13.8 %collective-permute-start.7 = (bf16[256,1024]{1,0:T(8,128)(2,1)S(1)}, bf16[256,1024]{1,0:T(8,128)(2,1)S(1)}, u32[]{:S(2)}, u32[]{:S(2)}) collective-permute-start(bf16[256,1024]{1,0:T(8,128)(2,1)S(1)} %get-tuple-element.254), channel_id=1, source_target_pairs={{0,1},{3,2},{4,5},{7,6},{8,9},{11,10},{12,13},{15,14},{16,17},{19,... | collective-permute-start | bytes 1572872 | tf_op jit(solution)/shard_map/ppermute | solution.py:937
  86.7 7.0 %collective-permute-start.10 = (bf16[4,80,1024]{2,1,0:T(8,128)(2,1)S(1)}, bf16[4,80,1024]{2,1,0:T(8,128)(2,1)S(1)}, u32[]{:S(2)}, u32[]{:S(2)}) collective-permute-start(bf16[4,80,1024]{2,1,0:T(8,128)(2,1)S(1)} %get-tuple-element.285), channel_id=1, source_target_pairs={{0,4},{4,0},{8,12},{12,8},{16,20},{20,16},{24,28},{28,24},{1,5},{5... | collective-permute-start | bytes 1966088 | tf_op jit(solution)/shard_map/ppermute | solution.py:804
  86.9 7.0 %collective-permute-start.8 = (bf16[256,1024]{1,0:T(8,128)(2,1)S(1)}, bf16[256,1024]{1,0:T(8,128)(2,1)S(1)}, u32[]{:S(2)}, u32[]{:S(2)}) collective-permute-start(bf16[256,1024]{1,0:T(8,128)(2,1)S(1)} %shard_map.255), channel_id=1, source_target_pairs={{1,2},{2,1},{5,6},{6,5},{9,10},{10,9},{13,14},{14,13},{17,18},{18,... | collective-permute-start | bytes 1572872 | tf_op jit(solution)/shard_map/ppermute | solution.py:937
  103.4 35.7 %collective-permute-start.19 = (bf16[4,64,1024]{2,1,0:T(8,128)(2,1)S(1)}, bf16[4,64,1024]{2,1,0:T(8,128)(2,1)S(1)}, u32[]{:S(2)}, u32[]{:S(2)}) collective-permute-start(bf16[4,64,1024]{2,1,0:T(8,128)(2,1)S(1)} %get-tuple-element.323), channel_id=1, source_target_pairs={{0,4},{4,0},{8,12},{12,8},{16,20},{20,16},{24,28},{28,24},{1,5},{5... | collective-permute-start | bytes 1572872 | tf_op jit(solution)/shard_map/ppermute | solution.py:804
  104.0 38.9 %collective-permute-start.12 = (bf16[256,1024]{1,0:T(8,128)(2,1)S(1)}, bf16[256,1024]{1,0:T(8,128)(2,1)S(1)}, u32[]{:S(2)}, u32[]{:S(2)}) collective-permute-start(bf16[256,1024]{1,0:T(8,128)(2,1)S(1)} %get-tuple-element.302), channel_id=1, source_target_pairs={{0,1},{3,2},{4,5},{7,6},{8,9},{11,10},{12,13},{15,14},{16,17},{19,... | collective-permute-start | bytes 1572872 | tf_op jit(solution)/shard_map/ppermute | solution.py:937
  114.2 6.4 %collective-permute-start.14 = (bf16[1,80,1024]{2,1,0:T(8,128)(2,1)S(1)}, bf16[1,80,1024]{2,1,0:T(8,128)(2,1)S(1)}, u32[]{:S(2)}, u32[]{:S(2)}) collective-permute-start(bf16[1,80,1024]{2,1,0:T(8,128)(2,1)S(1)} %get-tuple-element.304), channel_id=1, source_target_pairs={{0,16},{4,20},{8,24},{12,28},{16,0},{20,4},{24,8},{28,12},{1,17},{... | collective-permute-start | bytes 491528 | tf_op jit(solution)/shard_map/ppermute | solution.py:804
  117.0 38.7 %collective-permute-start.27 = (bf16[256,1024]{1,0:T(8,128)(2,1)S(1)}, bf16[256,1024]{1,0:T(8,128)(2,1)S(1)}, u32[]{:S(2)}, u32[]{:S(2)}) collective-permute-start(bf16[256,1024]{1,0:T(8,128)(2,1)S(1)} %shard_map.266), channel_id=1, source_target_pairs={{0,1},{1,0},{2,3},{3,2},{4,5},{5,4},{6,7},{7,6},{8,9},{9,8},{10,11... | collective-permute-start | bytes 1572872 | tf_op jit(solution)/shard_map/ppermute | solution.py:937
  117.1 6.1 %collective-permute-start.15 = (bf16[1,80,1024]{2,1,0:T(8,128)(2,1)S(1)}, bf16[1,80,1024]{2,1,0:T(8,128)(2,1)S(1)}, u32[]{:S(2)}, u32[]{:S(2)}) collective-permute-start(bf16[1,80,1024]{2,1,0:T(8,128)(2,1)S(1)} %get-tuple-element.305), channel_id=1, source_target_pairs={{0,8},{4,12},{8,0},{12,4},{16,24},{20,28},{24,16},{28,20},{1,9},{5... | collective-permute-start | bytes 491528 | tf_op jit(solution)/shard_map/ppermute | solution.py:804
  120.6 6.4 %collective-permute-start.16 = (bf16[1,80,1024]{2,1,0:T(8,128)(2,1)S(1)}, bf16[1,80,1024]{2,1,0:T(8,128)(2,1)S(1)}, u32[]{:S(2)}, u32[]{:S(2)}) collective-permute-start(bf16[1,80,1024]{2,1,0:T(8,128)(2,1)S(1)} %get-tuple-element.306), channel_id=1, source_target_pairs={{0,24},{4,28},{8,16},{12,20},{16,8},{20,12},{24,0},{28,4},{1,25},{... | collective-permute-start | bytes 491528 | tf_op jit(solution)/shard_map/ppermute | solution.py:804
  127.1 12.1 %collective-permute-start.17 = (bf16[1,48,1024]{2,1,0:T(8,128)(2,1)S(1)}, bf16[1,48,1024]{2,1,0:T(8,128)(2,1)S(1)}, u32[]{:S(2)}, u32[]{:S(2)}) collective-permute-start(bf16[1,48,1024]{2,1,0:T(8,128)(2,1)S(1)} %get-tuple-element.318.left_ref), channel_id=1, source_target_pairs={{0,1},{1,0},{2,3},{3,2},{4,5},{5,4},{6,7},{7,6},{8,9},{9,8},{10,11... | collective-permute-start | bytes 294920 | tf_op jit(solution)/shard_map/ppermute | solution.py:811
  139.3 11.5 %collective-permute-start.23 = (bf16[1,64,1024]{2,1,0:T(8,128)(2,1)S(1)}, bf16[1,64,1024]{2,1,0:T(8,128)(2,1)S(1)}, u32[]{:S(2)}, u32[]{:S(2)}) collective-permute-start(bf16[1,64,1024]{2,1,0:T(8,128)(2,1)S(1)} %get-tuple-element.334), channel_id=1, source_target_pairs={{0,16},{4,20},{8,24},{12,28},{16,0},{20,4},{24,8},{28,12},{1,17},{... | collective-permute-start | bytes 393224 | tf_op jit(solution)/shard_map/ppermute | solution.py:804
  140.9 11.4 %collective-permute-start.24 = (bf16[1,64,1024]{2,1,0:T(8,128)(2,1)S(1)}, bf16[1,64,1024]{2,1,0:T(8,128)(2,1)S(1)}, u32[]{:S(2)}, u32[]{:S(2)}) collective-permute-start(bf16[1,64,1024]{2,1,0:T(8,128)(2,1)S(1)} %get-tuple-element.335), channel_id=1, source_target_pairs={{0,8},{4,12},{8,0},{12,4},{16,24},{20,28},{24,16},{28,20},{1,9},{5... | collective-permute-start | bytes 393224 | tf_op jit(solution)/shard_map/ppermute | solution.py:804
  142.4 10.4 %collective-permute-start.25 = (bf16[1,64,1024]{2,1,0:T(8,128)(2,1)S(1)}, bf16[1,64,1024]{2,1,0:T(8,128)(2,1)S(1)}, u32[]{:S(2)}, u32[]{:S(2)}) collective-permute-start(bf16[1,64,1024]{2,1,0:T(8,128)(2,1)S(1)} %get-tuple-element.336), channel_id=1, source_target_pairs={{0,24},{4,28},{8,16},{12,20},{16,8},{20,12},{24,0},{28,4},{1,25},{... | collective-permute-start | bytes 393224 | tf_op jit(solution)/shard_map/ppermute | solution.py:804
  142.8 6.3 %collective-permute-start.18 = (bf16[1,48,1024]{2,1,0:T(8,128)(2,1)S(1)}, bf16[1,48,1024]{2,1,0:T(8,128)(2,1)S(1)}, u32[]{:S(2)}, u32[]{:S(2)}) collective-permute-start(bf16[1,48,1024]{2,1,0:T(8,128)(2,1)S(1)} %shard_map.267.shared_ref), channel_id=1, source_target_pairs={{0,2},{1,3},{2,0},{3,1},{4,6},{5,7},{6,4},{7,5},{8,10},{9,11},{10,... | collective-permute-start | bytes 294920 | tf_op jit(solution)/shard_map/ppermute | solution.py:811
  149.2 10.1 %collective-permute-start.20 = (bf16[1,80,1024]{2,1,0:T(8,128)(2,1)S(1)}, bf16[1,80,1024]{2,1,0:T(8,128)(2,1)S(1)}, u32[]{:S(2)}, u32[]{:S(2)}) collective-permute-start(bf16[1,80,1024]{2,1,0:T(8,128)(2,1)S(1)} %shard_map.271.refs_0_.refs_5_), channel_id=1, source_target_pairs={{0,16},{4,20},{8,24},{12,28},{16,0},{20,4},{24,8},{28,12},{1,17},{... | collective-permute-start | bytes 491528 | tf_op jit(solution)/shard_map/ppermute | solution.py:804
  150.8 8.5 %collective-permute-start.21 = (bf16[1,80,1024]{2,1,0:T(8,128)(2,1)S(1)}, bf16[1,80,1024]{2,1,0:T(8,128)(2,1)S(1)}, u32[]{:S(2)}, u32[]{:S(2)}) collective-permute-start(bf16[1,80,1024]{2,1,0:T(8,128)(2,1)S(1)} %shard_map.271.refs_0_.refs_5_), channel_id=1, source_target_pairs={{0,8},{4,12},{8,0},{12,4},{16,24},{20,28},{24,16},{28,20},{1,9},{5... | collective-permute-start | bytes 491528 | tf_op jit(solution)/shard_map/ppermute | solution.py:804
  152.3 7.0 %collective-permute-start.22 = (bf16[1,80,1024]{2,1,0:T(8,128)(2,1)S(1)}, bf16[1,80,1024]{2,1,0:T(8,128)(2,1)S(1)}, u32[]{:S(2)}, u32[]{:S(2)}) collective-permute-start(bf16[1,80,1024]{2,1,0:T(8,128)(2,1)S(1)} %shard_map.271.refs_0_.refs_5_), channel_id=1, source_target_pairs={{0,24},{4,28},{8,16},{12,20},{16,8},{20,12},{24,0},{28,4},{1,25},{... | collective-permute-start | bytes 491528 | tf_op jit(solution)/shard_map/ppermute | solution.py:804
  152.8 5.7 %collective-permute-start.26 = (bf16[1,48,1024]{2,1,0:T(8,128)(2,1)S(1)}, bf16[1,48,1024]{2,1,0:T(8,128)(2,1)S(1)}, u32[]{:S(2)}, u32[]{:S(2)}) collective-permute-start(bf16[1,48,1024]{2,1,0:T(8,128)(2,1)S(1)} %get-tuple-element.340.left_ref), channel_id=1, source_target_pairs={{0,1},{1,0},{2,3},{3,2},{4,5},{5,4},{6,7},{7,6},{8,9},{9,8},{10,11... | collective-permute-start | bytes 294920 | tf_op jit(solution)/shard_map/ppermute | solution.py:811
  155.7 12.6 %collective-permute-start.11 = (bf16[256,1024]{1,0:T(8,128)(2,1)S(1)}, bf16[256,1024]{1,0:T(8,128)(2,1)S(1)}, u32[]{:S(2)}, u32[]{:S(2)}) collective-permute-start(bf16[256,1024]{1,0:T(8,128)(2,1)S(1)} %shard_map.262), channel_id=1, source_target_pairs={{0,1},{1,0},{2,3},{3,2},{4,5},{5,4},{6,7},{7,6},{8,9},{9,8},{10,11... | collective-permute-start | bytes 1572872 | tf_op jit(solution)/shard_map/ppermute | solution.py:937
  158.5 5.3 %collective-permute-start.13 = (bf16[256,1024]{1,0:T(8,128)(2,1)S(1)}, bf16[256,1024]{1,0:T(8,128)(2,1)S(1)}, u32[]{:S(2)}, u32[]{:S(2)}) collective-permute-start(bf16[256,1024]{1,0:T(8,128)(2,1)S(1)} %shard_map.263), channel_id=1, source_target_pairs={{1,2},{2,1},{5,6},{6,5},{9,10},{10,9},{13,14},{14,13},{17,18},{18,... | collective-permute-start | bytes 1572872 | tf_op jit(solution)/shard_map/ppermute | solution.py:937
  159.3 19.2 %collective-permute-start.34 = (bf16[4,80,1024]{2,1,0:T(8,128)(2,1)S(1)}, bf16[4,80,1024]{2,1,0:T(8,128)(2,1)S(1)}, u32[]{:S(2)}, u32[]{:S(2)}) collective-permute-start(bf16[4,80,1024]{2,1,0:T(8,128)(2,1)S(1)} %shard_map.276), channel_id=1, source_target_pairs={{0,4},{4,0},{8,12},{12,8},{16,20},{20,16},{24,28},{28,24},{1,5},{5... | collective-permute-start | bytes 1966088 | tf_op jit(solution)/shard_map/ppermute | solution.py:804
  159.4 15.5 %collective-permute-start.30 = (bf16[1,48,1024]{2,1,0:T(8,128)(2,1)S(1)}, bf16[1,48,1024]{2,1,0:T(8,128)(2,1)S(1)}, u32[]{:S(2)}, u32[]{:S(2)}) collective-permute-start(bf16[1,48,1024]{2,1,0:T(8,128)(2,1)S(1)} %shard_map.275.shared_ref), channel_id=1, source_target_pairs={{0,2},{1,3},{2,0},{3,1},{4,6},{5,7},{6,4},{7,5},{8,10},{9,11},{10,... | collective-permute-start | bytes 294920 | tf_op jit(solution)/shard_map/ppermute | solution.py:811
  178.1 5.9 %collective-permute-start.33 = (bf16[1,64,1024]{2,1,0:T(8,128)(2,1)S(1)}, bf16[1,64,1024]{2,1,0:T(8,128)(2,1)S(1)}, u32[]{:S(2)}, u32[]{:S(2)}) collective-permute-start(bf16[1,64,1024]{2,1,0:T(8,128)(2,1)S(1)} %shard_map.278.refs_0_.refs_5_), channel_id=1, source_target_pairs={{0,24},{4,28},{8,16},{12,20},{16,8},{20,12},{24,0},{28,4},{1,25},{... | collective-permute-start | bytes 393224 | tf_op jit(solution)/shard_map/ppermute | solution.py:804
  184.0 14.9 %collective-permute-start.28 = (bf16[256,1024]{1,0:T(8,128)(2,1)S(1)}, bf16[256,1024]{1,0:T(8,128)(2,1)S(1)}, u32[]{:S(2)}, u32[]{:S(2)}) collective-permute-start(bf16[256,1024]{1,0:T(8,128)(2,1)S(1)} %shard_map.270), channel_id=1, source_target_pairs={{0,1},{1,0},{2,3},{3,2},{4,5},{5,4},{6,7},{7,6},{8,9},{9,8},{10,11... | collective-permute-start | bytes 1572872 | tf_op jit(solution)/shard_map/ppermute | solution.py:937
  184.6 25.0 %collective-permute-start.29 = (bf16[256,1024]{1,0:T(8,128)(2,1)S(1)}, bf16[256,1024]{1,0:T(8,128)(2,1)S(1)}, u32[]{:S(2)}, u32[]{:S(2)}) collective-permute-start(bf16[256,1024]{1,0:T(8,128)(2,1)S(1)} %shard_map.274), channel_id=1, source_target_pairs={{0,3},{1,2},{2,1},{3,0},{4,7},{5,6},{6,5},{7,4},{8,11},{9,10},{10,... | collective-permute-start | bytes 1572872 | tf_op jit(solution)/shard_map/ppermute | solution.py:937
  (30 other events, 73.3 us)

commit v3 on v2

--- a/solution.py
+++ b/solution.py
@@ -753,6 +753,15 @@
     both_ref[:, rows:] = split_ref[...]
 
 
+def close_all_kernel(own_ref, near_ref, second_ref, third_ref, split_ref, both_ref):
+    rows = own_ref.shape[1]
+    own, near, second, third = (
+        ref[...].astype(F32) for ref in (own_ref, near_ref, second_ref, third_ref)
+    )
+    both_ref[:, :rows] = ((own + near) + (second + third)).astype(BF)
+    both_ref[:, rows:] = split_ref[...]
+
+
 def join_kernel(*refs):
     low = 0
     for ref in refs[:-1]:
@@ -793,9 +802,11 @@
         halves = self.bits - 2
         self.steps = [("down", b) for b in range(halves)] + [("meet", 0)]
         jump = 1
-        while jump < self.n:
+        while jump < self.n and self.n != 4:
             self.steps.append(("across", jump))
             jump *= 2
+        if self.n == 4:
+            self.steps.append(("all", 0))
         self.steps += [("part", 0)] + [("back", b) for b in reversed(range(halves))]
         self.moving, self.at, self.results = None, 0, []
 
@@ -809,6 +820,11 @@
         if kind == "across":
             pairs = [(k, k ^ which) for k in range(self.n)]
             self.moving = lax.ppermute(self.shared, "tensor", pairs)
+        elif kind == "all":
+            self.moving = [
+                lax.ppermute(self.shared, "tensor", [(k, k ^ jump) for k in range(4)])
+                for jump in (1, 2, 3)
+            ]
         elif kind == "down":
             self.moving = self.hop(self.parts[which], 1 << which)
         elif kind == "meet":
@@ -840,6 +856,13 @@
                 [((1, self.n_shared, width), BF), ((1, rows - self.n_shared, width), BF)],
             )
             value = self.shared
+        elif kind == "all":
+            (self.have,) = call(
+                close_all_kernel,
+                [self.shared, *arrived, self.split],
+                [(self.parts[-1].shape, BF)],
+            )
+            value = self.have
         elif kind == "across":
             if self.steps[self.at + 1][0] == "part":
                 (self.have,) = call(
@@ -1147,23 +1170,19 @@
         late = late_parts()
         late.start()
         dx_far = in_part(3, BF)
-        last = early.finish(dx_far)
-        early.start()
         dx_swap = send(dx_far, swap)
-        last = late.finish(last)
+        last = late.finish(dx_far)
         late.start()
         dx_near = in_part(1, BF, last=last)
         last = early.finish(dx_near)
         early.start()
         last = late.finish(last)
         late.start()
-        dx_own = in_part(0, F32, last=last)
-        dx_facing = in_part(2, BF, after(dx_swap, dx_own))
-        last = late.finish(dx_facing)
-        late.start()
+        dx_facing = in_part(2, BF, after(dx_swap, last))
+        dx_own = in_part(0, F32, last=dx_facing)
         dx_a = send(dx_near, swap)
         dx_b = send(dx_facing, mirror)
-        last = early.finish(last)
+        last = early.finish(dx_own)
         early.start()
         (layer_output,) = call(
             output_kernel,

time: 212 us -> 214 us (level)
  starting transfers between devices: 58 us -> 62.5 us
  waiting for transfers between devices: 68.8 us -> 66.5 us
    ppermute x16, waiting for transfers between devices: 39.1 us -> 34.6 us  [send(): return lax.ppermute(value, 'tensor', pairs)]
    ppermute x16, starting transfers between devices: 30.9 us -> 35 us  [send(): return lax.ppermute(value, 'tensor', pairs)]
    ppermute x16, waiting for transfers between devices: 9.61 us -> 13.4 us  [hop(): return lax.ppermute(value, 'dp', pairs)]
    ppermute x4 -> x6, starting transfers between devices: 10.1 us -> 8.37 us  [start(): lax.ppermute(self.shared, 'tensor', [(k, k ^ jump) for k in range(4)])]
    ppermute x4 -> x6, waiting for transfers between devices: 20.1 us -> 18.6 us  [start(): lax.ppermute(self.shared, 'tensor', [(k, k ^ jump) for k in range(4)])]
    pallas_call x42 -> x40, Pallas kernels: 65.1 us -> 65.1 us  [call(): pl.pallas_call(kernel, in_specs=[pl.BlockSpec(memory_space=space) for spa...]
  transfers between devices with their start and end apart: 36 -> 38, of which waited for: 14 -> 14; matrix products, arithmetic and copies ran while one was open for 0% -> 0% of each run, Pallas kernels for 27% -> 27%
where the time goes in v3:
time: 214 us
  Pallas kernels  68 us (32%)
  waiting for transfers between devices  66.5 us (31%)
  starting transfers between devices  62.5 us (29%)
  local copies, waits for them, and re-layouts  15.4 us (7%)
    pallas_call x40, Pallas kernels, call(): pl.pallas_call(kernel, in_specs=[pl.BlockSpec(memory_space=space) for spa...  65.1 us
    ppermute x16, starting transfers between devices, send(): return lax.ppermute(value, 'tensor', pairs)  35 us
    ppermute x16, waiting for transfers between devices, send(): return lax.ppermute(value, 'tensor', pairs)  34.6 us
    ppermute x16, starting transfers between devices, hop(): return lax.ppermute(value, 'dp', pairs)  19.1 us
    ppermute x6, waiting for transfers between devices, start(): lax.ppermute(self.shared, 'tensor', [(k, k ^ jump) for k in range(4)])  18.6 us
    unnamed x52, local copies, waits for them, and re-layouts  15.4 us
    ppermute x16, waiting for transfers between devices, hop(): return lax.ppermute(value, 'dp', pairs)  13.4 us
    ppermute x6, starting transfers between devices, start(): lax.ppermute(self.shared, 'tensor', [(k, k ^ jump) for k in range(4)])  8.37 us
  transfers between devices with their start and end apart: 38, of which 14 were waited for; matrix products, arithmetic and copies ran while one was open for 0% of the time, Pallas kernels for 27%

profile of v3, /device:TPU:0, one launch (start us, length us, event | category | flops | bytes accessed | tf_op | source)
XLA Modules:
  0.0 213.6 jit_solution(9086183447038578025)
XLA Ops:
  0.7 3.1 %collective-permute-start = (bf16[256,1024]{1,0:T(8,128)(2,1)}, bf16[256,1024]{1,0:T(8,128)(2,1)S(1)}, u32[]{:S(2)}, u32[]{:S(2)}) collective-permute-start(bf16[256,1024]{1,0:T(8,128)(2,1)} %bitcast.11), channel_id=1, source_target_pairs={{0,1},{1,0},{2,3},{3,2},{4,5},{5,4},{6,7},{7,6},{8,9},{9,8},{10,11... | collective-permute-start | bytes 1572872 | tf_op jit(solution)/shard_map/ppermute | solution.py:960
  3.8 2.5 %collective-permute-start.1 = (bf16[256,1024]{1,0:T(8,128)(2,1)}, bf16[256,1024]{1,0:T(8,128)(2,1)S(1)}, u32[]{:S(2)}, u32[]{:S(2)}) collective-permute-start(bf16[256,1024]{1,0:T(8,128)(2,1)} %bitcast.12), channel_id=1, source_target_pairs={{0,3},{1,2},{2,1},{3,0},{4,7},{5,6},{6,5},{7,4},{8,11},{9,10},{10,... | collective-permute-start | bytes 1572872 | tf_op jit(solution)/shard_map/ppermute | solution.py:960
  22.3 2.8 %shard_map.242 = (bf16[1024,768]{1,0:T(8,128)(2,1)S(1)}, bf16[1024,1024]{1,0:T(8,128)(2,1)S(1)}, bf16[256,1024]{1,0:T(8,128)(2,1)S(1)}, bf16[1024,1024]{1,0:T(8,128)(2,1)S(1)}) custom-call(bf16[3,1024,256]{2,1,0:T(8,128)(2,1)S(1)} %copy-done.2, bf16[3,1024,128]{2,1,0:T(8,128)(2,1)S(1)} %copy-done.4, bf16[3,128,256]{2,1,0:T(8,128)(2,1)S(1)} %copy-done.7, ...), custom_call_target="tpu_custom_call" | custom-call | flops 805306368 | bytes 12582912 | tf_op jit(solution)/shard_map/pallas_call | solution.py:140
  25.2 4.3 %shard_map.241 = (bf16[3,4,64,256]{3,2,1,0:T(8,128)(2,1)S(1)}, bf16[256,512]{1,0:T(8,128)(2,1)S(1)}, bf16[256,1024]{1,0:T(8,128)(2,1)S(1)}, bf16[256,1024]{1,0:T(8,128)(2,1)S(1)}, bf16[256,1024]{1,0:T(8,128)(2,1)S(1)}) custom-call(bf16[256,1024]{1,0:T(8,128)(2,1)S(1)} %bitcast.13, f32[1,1024]{1,0:T(1,128)S(1)} %bitcast.29, f32[1,1024]{1,0:T(1,128)S(1)} %bitcast.22, ...), custom_call_target="tpu_custom_call" | custom-call | flops 1207959552 | bytes 4456448 | tf_op jit(solution)/shard_map/pallas_call | solution.py:33
  32.3 4.3 %shard_map.244 = (bf16[3,4,64,256]{3,2,1,0:T(8,128)(2,1)S(1)}, bf16[256,512]{1,0:T(8,128)(2,1)S(1)}, bf16[256,1024]{1,0:T(8,128)(2,1)S(1)}, bf16[256,1024]{1,0:T(8,128)(2,1)S(1)}, bf16[256,1024]{1,0:T(8,128)(2,1)S(1)}) custom-call(bf16[256,1024]{1,0:T(8,128)(2,1)S(1)} %collective-permute-done.1.x_ref, f32[1,1024]{1,0:T(1,128)S(1)} %bitcast.30, ...), custom_call_target="tpu_custom_call" | custom-call | flops 1207959552 | bytes 4456448 | tf_op jit(solution)/shard_map/pallas_call | solution.py:33
  36.6 4.3 %shard_map.243 = (bf16[3,4,64,256]{3,2,1,0:T(8,128)(2,1)S(1)}, bf16[256,512]{1,0:T(8,128)(2,1)S(1)}, bf16[256,1024]{1,0:T(8,128)(2,1)S(1)}, bf16[256,1024]{1,0:T(8,128)(2,1)S(1)}, bf16[256,1024]{1,0:T(8,128)(2,1)S(1)}) custom-call(bf16[256,1024]{1,0:T(8,128)(2,1)S(1)} %collective-permute-done.x_ref, f32[1,1024]{1,0:T(1,128)S(1)} %bitcast.31, ...), custom_call_target="tpu_custom_call" | custom-call | flops 1207959552 | bytes 4456448 | tf_op jit(solution)/shard_map/pallas_call | solution.py:33
  40.8 3.5 %collective-permute-done.2.x_ref = bf16[256,1024]{1,0:T(8,128)(2,1)S(1)} collective-permute-done((bf16[256,1024]{1,0:T(8,128)(2,1)S(1)}, bf16[256,1024]{1,0:T(8,128)(2,1)S(1)}, u32[]{:S(2)}, u32[]{:S(2)}) %collective-permute-start.2) | collective-permute-done | bytes 524320 | tf_op jit(solution)/shard_map/ppermute | solution.py:960
  44.4 4.3 %shard_map.245 = (bf16[3,4,64,256]{3,2,1,0:T(8,128)(2,1)S(1)}, bf16[256,512]{1,0:T(8,128)(2,1)S(1)}, bf16[256,1024]{1,0:T(8,128)(2,1)S(1)}, bf16[256,1024]{1,0:T(8,128)(2,1)S(1)}, bf16[256,1024]{1,0:T(8,128)(2,1)S(1)}) custom-call(bf16[256,1024]{1,0:T(8,128)(2,1)S(1)} %collective-permute-done.2.x_ref, f32[1,1024]{1,0:T(1,128)S(1)} %bitcast.32, ...), custom_call_target="tpu_custom_call" | custom-call | flops 1207959552 | bytes 4456448 | tf_op jit(solution)/shard_map/pallas_call | solution.py:33
  48.6 7.2 %shard_map.246 = (bf16[4,64,256]{2,1,0:T(8,128)(2,1)S(1)}, bf16[4,64,256]{2,1,0:T(8,128)(2,1)S(1)}, bf16[4,64,256]{2,1,0:T(8,128)(2,1)S(1)}, bf16[4,64,256]{2,1,0:T(8,128)(2,1)S(1)}, f32[4,1,1024]{2,1,0:T(1,128)S(1)}) custom-call(s32[4]{0:T(128)S(1)} %pad_add_fusion.places_ref.refs_0_, s32[1,1024]{1,0:T(1,128)S(1)} %get-tuple-element.192.refs_1_, ...), custom_call_target="tpu_custom_call" | custom-call | flops 2147483648 | bytes 1081344 | tf_op jit(solution)/shard_map/pallas_call | solution.py:33
  60.7 9.2 %collective-permute-done.6.right_ref = bf16[256,1024]{1,0:T(8,128)(2,1)S(1)} collective-permute-done((bf16[256,1024]{1,0:T(8,128)(2,1)S(1)}, bf16[256,1024]{1,0:T(8,128)(2,1)S(1)}, u32[]{:S(2)}, u32[]{:S(2)}) %collective-permute-start.6) | collective-permute-done | bytes 524320 | tf_op jit(solution)/shard_map/ppermute | solution.py:960
  72.9 4.6 %collective-permute-start.7 = (bf16[256,1024]{1,0:T(8,128)(2,1)S(1)}, bf16[256,1024]{1,0:T(8,128)(2,1)S(1)}, u32[]{:S(2)}, u32[]{:S(2)}) collective-permute-start(bf16[256,1024]{1,0:T(8,128)(2,1)S(1)} %get-tuple-element.256), channel_id=1, source_target_pairs={{0,1},{3,2},{4,5},{7,6},{8,9},{11,10},{12,13},{15,14},{16,17},{19,... | collective-permute-start | bytes 1572872 | tf_op jit(solution)/shard_map/ppermute | solution.py:960
  82.0 2.2 %shard_map.256 = (f32[384,1024]{1,0:T(8,128)S(1)}, f32[256,1024]{1,0:T(8,128)S(1)}, f32[128,256]{1,0:T(8,128)S(1)}) custom-call(s32[1]{0:T(128)} %bitcast.4.refs_0_, bf16[128,1024]{1,0:T(8,128)(2,1)S(1)} %copy-done.6, f32[1,1024]{1,0:T(1,128)S(1)} %bitcast.26, bf16[256,1024]{1,0:T(8,128)(2,1)S(1)} %bitcast.19, ...), custom_call_target="tpu_custom_call" | custom-call | flops 1207959552 | bytes 5505024 | tf_op jit(solution)/shard_map/pallas_call | solution.py:33
  87.8 5.9 %shard_map.260 = (bf16[3,2,64,256]{3,2,1,0:T(8,128)(2,1)S(1)}, bf16[3,2,64,256]{3,2,1,0:T(8,128)(2,1)S(1)}, bf16[3,2,64,256]{3,2,1,0:T(8,128)(2,1)S(1)}, bf16[3,2,64,256]{3,2,1,0:T(8,128)(2,1)S(1)}) custom-call(s32[4]{0:T(128)S(1)} %pad_add_fusion.places_ref.refs_0_, s32[1,1024]{1,0:T(1,128)S(1)} %get-tuple-element.192.refs_1_, ...), custom_call_target="tpu_custom_call" | custom-call | flops 2684354560 | bytes 1572864 | tf_op jit(solution)/shard_map/pallas_call | solution.py:33
  94.0 5.9 %shard_map.264 = (bf16[3,2,64,256]{3,2,1,0:T(8,128)(2,1)S(1)}, bf16[3,2,64,256]{3,2,1,0:T(8,128)(2,1)S(1)}, bf16[3,2,64,256]{3,2,1,0:T(8,128)(2,1)S(1)}, bf16[3,2,64,256]{3,2,1,0:T(8,128)(2,1)S(1)}) custom-call(s32[4]{0:T(128)S(1)} %pad_add_fusion.places_ref.refs_0_, s32[1,1024]{1,0:T(1,128)S(1)} %get-tuple-element.192.refs_1_, ...), custom_call_target="tpu_custom_call" | custom-call | flops 2684354560 | bytes 1572864 | tf_op jit(solution)/shard_map/pallas_call | solution.py:33
  99.9 3.5 %shard_map.266 = (bf16[4,64,1024]{2,1,0:T(8,128)(2,1)S(1)}, bf16[1,64,1024]{2,1,0:T(8,128)(2,1)S(1)}, bf16[1,64,1024]{2,1,0:T(8,128)(2,1)S(1)}, bf16[1,64,1024]{2,1,0:T(8,128)(2,1)S(1)}, bf16[1,64,1024]{2,1,0:T(8,128)(2,1)S(1)}) custom-call(s32[1]{0:T(128)} %bitcast.4.refs_0_, bf16[3,128,256]{2,1,0:T(8,128)(2,1)S(1)} %copy-done.8, f32[1,1024]{1,0:T(1,128)S(1)} %bitcast.33, ...), custom_call_target="tpu_custom_call" | custom-call | flops 1207959552 | bytes 2097152 | tf_op jit(solution)/shard_map/pallas_call | solution.py:33
  103.9 10.0 %collective-permute-start.12 = (bf16[256,1024]{1,0:T(8,128)(2,1)S(1)}, bf16[256,1024]{1,0:T(8,128)(2,1)S(1)}, u32[]{:S(2)}, u32[]{:S(2)}) collective-permute-start(bf16[256,1024]{1,0:T(8,128)(2,1)S(1)} %get-tuple-element.304), channel_id=1, source_target_pairs={{0,1},{3,2},{4,5},{7,6},{8,9},{11,10},{12,13},{15,14},{16,17},{19,... | collective-permute-start | bytes 1572872 | tf_op jit(solution)/shard_map/ppermute | solution.py:960
  118.4 2.0 collective-permute-done.14.refs_1_
  120.3 2.5 %collective-permute-start.16 = (bf16[1,80,1024]{2,1,0:T(8,128)(2,1)S(1)}, bf16[1,80,1024]{2,1,0:T(8,128)(2,1)S(1)}, u32[]{:S(2)}, u32[]{:S(2)}) collective-permute-start(bf16[1,80,1024]{2,1,0:T(8,128)(2,1)S(1)} %get-tuple-element.308), channel_id=1, source_target_pairs={{0,24},{4,28},{8,16},{12,20},{16,8},{20,12},{24,0},{28,4},{1,25},{... | collective-permute-start | bytes 491528 | tf_op jit(solution)/shard_map/ppermute | solution.py:815
  122.9 3.8 %collective-permute-done.16.refs_3_ = bf16[1,80,1024]{2,1,0:T(8,128)(2,1)S(1)} collective-permute-done((bf16[1,80,1024]{2,1,0:T(8,128)(2,1)S(1)}, bf16[1,80,1024]{2,1,0:T(8,128)(2,1)S(1)}, u32[]{:S(2)}, u32[]{:S(2)}) %collective-permute-start.16) | collective-permute-done | bytes 163872 | tf_op jit(solution)/shard_map/ppermute | solution.py:815
  132.1 7.5 %collective-permute-done.17.near_ref = bf16[1,48,1024]{2,1,0:T(8,128)(2,1)S(1)} collective-permute-done((bf16[1,48,1024]{2,1,0:T(8,128)(2,1)S(1)}, bf16[1,48,1024]{2,1,0:T(8,128)(2,1)S(1)}, u32[]{:S(2)}, u32[]{:S(2)}) %collective-permute-start.17) | collective-permute-done | bytes 98336 | tf_op jit(solution)/shard_map/ppermute | solution.py:825
  139.6 2.5 %collective-permute-start.27 = (bf16[1,64,1024]{2,1,0:T(8,128)(2,1)S(1)}, bf16[1,64,1024]{2,1,0:T(8,128)(2,1)S(1)}, u32[]{:S(2)}, u32[]{:S(2)}) collective-permute-start(bf16[1,64,1024]{2,1,0:T(8,128)(2,1)S(1)} %get-tuple-element.339), channel_id=1, source_target_pairs={{0,24},{4,28},{8,16},{12,20},{16,8},{20,12},{24,0},{28,4},{1,25},{... | collective-permute-start | bytes 393224 | tf_op jit(solution)/shard_map/ppermute | solution.py:815
  144.8 3.8 %collective-permute-done.19.third_ref = bf16[1,48,1024]{2,1,0:T(8,128)(2,1)S(1)} collective-permute-done((bf16[1,48,1024]{2,1,0:T(8,128)(2,1)S(1)}, bf16[1,48,1024]{2,1,0:T(8,128)(2,1)S(1)}, u32[]{:S(2)}, u32[]{:S(2)}) %collective-permute-start.19) | collective-permute-done | bytes 98336 | tf_op jit(solution)/shard_map/ppermute | solution.py:825
  157.2 2.5 %collective-permute-done.22.refs_2_.refs_3_ = bf16[1,80,1024]{2,1,0:T(8,128)(2,1)S(1)} collective-permute-done((bf16[1,80,1024]{2,1,0:T(8,128)(2,1)S(1)}, bf16[1,80,1024]{2,1,0:T(8,128)(2,1)S(1)}, u32[]{:S(2)}, u32[]{:S(2)}) %collective-permute-start.22) | collective-permute-done | bytes 163872 | tf_op jit(solution)/shard_map/ppermute | solution.py:815
  159.7 1.8 collective-permute-done.23.refs_3_.refs_2_
  161.6 2.4 %collective-permute-start.30 = (bf16[1,48,1024]{2,1,0:T(8,128)(2,1)S(1)}, bf16[1,48,1024]{2,1,0:T(8,128)(2,1)S(1)}, u32[]{:S(2)}, u32[]{:S(2)}) collective-permute-start(bf16[1,48,1024]{2,1,0:T(8,128)(2,1)S(1)} %get-tuple-element.343.own_ref), channel_id=1, source_target_pairs={{0,1},{1,0},{2,3},{3,2},{4,5},{5,4},{6,7},{7,6},{8,9},{9,8},{10,11... | collective-permute-start | bytes 294920 | tf_op jit(solution)/shard_map/ppermute | solution.py:825
  167.4 7.3 %collective-permute-done.31.second_ref = bf16[1,48,1024]{2,1,0:T(8,128)(2,1)S(1)} collective-permute-done((bf16[1,48,1024]{2,1,0:T(8,128)(2,1)S(1)}, bf16[1,48,1024]{2,1,0:T(8,128)(2,1)S(1)}, u32[]{:S(2)}, u32[]{:S(2)}) %collective-permute-start.31) | collective-permute-done | bytes 98336 | tf_op jit(solution)/shard_map/ppermute | solution.py:825
  181.2 2.0 collective-permute-done.35.refs_3_.refs_2_
  183.3 2.5 %collective-permute-start.28 = (bf16[256,1024]{1,0:T(8,128)(2,1)S(1)}, bf16[256,1024]{1,0:T(8,128)(2,1)S(1)}, u32[]{:S(2)}, u32[]{:S(2)}) collective-permute-start(bf16[256,1024]{1,0:T(8,128)(2,1)S(1)} %shard_map.269), channel_id=1, source_target_pairs={{0,1},{1,0},{2,3},{3,2},{4,5},{5,4},{6,7},{7,6},{8,9},{9,8},{10,11... | collective-permute-start | bytes 1572872 | tf_op jit(solution)/shard_map/ppermute | solution.py:960
  185.8 2.6 %collective-permute-start.29 = (bf16[256,1024]{1,0:T(8,128)(2,1)S(1)}, bf16[256,1024]{1,0:T(8,128)(2,1)S(1)}, u32[]{:S(2)}, u32[]{:S(2)}) collective-permute-start(bf16[256,1024]{1,0:T(8,128)(2,1)S(1)} %shard_map.272), channel_id=1, source_target_pairs={{0,3},{1,2},{2,1},{3,0},{4,7},{5,6},{6,5},{7,4},{8,11},{9,10},{10,... | collective-permute-start | bytes 1572872 | tf_op jit(solution)/shard_map/ppermute | solution.py:960
  190.0 8.3 %collective-permute-done.28.rest_0_ = bf16[256,1024]{1,0:T(8,128)(2,1)S(1)} collective-permute-done((bf16[256,1024]{1,0:T(8,128)(2,1)S(1)}, bf16[256,1024]{1,0:T(8,128)(2,1)S(1)}, u32[]{:S(2)}, u32[]{:S(2)}) %collective-permute-start.28) | collective-permute-done | bytes 524320 | tf_op jit(solution)/shard_map/ppermute | solution.py:960
  198.3 13.5 %collective-permute-done.29.rest_1_ = bf16[256,1024]{1,0:T(8,128)(2,1)S(1)} collective-permute-done((bf16[256,1024]{1,0:T(8,128)(2,1)S(1)}, bf16[256,1024]{1,0:T(8,128)(2,1)S(1)}, u32[]{:S(2)}, u32[]{:S(2)}) %collective-permute-start.29) | collective-permute-done | bytes 524320 | tf_op jit(solution)/shard_map/ppermute | solution.py:960
  211.9 1.7 shard_map.280
  (138 shorter events, 68.4 us)
Async XLA Ops:
  0.7 28.8 %collective-permute-start = (bf16[256,1024]{1,0:T(8,128)(2,1)}, bf16[256,1024]{1,0:T(8,128)(2,1)S(1)}, u32[]{:S(2)}, u32[]{:S(2)}) collective-permute-start(bf16[256,1024]{1,0:T(8,128)(2,1)} %bitcast.11), channel_id=1, source_target_pairs={{0,1},{1,0},{2,3},{3,2},{4,5},{5,4},{6,7},{7,6},{8,9},{9,8},{10,11... | collective-permute-start | bytes 1572872 | tf_op jit(solution)/shard_map/ppermute | solution.py:960
  3.8 25.7 %collective-permute-start.1 = (bf16[256,1024]{1,0:T(8,128)(2,1)}, bf16[256,1024]{1,0:T(8,128)(2,1)S(1)}, u32[]{:S(2)}, u32[]{:S(2)}) collective-permute-start(bf16[256,1024]{1,0:T(8,128)(2,1)} %bitcast.12), channel_id=1, source_target_pairs={{0,3},{1,2},{2,1},{3,0},{4,7},{5,6},{6,5},{7,4},{8,11},{9,10},{10,... | collective-permute-start | bytes 1572872 | tf_op jit(solution)/shard_map/ppermute | solution.py:960
  29.5 14.9 %collective-permute-start.2 = (bf16[256,1024]{1,0:T(8,128)(2,1)S(1)}, bf16[256,1024]{1,0:T(8,128)(2,1)S(1)}, u32[]{:S(2)}, u32[]{:S(2)}) collective-permute-start(bf16[256,1024]{1,0:T(8,128)(2,1)S(1)} %collective-permute-done.1.x_ref), channel_id=1, source_target_pairs={{0,1},{1,0},{2,3},{3,2},{4,5},{5,4},{6,7},{7,6},{8,9},{9,8},{10,11... | collective-permute-start | bytes 1572872 | tf_op jit(solution)/shard_map/ppermute | solution.py:960
  30.3 25.6 %collective-permute-start.3 = (bf16[256,1024]{1,0:T(8,128)(2,1)S(1)}, bf16[256,1024]{1,0:T(8,128)(2,1)S(1)}, u32[]{:S(2)}, u32[]{:S(2)}) collective-permute-start(bf16[256,1024]{1,0:T(8,128)(2,1)S(1)} %bitcast.16), channel_id=1, source_target_pairs={{0,1},{1,0},{2,3},{3,2},{4,5},{5,4},{6,7},{7,6},{8,9},{9,8},{10,11... | collective-permute-start | bytes 1572872 | tf_op jit(solution)/shard_map/ppermute | solution.py:960
  31.6 24.3 %collective-permute-start.4 = (bf16[256,1024]{1,0:T(8,128)(2,1)S(1)}, bf16[256,1024]{1,0:T(8,128)(2,1)S(1)}, u32[]{:S(2)}, u32[]{:S(2)}) collective-permute-start(bf16[256,1024]{1,0:T(8,128)(2,1)S(1)} %bitcast.17), channel_id=1, source_target_pairs={{1,2},{2,1},{5,6},{6,5},{9,10},{10,9},{13,14},{14,13},{17,18},{18,... | collective-permute-start | bytes 1572872 | tf_op jit(solution)/shard_map/ppermute | solution.py:960
  56.7 13.2 %collective-permute-start.6 = (bf16[256,1024]{1,0:T(8,128)(2,1)S(1)}, bf16[256,1024]{1,0:T(8,128)(2,1)S(1)}, u32[]{:S(2)}, u32[]{:S(2)}) collective-permute-start(bf16[256,1024]{1,0:T(8,128)(2,1)S(1)} %collective-permute-done.4.left_ref), channel_id=1, source_target_pairs={{1,0},{2,3},{5,4},{6,7},{9,8},{10,11},{13,12},{14,15},{17,16},{18,... | collective-permute-start | bytes 1572872 | tf_op jit(solution)/shard_map/ppermute | solution.py:960
  69.9 14.4 %collective-permute-start.9 = (bf16[256,1024]{1,0:T(8,128)(2,1)S(1)}, bf16[256,1024]{1,0:T(8,128)(2,1)S(1)}, u32[]{:S(2)}, u32[]{:S(2)}) collective-permute-start(bf16[256,1024]{1,0:T(8,128)(2,1)S(1)} %collective-permute-done.5.left_ref), channel_id=1, source_target_pairs={{1,0},{2,3},{5,4},{6,7},{9,8},{10,11},{13,12},{14,15},{17,16},{18,... | collective-permute-start | bytes 1572872 | tf_op jit(solution)/shard_map/ppermute | solution.py:960
  72.9 13.8 %collective-permute-start.7 = (bf16[256,1024]{1,0:T(8,128)(2,1)S(1)}, bf16[256,1024]{1,0:T(8,128)(2,1)S(1)}, u32[]{:S(2)}, u32[]{:S(2)}) collective-permute-start(bf16[256,1024]{1,0:T(8,128)(2,1)S(1)} %get-tuple-element.256), channel_id=1, source_target_pairs={{0,1},{3,2},{4,5},{7,6},{8,9},{11,10},{12,13},{15,14},{16,17},{19,... | collective-permute-start | bytes 1572872 | tf_op jit(solution)/shard_map/ppermute | solution.py:960
  86.7 7.0 %collective-permute-start.10 = (bf16[4,80,1024]{2,1,0:T(8,128)(2,1)S(1)}, bf16[4,80,1024]{2,1,0:T(8,128)(2,1)S(1)}, u32[]{:S(2)}, u32[]{:S(2)}) collective-permute-start(bf16[4,80,1024]{2,1,0:T(8,128)(2,1)S(1)} %get-tuple-element.287), channel_id=1, source_target_pairs={{0,4},{4,0},{8,12},{12,8},{16,20},{20,16},{24,28},{28,24},{1,5},{5... | collective-permute-start | bytes 1966088 | tf_op jit(solution)/shard_map/ppermute | solution.py:815
  86.9 7.0 %collective-permute-start.8 = (bf16[256,1024]{1,0:T(8,128)(2,1)S(1)}, bf16[256,1024]{1,0:T(8,128)(2,1)S(1)}, u32[]{:S(2)}, u32[]{:S(2)}) collective-permute-start(bf16[256,1024]{1,0:T(8,128)(2,1)S(1)} %shard_map.255), channel_id=1, source_target_pairs={{1,2},{2,1},{5,6},{6,5},{9,10},{10,9},{13,14},{14,13},{17,18},{18,... | collective-permute-start | bytes 1572872 | tf_op jit(solution)/shard_map/ppermute | solution.py:960
  103.4 25.5 %collective-permute-start.20 = (bf16[4,64,1024]{2,1,0:T(8,128)(2,1)S(1)}, bf16[4,64,1024]{2,1,0:T(8,128)(2,1)S(1)}, u32[]{:S(2)}, u32[]{:S(2)}) collective-permute-start(bf16[4,64,1024]{2,1,0:T(8,128)(2,1)S(1)} %get-tuple-element.322), channel_id=1, source_target_pairs={{0,4},{4,0},{8,12},{12,8},{16,20},{20,16},{24,28},{28,24},{1,5},{5... | collective-permute-start | bytes 1572872 | tf_op jit(solution)/shard_map/ppermute | solution.py:815
  103.9 26.7 %collective-permute-start.12 = (bf16[256,1024]{1,0:T(8,128)(2,1)S(1)}, bf16[256,1024]{1,0:T(8,128)(2,1)S(1)}, u32[]{:S(2)}, u32[]{:S(2)}) collective-permute-start(bf16[256,1024]{1,0:T(8,128)(2,1)S(1)} %get-tuple-element.304), channel_id=1, source_target_pairs={{0,1},{3,2},{4,5},{7,6},{8,9},{11,10},{12,13},{15,14},{16,17},{19,... | collective-permute-start | bytes 1572872 | tf_op jit(solution)/shard_map/ppermute | solution.py:960
  114.0 6.4 %collective-permute-start.14 = (bf16[1,80,1024]{2,1,0:T(8,128)(2,1)S(1)}, bf16[1,80,1024]{2,1,0:T(8,128)(2,1)S(1)}, u32[]{:S(2)}, u32[]{:S(2)}) collective-permute-start(bf16[1,80,1024]{2,1,0:T(8,128)(2,1)S(1)} %get-tuple-element.306), channel_id=1, source_target_pairs={{0,16},{4,20},{8,24},{12,28},{16,0},{20,4},{24,8},{28,12},{1,17},{... | collective-permute-start | bytes 491528 | tf_op jit(solution)/shard_map/ppermute | solution.py:815
  116.7 37.5 %collective-permute-start.24 = (bf16[256,1024]{1,0:T(8,128)(2,1)S(1)}, bf16[256,1024]{1,0:T(8,128)(2,1)S(1)}, u32[]{:S(2)}, u32[]{:S(2)}) collective-permute-start(bf16[256,1024]{1,0:T(8,128)(2,1)S(1)} %shard_map.267), channel_id=1, source_target_pairs={{0,1},{1,0},{2,3},{3,2},{4,5},{5,4},{6,7},{7,6},{8,9},{9,8},{10,11... | collective-permute-start | bytes 1572872 | tf_op jit(solution)/shard_map/ppermute | solution.py:960
  116.8 6.1 %collective-permute-start.15 = (bf16[1,80,1024]{2,1,0:T(8,128)(2,1)S(1)}, bf16[1,80,1024]{2,1,0:T(8,128)(2,1)S(1)}, u32[]{:S(2)}, u32[]{:S(2)}) collective-permute-start(bf16[1,80,1024]{2,1,0:T(8,128)(2,1)S(1)} %get-tuple-element.307), channel_id=1, source_target_pairs={{0,8},{4,12},{8,0},{12,4},{16,24},{20,28},{24,16},{28,20},{1,9},{5... | collective-permute-start | bytes 491528 | tf_op jit(solution)/shard_map/ppermute | solution.py:815
  120.3 6.4 %collective-permute-start.16 = (bf16[1,80,1024]{2,1,0:T(8,128)(2,1)S(1)}, bf16[1,80,1024]{2,1,0:T(8,128)(2,1)S(1)}, u32[]{:S(2)}, u32[]{:S(2)}) collective-permute-start(bf16[1,80,1024]{2,1,0:T(8,128)(2,1)S(1)} %get-tuple-element.308), channel_id=1, source_target_pairs={{0,24},{4,28},{8,16},{12,20},{16,8},{20,12},{24,0},{28,4},{1,25},{... | collective-permute-start | bytes 491528 | tf_op jit(solution)/shard_map/ppermute | solution.py:815
  126.8 12.8 %collective-permute-start.17 = (bf16[1,48,1024]{2,1,0:T(8,128)(2,1)S(1)}, bf16[1,48,1024]{2,1,0:T(8,128)(2,1)S(1)}, u32[]{:S(2)}, u32[]{:S(2)}) collective-permute-start(bf16[1,48,1024]{2,1,0:T(8,128)(2,1)S(1)} %get-tuple-element.320.own_ref), channel_id=1, source_target_pairs={{0,1},{1,0},{2,3},{3,2},{4,5},{5,4},{6,7},{7,6},{8,9},{9,8},{10,11... | collective-permute-start | bytes 294920 | tf_op jit(solution)/shard_map/ppermute | solution.py:825
  128.2 13.9 %collective-permute-start.18 = (bf16[1,48,1024]{2,1,0:T(8,128)(2,1)S(1)}, bf16[1,48,1024]{2,1,0:T(8,128)(2,1)S(1)}, u32[]{:S(2)}, u32[]{:S(2)}) collective-permute-start(bf16[1,48,1024]{2,1,0:T(8,128)(2,1)S(1)} %get-tuple-element.320.own_ref), channel_id=1, source_target_pairs={{0,2},{1,3},{2,0},{3,1},{4,6},{5,7},{6,4},{7,5},{8,10},{9,11},{10,... | collective-permute-start | bytes 294920 | tf_op jit(solution)/shard_map/ppermute | solution.py:825
  129.0 21.1 %collective-permute-start.25 = (bf16[1,64,1024]{2,1,0:T(8,128)(2,1)S(1)}, bf16[1,64,1024]{2,1,0:T(8,128)(2,1)S(1)}, u32[]{:S(2)}, u32[]{:S(2)}) collective-permute-start(bf16[1,64,1024]{2,1,0:T(8,128)(2,1)S(1)} %get-tuple-element.337), channel_id=1, source_target_pairs={{0,16},{4,20},{8,24},{12,28},{16,0},{20,4},{24,8},{28,12},{1,17},{... | collective-permute-start | bytes 393224 | tf_op jit(solution)/shard_map/ppermute | solution.py:815
  130.6 20.5 %collective-permute-start.26 = (bf16[1,64,1024]{2,1,0:T(8,128)(2,1)S(1)}, bf16[1,64,1024]{2,1,0:T(8,128)(2,1)S(1)}, u32[]{:S(2)}, u32[]{:S(2)}) collective-permute-start(bf16[1,64,1024]{2,1,0:T(8,128)(2,1)S(1)} %get-tuple-element.338), channel_id=1, source_target_pairs={{0,8},{4,12},{8,0},{12,4},{16,24},{20,28},{24,16},{28,20},{1,9},{5... | collective-permute-start | bytes 393224 | tf_op jit(solution)/shard_map/ppermute | solution.py:815
  139.6 13.0 %collective-permute-start.27 = (bf16[1,64,1024]{2,1,0:T(8,128)(2,1)S(1)}, bf16[1,64,1024]{2,1,0:T(8,128)(2,1)S(1)}, u32[]{:S(2)}, u32[]{:S(2)}) collective-permute-start(bf16[1,64,1024]{2,1,0:T(8,128)(2,1)S(1)} %get-tuple-element.339), channel_id=1, source_target_pairs={{0,24},{4,28},{8,16},{12,20},{16,8},{20,12},{24,0},{28,4},{1,25},{... | collective-permute-start | bytes 393224 | tf_op jit(solution)/shard_map/ppermute | solution.py:815
  142.0 6.5 %collective-permute-start.19 = (bf16[1,48,1024]{2,1,0:T(8,128)(2,1)S(1)}, bf16[1,48,1024]{2,1,0:T(8,128)(2,1)S(1)}, u32[]{:S(2)}, u32[]{:S(2)}) collective-permute-start(bf16[1,48,1024]{2,1,0:T(8,128)(2,1)S(1)} %get-tuple-element.320.own_ref), channel_id=1, source_target_pairs={{0,3},{1,2},{2,1},{3,0},{4,7},{5,6},{6,5},{7,4},{8,11},{9,10},{10,... | collective-permute-start | bytes 294920 | tf_op jit(solution)/shard_map/ppermute | solution.py:825
  148.6 17.8 %collective-permute-start.11 = (bf16[256,1024]{1,0:T(8,128)(2,1)S(1)}, bf16[256,1024]{1,0:T(8,128)(2,1)S(1)}, u32[]{:S(2)}, u32[]{:S(2)}) collective-permute-start(bf16[256,1024]{1,0:T(8,128)(2,1)S(1)} %shard_map.262), channel_id=1, source_target_pairs={{0,1},{1,0},{2,3},{3,2},{4,5},{5,4},{6,7},{7,6},{8,9},{9,8},{10,11... | collective-permute-start | bytes 1572872 | tf_op jit(solution)/shard_map/ppermute | solution.py:960
  150.1 14.8 %collective-permute-start.13 = (bf16[256,1024]{1,0:T(8,128)(2,1)S(1)}, bf16[256,1024]{1,0:T(8,128)(2,1)S(1)}, u32[]{:S(2)}, u32[]{:S(2)}) collective-permute-start(bf16[256,1024]{1,0:T(8,128)(2,1)S(1)} %shard_map.263), channel_id=1, source_target_pairs={{1,2},{2,1},{5,6},{6,5},{9,10},{10,9},{13,14},{14,13},{17,18},{18,... | collective-permute-start | bytes 1572872 | tf_op jit(solution)/shard_map/ppermute | solution.py:960
  152.6 7.1 %collective-permute-start.22 = (bf16[1,80,1024]{2,1,0:T(8,128)(2,1)S(1)}, bf16[1,80,1024]{2,1,0:T(8,128)(2,1)S(1)}, u32[]{:S(2)}, u32[]{:S(2)}) collective-permute-start(bf16[1,80,1024]{2,1,0:T(8,128)(2,1)S(1)} %shard_map.270.refs_0_.refs_5_), channel_id=1, source_target_pairs={{0,8},{4,12},{8,0},{12,4},{16,24},{20,28},{24,16},{28,20},{1,9},{5... | collective-permute-start | bytes 491528 | tf_op jit(solution)/shard_map/ppermute | solution.py:815
  154.2 7.3 %collective-permute-start.23 = (bf16[1,80,1024]{2,1,0:T(8,128)(2,1)S(1)}, bf16[1,80,1024]{2,1,0:T(8,128)(2,1)S(1)}, u32[]{:S(2)}, u32[]{:S(2)}) collective-permute-start(bf16[1,80,1024]{2,1,0:T(8,128)(2,1)S(1)} %shard_map.270.refs_0_.refs_5_), channel_id=1, source_target_pairs={{0,24},{4,28},{8,16},{12,20},{16,8},{20,12},{24,0},{28,4},{1,25},{... | collective-permute-start | bytes 491528 | tf_op jit(solution)/shard_map/ppermute | solution.py:815
  161.5 16.8 %collective-permute-start.36 = (bf16[4,80,1024]{2,1,0:T(8,128)(2,1)S(1)}, bf16[4,80,1024]{2,1,0:T(8,128)(2,1)S(1)}, u32[]{:S(2)}, u32[]{:S(2)}) collective-permute-start(bf16[4,80,1024]{2,1,0:T(8,128)(2,1)S(1)} %shard_map.274), channel_id=1, source_target_pairs={{0,4},{4,0},{8,12},{12,8},{16,20},{20,16},{24,28},{28,24},{1,5},{5... | collective-permute-start | bytes 1966088 | tf_op jit(solution)/shard_map/ppermute | solution.py:815
  164.0 10.8 %collective-permute-start.31 = (bf16[1,48,1024]{2,1,0:T(8,128)(2,1)S(1)}, bf16[1,48,1024]{2,1,0:T(8,128)(2,1)S(1)}, u32[]{:S(2)}, u32[]{:S(2)}) collective-permute-start(bf16[1,48,1024]{2,1,0:T(8,128)(2,1)S(1)} %get-tuple-element.343.own_ref), channel_id=1, source_target_pairs={{0,2},{1,3},{2,0},{3,1},{4,6},{5,7},{6,4},{7,5},{8,10},{9,11},{10,... | collective-permute-start | bytes 294920 | tf_op jit(solution)/shard_map/ppermute | solution.py:825
  164.9 9.8 %collective-permute-start.32 = (bf16[1,48,1024]{2,1,0:T(8,128)(2,1)S(1)}, bf16[1,48,1024]{2,1,0:T(8,128)(2,1)S(1)}, u32[]{:S(2)}, u32[]{:S(2)}) collective-permute-start(bf16[1,48,1024]{2,1,0:T(8,128)(2,1)S(1)} %get-tuple-element.343.own_ref), channel_id=1, source_target_pairs={{0,3},{1,2},{2,1},{3,0},{4,7},{5,6},{6,5},{7,4},{8,11},{9,10},{10,... | collective-permute-start | bytes 294920 | tf_op jit(solution)/shard_map/ppermute | solution.py:825
  174.8 6.4 %collective-permute-start.33 = (bf16[1,64,1024]{2,1,0:T(8,128)(2,1)S(1)}, bf16[1,64,1024]{2,1,0:T(8,128)(2,1)S(1)}, u32[]{:S(2)}, u32[]{:S(2)}) collective-permute-start(bf16[1,64,1024]{2,1,0:T(8,128)(2,1)S(1)} %shard_map.276.refs_0_.refs_5_), channel_id=1, source_target_pairs={{0,16},{4,20},{8,24},{12,28},{16,0},{20,4},{24,8},{28,12},{1,17},{... | collective-permute-start | bytes 393224 | tf_op jit(solution)/shard_map/ppermute | solution.py:815
  183.3 15.0 %collective-permute-start.28 = (bf16[256,1024]{1,0:T(8,128)(2,1)S(1)}, bf16[256,1024]{1,0:T(8,128)(2,1)S(1)}, u32[]{:S(2)}, u32[]{:S(2)}) collective-permute-start(bf16[256,1024]{1,0:T(8,128)(2,1)S(1)} %shard_map.269), channel_id=1, source_target_pairs={{0,1},{1,0},{2,3},{3,2},{4,5},{5,4},{6,7},{7,6},{8,9},{9,8},{10,11... | collective-permute-start | bytes 1572872 | tf_op jit(solution)/shard_map/ppermute | solution.py:960
  185.8 26.0 %collective-permute-start.29 = (bf16[256,1024]{1,0:T(8,128)(2,1)S(1)}, bf16[256,1024]{1,0:T(8,128)(2,1)S(1)}, u32[]{:S(2)}, u32[]{:S(2)}) collective-permute-start(bf16[256,1024]{1,0:T(8,128)(2,1)S(1)} %shard_map.272), channel_id=1, source_target_pairs={{0,3},{1,2},{2,1},{3,0},{4,7},{5,6},{6,5},{7,4},{8,11},{9,10},{10,... | collective-permute-start | bytes 1572872 | tf_op jit(solution)/shard_map/ppermute | solution.py:960
  (32 other events, 89.2 us)
